TPU v7x, 128 devices: a whole 4x4x4 slice. The times are simulated.
128 devices in a mesh: gx: 32 (over z, y, core), gy: 4 (over x).
Axes of the slice: x: 4, y: 4, z: 4, core: 2. Of those that a mesh axis runs over, the one named last changes fastest.
Arguments:
- scalar: float32 [2, 512, 32, 4, 128], P(None, None, 'gx', 'gy'), may hold values from -6 to 6
- velocity: float32 [3, 2, 512, 32, 4, 128], P(None, None, None, 'gx', 'gy'), may hold values from -1 to 1
- diffusivity: float32 [2, 32, 4, 128], P(None, 'gx', 'gy'), may hold values from 0.005 to 0.05
- recv_owner: int32 [262144, 1], P(('gx', 'gy')), may hold values from 0 to 127; in each aligned block of 2048 rows (0 to 2047, 2048 to 4095, ...) at most 32 rows name the same one
- donor_elem: int32 [262144], P(('gx', 'gy')), may hold values from 0 to 127
- recv_point: int32 [262144], P(('gx', 'gy')), may hold values from 0 to 65535
- recv_coords: float32 [3, 262144], P(None, ('gx', 'gy')), may hold values from -1 to 1
Outputs:
- advanced: float32 [2, 512, 32, 4, 128], P(None, None, 'gx', 'gy')
Inputs may be any that keep to these rules, and one draw needn't show every extreme that they name: `recv_owner`: among the 2048 receivers of one device no owner is named more than 32 times, a bound that some block reaches.
All inputs are finite; a program needn't handle non-finite values.
Results may differ from a plain program's by a relative error of at most 0.0003.
Values sent between devices are 32-bit elements; how exact they have to be, the bound alone decides.
No kernel may reach another device: no remote copies, remote signals or barrier semaphores. Data moves between devices by JAX's collectives and lax.ppermute only.
A program may use at most 128 MiB of HBM per device.

v0:
```python
import jax
import jax.numpy as jnp
from jax import lax
from jax.sharding import PartitionSpec as P

time_step = 0.01
penalty_rate = 50.0
metric = 2.0
volume_factor = 0.125
node_inner = [0.8717401485096066, 0.5917001814331423, 0.20929921790247888]


def passed_along(value, axis, steps):
    count = lax.axis_size(axis)
    leading, last = (max(0, -steps), min(count, count - steps))
    return lax.ppermute(value, axis, [(source, source + steps) for source in range(leading, last)])


def legendre_seven(point):
    before, current = (1.0, point)
    for order in range(1, 7):
        before, current = (
            current,
            ((2 * order + 1) * point * current - order * before) / (order + 1),
        )
    return current


def gll_tables():
    degree = 7
    gll_nodes = [
        -1.0,
        -node_inner[0],
        -node_inner[1],
        -node_inner[2],
        node_inner[2],
        node_inner[1],
        node_inner[0],
        1.0,
    ]
    end_values = [legendre_seven(v) for v in gll_nodes]
    weights = [2.0 / (degree * (degree + 1) * v * v) for v in end_values]
    derivative = [[0.0] * 8 for _ in range(8)]
    for a in range(8):
        for b in range(8):
            if a != b:
                derivative[a][b] = end_values[a] / (end_values[b] * (gll_nodes[a] - gll_nodes[b]))
    derivative[0][0] = -degree * (degree + 1) / 4.0
    derivative[7][7] = degree * (degree + 1) / 4.0
    weight_row = jnp.asarray(weights, jnp.float32)
    cube_weights = weight_row[:, None, None] * weight_row[None, :, None] * weight_row[None, None, :]
    return (gll_nodes, cube_weights, derivative)


def lagrange_rows(position, gll_nodes):
    columns = []
    for j in range(8):
        factor = jnp.ones_like(position)
        for m in range(8):
            if m != j:
                factor = factor * ((position - gll_nodes[m]) / (gll_nodes[j] - gll_nodes[m]))
        columns.append(factor)
    return jnp.stack(columns, axis=-1)


def element_rate(values, velocity, diffusivity, derivative, cube_weights):
    highest = lax.Precision.HIGHEST
    grad_x = metric * jnp.einsum("ai,ijkxyz->ajkxyz", derivative, values, precision=highest)
    grad_y = metric * jnp.einsum("bj,ijkxyz->ibkxyz", derivative, values, precision=highest)
    grad_z = metric * jnp.einsum("ck,ijkxyz->ijcxyz", derivative, values, precision=highest)
    mass_local = volume_factor * cube_weights[:, :, :, None, None, None]
    advect = velocity[0] * grad_x + velocity[1] * grad_y + velocity[2] * grad_z
    scaled = metric * mass_local * diffusivity[None, None, None]
    diffuse = jnp.einsum("ai,ajkxyz->ijkxyz", derivative, scaled * grad_x, precision=highest)
    diffuse = diffuse + jnp.einsum(
        "bj,ibkxyz->ijkxyz", derivative, scaled * grad_y, precision=highest
    )
    diffuse = diffuse + jnp.einsum(
        "ck,ijcxyz->ijkxyz", derivative, scaled * grad_z, precision=highest
    )
    return -(mass_local * advect) - diffuse


def face_sum(values, pdim, edim, next_slab, prev_slab):
    left = lax.index_in_dim(values, 0, pdim, keepdims=True)
    right = lax.index_in_dim(values, 7, pdim, keepdims=True)
    count = values.shape[edim]
    after = jnp.concatenate([lax.slice_in_dim(left, 1, count, axis=edim), next_slab], axis=edim)
    before = jnp.concatenate(
        [prev_slab, lax.slice_in_dim(right, 0, count - 1, axis=edim)], axis=edim
    )
    middle = lax.slice_in_dim(values, 1, 7, axis=pdim)
    return jnp.concatenate([left + before, middle, right + after], axis=pdim)


def edge_slabs(values, pdim, edim):
    left = lax.index_in_dim(values, 0, pdim, keepdims=True)
    right = lax.index_in_dim(values, 7, pdim, keepdims=True)
    count = values.shape[edim]
    return (
        lax.index_in_dim(left, 0, edim, keepdims=True),
        lax.index_in_dim(right, count - 1, edim, keepdims=True),
    )


def assemble(values):
    left_first, right_last = edge_slabs(values, 1, 4)
    next_slab = passed_along(left_first, "gx", -1)
    prev_slab = passed_along(right_last, "gx", 1)
    values = face_sum(values, 1, 4, next_slab, prev_slab)
    left_first, right_last = edge_slabs(values, 2, 5)
    next_slab = passed_along(left_first, "gy", -1)
    prev_slab = passed_along(right_last, "gy", 1)
    values = face_sum(values, 2, 5, next_slab, prev_slab)
    zeros_slab = jnp.zeros_like(edge_slabs(values, 3, 6)[0])
    return face_sum(values, 3, 6, zeros_slab, zeros_slab)


def body(scalar, velocity, diffusivity, recv_owner, donor_elem, recv_point, recv_coords):
    gll_nodes, cube_np, derivative_np = gll_tables()
    derivative = jnp.asarray(derivative_np, jnp.float32)
    cube_weights = jnp.asarray(cube_np, jnp.float32)
    cube_flat = cube_weights.reshape(512)
    count_x, count_y, count_z = (scalar.shape[2], scalar.shape[3], scalar.shape[4])
    elems = count_x * count_y * count_z
    shape_full = (2, 8, 8, 8, count_x, count_y, count_z)
    flow = velocity.reshape((3,) + shape_full)
    mass_total = assemble(
        jnp.broadcast_to(volume_factor * cube_weights[None, :, :, :, None, None, None], shape_full)
    )
    width_x = lax.axis_size("gx")
    width_y = lax.axis_size("gy")
    devices = width_x * width_y
    rows = recv_owner.shape[0]
    capacity = max(2, 2 * rows // devices)
    slots_all = devices * capacity
    owners = recv_owner[:, 0]
    one_hot = (owners[:, None] == jnp.arange(devices, dtype=jnp.int32)[None, :]).astype(jnp.int32)
    slots = jnp.sum(jnp.cumsum(one_hot, axis=0) * one_hot, axis=1) - 1
    target = owners * capacity + slots
    own_mesh = (jnp.arange(rows, dtype=jnp.int32) >= rows // 2).astype(jnp.int32)
    donor_ids = (1 - own_mesh) * elems + donor_elem
    queries = jnp.concatenate([recv_coords, donor_ids.astype(jnp.float32)[None]], axis=0)
    payload = jnp.zeros((4, slots_all), jnp.float32).at[:, target].set(queries)
    point_q = recv_point // elems
    flat_index = own_mesh * (512 * elems) + recv_point
    point_mass = volume_factor * cube_flat[point_q]
    received = lax.all_to_all(
        payload.reshape(4, devices, capacity), ("gx", "gy"), split_axis=1, concat_axis=1, tiled=True
    )
    received = received.reshape(4, slots_all)

    def send_answers(answers):
        moved = lax.all_to_all(
            answers.reshape(devices, capacity),
            ("gx", "gy"),
            split_axis=0,
            concat_axis=0,
            tiled=True,
        )
        return moved.reshape(slots_all)

    block_count = 1
    row_ids = received[3].astype(jnp.int32)
    kept = (
        row_ids,
        lagrange_rows(received[0], gll_nodes),
        lagrange_rows(received[1], gll_nodes),
        lagrange_rows(received[2], gll_nodes),
    )
    kept = tuple(
        (piece.reshape((block_count, slots_all // block_count) + piece.shape[1:]) for piece in kept)
    )

    def interpolate(values):
        element_rows = jnp.transpose(values.reshape(2, 512, elems), (0, 2, 1)).reshape(
            2 * elems, 512
        )

        def one_block(pieces):
            ids, wx, wy, wz = pieces
            element_values = element_rows[ids].reshape(-1, 8, 8, 8)
            return jnp.einsum(
                "nijk,ni,nj,nk->n", element_values, wx, wy, wz, precision=lax.Precision.HIGHEST
            )

        return lax.map(one_block, kept).reshape(slots_all)

    def rate(values):
        local = jnp.stack(
            [
                element_rate(values[m], flow[:, m], diffusivity[m], derivative, cube_weights)
                for m in range(2)
            ]
        )
        answers = interpolate(values)
        replies = send_answers(answers)
        donor_values = replies[target]
        current = values.reshape(-1)[flat_index]
        added = penalty_rate * point_mass * (donor_values - current)
        local = local.reshape(-1).at[flat_index].add(added).reshape(shape_full)
        return assemble(local) / mass_total

    start = scalar.reshape(shape_full)
    first = start + time_step * rate(start)
    second = 0.75 * start + 0.25 * (first + time_step * rate(first))
    third = start / 3.0 + 2.0 / 3.0 * (second + time_step * rate(second))
    return third.reshape(2, 512, count_x, count_y, count_z)


def solution(mesh):
    return jax.shard_map(
        body,
        mesh=mesh,
        in_specs=(
            P(None, None, "gx", "gy", None),
            P(None, None, None, "gx", "gy", None),
            P(None, "gx", "gy", None),
            P(("gx", "gy"), None),
            P(("gx", "gy")),
            P(("gx", "gy")),
            P(None, ("gx", "gy")),
        ),
        out_specs=P(None, None, "gx", "gy", None),
        check_vma=False,
    )
```

profile of v0, /device:TPU:34, one launch (start us, length us, event | category | flops | bytes accessed | tf_op | source)
XLA Modules:
  0.0 441.6 jit_solution(8866644987064279442)
XLA Ops:
  2.4 3.9 collective-permute-start.5
  7.1 1.9 collective-permute-start.4
  10.6 1.3 fusion.25
  14.1 1.4 copy.1044
  15.5 6.5 %scatter_custom_fusion = f32[4,4096]{0,1:T(8,128)S(1)} fusion(s32[2048]{0:T(1024)S(1)} %bitcast.586, f32[2048,4]{1,0:T(8,128)} %copy.1044, f32[]{:T(128)} %constant.334.clone.1), kind=kCustom, calls=%fused_computation.58 | custom fusion | bytes 66048 | tf_op jit(solution)/shard_map/scatter | solution.py:144
  23.7 11.5 %all-to-all-start = ((f32[128,1,128]{2,1,0:T(1,128)}), f32[128,1,128]{2,1,0:T(1,128)S(1)}, u32[]{:S(2)}, u32[]{:S(2)}) async-start(f32[128,1,128]{2,1,0:T(1,128)} %reshape.3171), calls=%async_computation | async-start | bytes 131072 | tf_op jit(solution)/shard_map/all_to_all | solution.py:148
  39.3 2.3 slice_bitcast_fusion.13
  47.0 11.8 %gather_fusion.3 = f32[2048]{0:T(1024)S(1)} fusion(f32[131072]{0:T(1024)S(1)} %bitcast.535, s32[2048]{0:T(1024)S(1)} %get-tuple-element.169), kind=kCustom, calls=%fused_computation.3 | custom fusion | bytes 24576 | tf_op jit(solution)/shard_map/gather | solution.py:199
  58.8 13.2 %gather_fusion = f32[2048]{0:T(1024)S(1)} fusion(f32[512]{0:T(512)S(1)} %mul.2275, s32[2048]{0:T(1024)S(1)} %get-tuple-element.168), kind=kCustom, calls=%fused_computation | custom fusion | bytes 24576 | tf_op jit(solution)/shard_map/gather | solution.py:147
  76.0 16.8 %gather_fusion.1 = f32[4096,512]{1,0:T(8,128)} fusion(f32[256,512]{1,0:T(8,128)S(1)} %bitcast.530, s32[4096]{0:T(1024)S(1)} %broadcast_clamp_fusion), kind=kCustom, calls=%fused_computation.1 | custom fusion | bytes 16793600 | tf_op jit(solution)/shard_map/while/body/eval_jaxpr/gather | solution.py:182
  92.8 9.2 %copy.1056 = f32[4096,512]{0,1:T(8,128)} copy(f32[4096,512]{1,0:T(8,128)} %gather_fusion.1) | data formatting | bytes 16777216 | tf_op jit(solution)/shard_map/while/body/eval_jaxpr/gather | solution.py:182
  106.7 4.1 multiply_reduce_fusion.2
  111.8 9.8 %all-to-all-start.1 = ((f32[128,1,32]{2,1,0:T(1,128)}), f32[128,1,32]{2,1,0:T(1,128)S(1)}, u32[]{:S(2)}, u32[]{:S(2)}) async-start(f32[128,1,32]{2,1,0:T(1,128)} %bitcast.82), calls=%async_computation.1 | async-start | bytes 131072 | tf_op jit(solution)/shard_map/all_to_all | solution.py:154
  123.7 3.4 collective-permute-start.6
  127.1 2.3 all-to-all-done.1
  130.8 11.8 %gather_fusion.2 = f32[2048]{0:T(1024)S(1)} fusion(f32[4096]{0:T(1024)S(1)} %reshape.2865, s32[2048]{0:T(1024)S(1)} %broadcast_clamp_fusion.2), kind=kCustom, calls=%fused_computation.2 | custom fusion | bytes 24576 | tf_op jit(solution)/shard_map/gather | solution.py:198
  142.7 11.7 %scatter_fusion = f32[131072]{0:T(1024)S(1)} fusion(f32[131072]{0:T(1024)S(1)} %bitcast.543, s32[2048]{0:T(1024)S(1)} %get-tuple-element.170, f32[2048]{0:T(1024)S(1)} %subtract_multiply_fusion.2), kind=kCustom, calls=%fused_computation.11 | custom fusion | flops 2048 | bytes 32768 | tf_op jit(solution)/shard_map/scatter-add | solution.py:201
  154.5 3.1 collective-permute-start.1
  157.9 2.1 collective-permute-start
  160.0 3.4 collective-permute-start.7
  163.5 2.2 collective-permute-done
  165.8 2.6 collective-permute-start.2
  168.7 3.3 collective-permute-done.2
  172.0 2.4 collective-permute-start.3
  174.6 3.6 collective-permute-done.3
  187.9 1.2 fusion.74
  190.6 16.8 %gather_fusion.4 = f32[4096,512]{1,0:T(8,128)} fusion(f32[256,512]{1,0:T(8,128)S(1)} %bitcast.532, s32[4096]{0:T(1024)S(1)} %copy-done.42), kind=kCustom, calls=%fused_computation.4 | custom fusion | bytes 16793600 | tf_op jit(solution)/shard_map/while/body/eval_jaxpr/gather | solution.py:182
  207.5 9.0 %copy.1119 = f32[4096,512]{0,1:T(8,128)} copy(f32[4096,512]{1,0:T(8,128)} %gather_fusion.4) | data formatting | bytes 16777216 | tf_op jit(solution)/shard_map/while/body/eval_jaxpr/gather | solution.py:182
  216.5 4.2 multiply_reduce_fusion.1
  221.5 6.2 %all-to-all-start.2 = ((f32[128,1,32]{2,1,0:T(1,128)}), f32[128,1,32]{2,1,0:T(1,128)}, u32[]{:S(2)}, u32[]{:S(2)}) async-start(f32[128,1,32]{2,1,0:T(1,128)} %bitcast.134), calls=%async_computation.2 | async-start | bytes 131072 | tf_op jit(solution)/shard_map/all_to_all | solution.py:154
  227.7 2.2 fusion.12
  230.0 2.6 fusion.16
  232.8 20.5 %gather_fusion.6 = f32[2048]{0:T(1024)} fusion(f32[131072]{0:T(1024)S(1)} %add.1140, s32[2048]{0:T(1024)S(1)} %copy-done.50), kind=kCustom, calls=%fused_computation.6 | custom fusion | bytes 24576 | tf_op jit(solution)/shard_map/gather | solution.py:199
  253.3 2.2 reduce.26
  256.5 20.7 %gather_fusion.5 = f32[2048]{0:T(1024)} fusion(f32[4096]{0:T(1024)S(1)} %reshape.2877, s32[2048]{0:T(1024)} %copy-done.47), kind=kCustom, calls=%fused_computation.5 | custom fusion | bytes 24576 | tf_op jit(solution)/shard_map/gather | solution.py:198
  277.9 12.0 %scatter_fusion.1 = f32[131072]{0:T(1024)S(1)} fusion(f32[131072]{0:T(1024)S(1)} %bitcast.549, s32[2048]{0:T(1024)} %copy-done.43, f32[2048]{0:T(1024)S(1)} %subtract_multiply_fusion.1), kind=kCustom, calls=%fused_computation.12 | custom fusion | flops 2048 | bytes 32768 | tf_op jit(solution)/shard_map/scatter-add | solution.py:201
  290.0 4.3 collective-permute-start.9
  294.3 1.9 collective-permute-start.8
  296.6 5.4 %collective-permute-done.8 = f32[2,1,8,8,1,1,128]{6,1,3,2,5,4,0:T(1,128)S(1)} collective-permute-done((f32[2,1,8,8,1,1,128]{6,1,3,2,5,4,0:T(1,128)S(1)}, f32[2,1,8,8,1,1,128]{6,1,3,2,5,4,0:T(1,128)S(1)}, u32[]{:S(2)}, u32[]{:S(2)}) %collective-permute-start.8) | collective-permute-done | bytes 65568 | tf_op jit(solution)/shard_map/ppermute | solution.py:16
  302.1 3.4 collective-permute-start.10
  305.5 2.8 collective-permute-done.10
  308.3 1.9 collective-permute-start.11
  310.2 4.2 collective-permute-done.11
  314.8 1.5 multiply_add_fusion.1
  319.4 1.1 fusion.87
  320.5 1.2 fusion.89
  328.6 1.2 copy.1161
  329.9 18.0 %gather_fusion.7 = f32[4096,512]{1,0:T(8,128)} fusion(f32[256,512]{1,0:T(8,128)S(1)} %bitcast.531, s32[4096]{0:T(1024)} %copy-done.41), kind=kCustom, calls=%fused_computation.7 | custom fusion | bytes 16793600 | tf_op jit(solution)/shard_map/while/body/eval_jaxpr/gather | solution.py:182
  347.9 9.0 %copy.1162 = f32[4096,512]{0,1:T(8,128)} copy(f32[4096,512]{1,0:T(8,128)} %gather_fusion.7) | data formatting | bytes 16777216 | tf_op jit(solution)/shard_map/while/body/eval_jaxpr/gather | solution.py:182
  356.9 4.2 multiply_reduce_fusion
  361.8 8.4 %all-to-all-start.3 = ((f32[128,1,32]{2,1,0:T(1,128)}), f32[128,1,32]{2,1,0:T(1,128)}, u32[]{:S(2)}, u32[]{:S(2)}) async-start(f32[128,1,32]{2,1,0:T(1,128)} %bitcast.182), calls=%async_computation.3 | async-start | bytes 131072 | tf_op jit(solution)/shard_map/all_to_all | solution.py:154
  371.3 3.1 fusion.24
  374.4 2.7 fusion.20
  377.3 11.8 %gather_fusion.9 = f32[2048]{0:T(1024)S(1)} fusion(f32[131072]{0:T(1024)S(1)} %multiply_add_fusion, s32[2048]{0:T(1024)S(1)} %copy-done.51), kind=kCustom, calls=%fused_computation.9 | custom fusion | bytes 24576 | tf_op jit(solution)/shard_map/gather | solution.py:199
  389.1 1.6 reduce.27
  390.8 11.8 %gather_fusion.8 = f32[2048]{0:T(1024)S(1)} fusion(f32[4096]{0:T(1024)S(1)} %reshape.2888, s32[2048]{0:T(1024)S(1)} %copy-done.48), kind=kCustom, calls=%fused_computation.8 | custom fusion | bytes 24576 | tf_op jit(solution)/shard_map/gather | solution.py:198
  402.6 11.7 %scatter_fusion.2 = f32[131072]{0:T(1024)S(1)} fusion(f32[131072]{0:T(1024)S(1)} %bitcast.546, s32[2048]{0:T(1024)S(1)} %copy-done.44, f32[2048]{0:T(1024)S(1)} %subtract_multiply_fusion), kind=kCustom, calls=%fused_computation.13 | custom fusion | flops 2048 | bytes 32768 | tf_op jit(solution)/shard_map/scatter-add | solution.py:201
  414.4 4.4 collective-permute-start.13
  418.8 1.9 collective-permute-start.12
  421.1 5.4 %collective-permute-done.12 = f32[2,1,8,8,1,1,128]{6,1,3,2,5,4,0:T(1,128)S(1)} collective-permute-done((f32[2,1,8,8,1,1,128]{6,1,3,2,5,4,0:T(1,128)S(1)}, f32[2,1,8,8,1,1,128]{6,1,3,2,5,4,0:T(1,128)S(1)}, u32[]{:S(2)}, u32[]{:S(2)}) %collective-permute-start.12) | collective-permute-done | bytes 65568 | tf_op jit(solution)/shard_map/ppermute | solution.py:16
  426.6 3.4 collective-permute-start.14
  430.0 2.8 collective-permute-done.14
  432.8 1.9 collective-permute-start.15
  434.8 4.2 collective-permute-done.15
  (353 shorter events, 60.8 us)
Async XLA Ops:
  0.0 35.2 %copy-start.61 = (f32[8]{0:T(128)S(1)}, f32[8]{0:T(128)}, u32[]{:S(2)}) copy-start(f32[8]{0:T(128)} %constant.381.clone) | copy-start | bytes 100
  0.0 35.4 %copy-start.3 = (f32[8,8,1,1]{1,0,3,2:T(8,128)S(1)}, f32[8,8,1,1]{1,0,3,2:T(8,128)}, u32[]{:S(2)}) copy-start(f32[8,8,1,1]{1,0,3,2:T(8,128)} %constant.408) | copy-start | bytes 772
  0.0 35.3 %copy-start = (f32[2,512,1,1,128]{4,3,2,1,0:T(1,128)S(1)}, f32[2,512,1,1,128]{4,3,2,1,0:T(1,128)}, u32[]{:S(2)}) copy-start(f32[2,512,1,1,128]{4,3,2,1,0:T(1,128)} %param.9) | copy-start | bytes 1572868
  0.9 36.5 %copy-start.63 = (f32[2,1,1,128]{3,2,1,0:T(1,128)S(1)}, f32[2,1,1,128]{3,2,1,0:T(1,128)}, u32[]{:S(2)}) copy-start(f32[2,1,1,128]{3,2,1,0:T(1,128)} %param.11) | copy-start | bytes 3076
  2.4 119.1 %collective-permute-start.5 = (f32[2,1,8,8,1,1,128]{6,1,3,2,5,4,0:T(1,128)}, f32[2,1,8,8,1,1,128]{6,1,3,2,5,4,0:T(1,128)}, u32[]{:S(2)}, u32[]{:S(2)}) collective-permute-start(f32[2,1,8,8,1,1,128]{6,1,3,2,5,4,0:T(1,128)} %broadcast_in_dim.30), channel_id=1, source_target_pairs={{4,0},{8,4},{12,8},{16,12},{20,16},{24,20},{28,24},{32,28},{36,32}... | collective-permute-start | bytes 196616 | tf_op jit(solution)/shard_map/ppermute | solution.py:16
  7.1 115.5 %collective-permute-start.4 = (f32[2,1,8,8,1,1,128]{6,1,3,2,5,4,0:T(1,128)}, f32[2,1,8,8,1,1,128]{6,1,3,2,5,4,0:T(1,128)}, u32[]{:S(2)}, u32[]{:S(2)}) collective-permute-start(f32[2,1,8,8,1,1,128]{6,1,3,2,5,4,0:T(1,128)} %broadcast_in_dim.32), channel_id=1, source_target_pairs={{0,4},{4,8},{8,12},{12,16},{16,20},{20,24},{24,28},{28,32},{32,36}... | collective-permute-start | bytes 196616 | tf_op jit(solution)/shard_map/ppermute | solution.py:16
  11.9 29.7 %copy-start.59 = (f32[8,8,1,1]{1,0,2,3:T(8,128)S(1)}, f32[8,8,1,1]{1,0,2,3:T(8,128)}, u32[]{:S(2)}) copy-start(f32[8,8,1,1]{1,0,2,3:T(8,128)} %constant.409) | copy-start | bytes 772
  23.7 48.4 %all-to-all-start = ((f32[128,1,128]{2,1,0:T(1,128)}), f32[128,1,128]{2,1,0:T(1,128)S(1)}, u32[]{:S(2)}, u32[]{:S(2)}) async-start(f32[128,1,128]{2,1,0:T(1,128)} %reshape.3171), calls=%async_computation | async-start | bytes 131072 | tf_op jit(solution)/shard_map/all_to_all | solution.py:148
  37.4 93.4 %copy-start.47 = (s32[2048]{0:T(1024)}, s32[2048]{0:T(1024)S(1)}, u32[]{:S(2)}) copy-start(s32[2048]{0:T(1024)S(1)} %broadcast_clamp_fusion.2) | copy-start | bytes 24580
  37.6 143.5 %copy-start.20 = (f32[8,8,8]{0,2,1:T(8,128)}, f32[8,8,8]{0,2,1:T(8,128)S(1)}, u32[]{:S(2)}) copy-start(f32[8,8,8]{0,2,1:T(8,128)S(1)} %copy.1010) | copy-start | bytes 6148
  41.7 146.2 %copy-start.9 = (f32[1,1,8,8,8,1,1,128]{7,4,3,2,1,0,6,5:T(8,128)}, f32[1,1,8,8,8,1,1,128]{7,4,3,2,1,0,6,5:T(8,128)S(1)}, u32[]{:S(2)}) copy-start(f32[1,1,8,8,8,1,1,128]{7,4,3,2,1,0,6,5:T(8,128)S(1)} %get-tuple-element.75) | copy-start | bytes 786436
  44.4 27.6 %copy-start.49 = (s32[2048]{0:T(1024)}, s32[2048]{0:T(1024)S(1)}, u32[]{:S(2)}) copy-start(s32[2048]{0:T(1024)S(1)} %get-tuple-element.169) | copy-start | bytes 24580
  44.5 98.2 %copy-start.43 = (s32[2048]{0:T(1024)}, s32[2048]{0:T(1024)S(1)}, u32[]{:S(2)}) copy-start(s32[2048]{0:T(1024)S(1)} %get-tuple-element.170) | copy-start | bytes 24580
  72.0 70.6 %copy-start.45 = (f32[2048]{0:T(1024)}, f32[2048]{0:T(1024)S(1)}, u32[]{:S(2)}) copy-start(f32[2048]{0:T(1024)S(1)} %gather_fusion) | copy-start | bytes 24580
  75.9 16.8 %copy-start.41 = (s32[4096]{0:T(1024)}, s32[4096]{0:T(1024)S(1)}, u32[]{:S(2)}) copy-start(s32[4096]{0:T(1024)S(1)} %broadcast_clamp_fusion) | copy-start | bytes 49156
  111.0 11.5 %copy-start.33 = (f32[4096,8]{0,1:T(8,128)}, f32[4096,8]{0,1:T(8,128)S(1)}, u32[]{:S(2)}) copy-start(f32[4096,8]{0,1:T(8,128)S(1)} %stack.27) | copy-start | bytes 393220
  111.8 17.6 %all-to-all-start.1 = ((f32[128,1,32]{2,1,0:T(1,128)}), f32[128,1,32]{2,1,0:T(1,128)S(1)}, u32[]{:S(2)}, u32[]{:S(2)}) async-start(f32[128,1,32]{2,1,0:T(1,128)} %bitcast.82), calls=%async_computation.1 | async-start | bytes 131072 | tf_op jit(solution)/shard_map/all_to_all | solution.py:154
  123.7 36.2 %collective-permute-start.6 = (f32[2,8,1,8,1,1,128]{6,1,3,2,5,4,0:T(8,128)S(1)}, f32[2,8,1,8,1,1,128]{6,1,3,2,5,4,0:T(8,128)S(1)}, u32[]{:S(2)}, u32[]{:S(2)}) collective-permute-start(f32[2,8,1,8,1,1,128]{6,1,3,2,5,4,0:T(8,128)S(1)} %pad_maximum_fusion.8), channel_id=1, source_target_pairs={{0,1},{1,2},{2,3},{4,5},{5,6},{6,7},{8,9},{9,10},{10,11},{12,13},{... | collective-permute-start | bytes 196616 | tf_op jit(solution)/shard_map/ppermute | solution.py:16
  154.4 26.7 %copy-start.53 = (f32[128]{0:T(128)S(1)}, f32[128]{0:T(128)}, u32[]{:S(2)}) copy-start(f32[128]{0:T(128)} %copy-done.52) | copy-start | bytes 1540
  154.4 26.7 %copy-start.56 = (f32[128]{0:T(128)S(1)}, f32[128]{0:T(128)}, u32[]{:S(2)}) copy-start(f32[128]{0:T(128)} %copy-done.55) | copy-start | bytes 1540
  154.5 9.0 %collective-permute-start.1 = (f32[2,1,8,8,1,1,128]{6,1,3,2,5,4,0:T(1,128)S(1)}, f32[2,1,8,8,1,1,128]{6,1,3,2,5,4,0:T(1,128)S(1)}, u32[]{:S(2)}, u32[]{:S(2)}) collective-permute-start(f32[2,1,8,8,1,1,128]{6,1,3,2,5,4,0:T(1,128)S(1)} %bitcast.571), channel_id=1, source_target_pairs={{4,0},{8,4},{12,8},{16,12},{20,16},{24,20},{28,24},{32,28},{36,32}... | collective-permute-start | bytes 196616 | tf_op jit(solution)/shard_map/ppermute | solution.py:16
  157.8 24.8 %copy-start.12 = (f32[1,1,8,8,8,1,1,128]{7,4,3,2,1,0,6,5:T(8,128)S(1)}, f32[1,1,8,8,8,1,1,128]{7,4,3,2,1,0,6,5:T(8,128)}, u32[]{:S(2)}) copy-start(f32[1,1,8,8,8,1,1,128]{7,4,3,2,1,0,6,5:T(8,128)} %copy-done.11) | copy-start | bytes 786436
  157.8 24.8 %copy-start.26 = (f32[8,8,8,1,1,128]{5,0,2,1,4,3:T(8,128)S(1)}, f32[8,8,8,1,1,128]{5,0,2,1,4,3:T(8,128)}, u32[]{:S(2)}) copy-start(f32[8,8,8,1,1,128]{5,0,2,1,4,3:T(8,128)} %copy-done.25) | copy-start | bytes 786436
  157.9 7.8 %collective-permute-start = (f32[2,1,8,8,1,1,128]{6,1,3,2,5,4,0:T(1,128)S(1)}, f32[2,1,8,8,1,1,128]{6,1,3,2,5,4,0:T(1,128)S(1)}, u32[]{:S(2)}, u32[]{:S(2)}) collective-permute-start(f32[2,1,8,8,1,1,128]{6,1,3,2,5,4,0:T(1,128)S(1)} %bitcast.573), channel_id=1, source_target_pairs={{0,4},{4,8},{8,12},{12,16},{16,20},{20,24},{24,28},{28,32},{32,36}... | collective-permute-start | bytes 196616 | tf_op jit(solution)/shard_map/ppermute | solution.py:16
  160.0 8.4 %collective-permute-start.7 = (f32[2,8,1,8,1,1,128]{6,1,3,2,5,4,0:T(8,128)S(1)}, f32[2,8,1,8,1,1,128]{6,1,3,2,5,4,0:T(8,128)S(1)}, u32[]{:S(2)}, u32[]{:S(2)}) collective-permute-start(f32[2,8,1,8,1,1,128]{6,1,3,2,5,4,0:T(8,128)S(1)} %get-tuple-element.61), channel_id=1, source_target_pairs={{1,0},{2,1},{3,2},{5,4},{6,5},{7,6},{9,8},{10,9},{11,10},{13,12},{... | collective-permute-start | bytes 196616 | tf_op jit(solution)/shard_map/ppermute | solution.py:16
  165.8 6.2 %collective-permute-start.2 = (f32[2,8,1,8,1,1,128]{6,1,3,2,5,4,0:T(8,128)S(1)}, f32[2,8,1,8,1,1,128]{6,1,3,2,5,4,0:T(8,128)S(1)}, u32[]{:S(2)}, u32[]{:S(2)}) collective-permute-start(f32[2,8,1,8,1,1,128]{6,1,3,2,5,4,0:T(8,128)S(1)} %pad_maximum_fusion.10), channel_id=1, source_target_pairs={{0,1},{1,2},{2,3},{4,5},{5,6},{6,7},{8,9},{9,10},{10,11},{12,13},{... | collective-permute-start | bytes 196616 | tf_op jit(solution)/shard_map/ppermute | solution.py:16
  168.4 18.4 %copy-start.40 = (f32[8,8,8,128]{3,0,2,1:T(8,128)S(1)}, f32[8,8,8,128]{3,0,2,1:T(8,128)}, u32[]{:S(2)}) copy-start(f32[8,8,8,128]{3,0,2,1:T(8,128)} %get-tuple-element.136) | copy-start | bytes 786436
  168.4 18.4 %copy-start.60 = (f32[8,8,1,1]{1,0,2,3:T(8,128)S(1)}, f32[8,8,1,1]{1,0,2,3:T(8,128)}, u32[]{:S(2)}) copy-start(f32[8,8,1,1]{1,0,2,3:T(8,128)} %constant.409) | copy-start | bytes 772
  168.7 19.2 %copy-start.16 = (f32[8,8,8,1,1,128]{5,0,2,1,4,3:T(8,128)S(1)}, f32[8,8,8,1,1,128]{5,0,2,1,4,3:T(8,128)}, u32[]{:S(2)}) copy-start(f32[8,8,8,1,1,128]{5,0,2,1,4,3:T(8,128)} %copy-done.15) | copy-start | bytes 786436
  168.7 19.2 %copy-start.24 = (f32[1,1,8,8,8,1,1,128]{7,4,3,2,1,0,6,5:T(8,128)S(1)}, f32[1,1,8,8,8,1,1,128]{7,4,3,2,1,0,6,5:T(8,128)}, u32[]{:S(2)}) copy-start(f32[1,1,8,8,8,1,1,128]{7,4,3,2,1,0,6,5:T(8,128)} %copy-done.23) | copy-start | bytes 786436
  172.0 6.2 %collective-permute-start.3 = (f32[2,8,1,8,1,1,128]{6,1,3,2,5,4,0:T(8,128)S(1)}, f32[2,8,1,8,1,1,128]{6,1,3,2,5,4,0:T(8,128)S(1)}, u32[]{:S(2)}, u32[]{:S(2)}) collective-permute-start(f32[2,8,1,8,1,1,128]{6,1,3,2,5,4,0:T(8,128)S(1)} %get-tuple-element.70), channel_id=1, source_target_pairs={{1,0},{2,1},{3,2},{5,4},{6,5},{7,6},{9,8},{10,9},{11,10},{13,12},{... | collective-permute-start | bytes 196616 | tf_op jit(solution)/shard_map/ppermute | solution.py:16
  174.5 14.6 %copy-start.38 = (f32[2,8,8,1,1,1,128]{6,1,3,2,5,4,0:T(8,128)}, f32[2,8,8,1,1,1,128]{6,1,3,2,5,4,0:T(8,128)S(1)}, u32[]{:S(2)}) copy-start(f32[2,8,8,1,1,1,128]{6,1,3,2,5,4,0:T(8,128)S(1)} %get-tuple-element.112) | copy-start | bytes 196612
  174.5 14.6 %copy-start.39 = (f32[2,8,8,1,1,1,128]{6,1,3,2,5,4,0:T(8,128)}, f32[2,8,8,1,1,1,128]{6,1,3,2,5,4,0:T(8,128)S(1)}, u32[]{:S(2)}) copy-start(f32[2,8,8,1,1,1,128]{6,1,3,2,5,4,0:T(8,128)S(1)} %get-tuple-element.113) | copy-start | bytes 196612
  178.5 12.1 %copy-start.42 = (s32[4096]{0:T(1024)S(1)}, s32[4096]{0:T(1024)}, u32[]{:S(2)}) copy-start(s32[4096]{0:T(1024)} %copy-done.41) | copy-start | bytes 49156
  178.9 11.5 %copy-start.6 = (f32[2,8,8,8,1,1,128]{6,1,3,2,5,4,0:T(8,128)}, f32[2,8,8,8,1,1,128]{6,1,3,2,5,4,0:T(8,128)S(1)}, u32[]{:S(2)}) copy-start(f32[2,8,8,8,1,1,128]{6,1,3,2,5,4,0:T(8,128)S(1)} %get-tuple-element.59) | copy-start | bytes 1572868
  190.4 17.1 %copy-start.7 = (f32[2,512,128]{2,1,0:T(8,128)}, f32[2,512,128]{2,1,0:T(8,128)S(1)}, u32[]{:S(2)}) copy-start(f32[2,512,128]{2,1,0:T(8,128)S(1)} %add.1139) | copy-start | bytes 1572868
  216.4 11.3 %copy-start.37 = (f32[8,8,8]{0,2,1:T(8,128)S(1)}, f32[8,8,8]{0,2,1:T(8,128)}, u32[]{:S(2)}) copy-start(f32[8,8,8]{0,2,1:T(8,128)} %copy-done.36) | copy-start | bytes 6148
  216.4 13.5 %copy-start.19 = (f32[1,1,8,8,8,1,1,128]{7,4,3,2,1,0,6,5:T(8,128)S(1)}, f32[1,1,8,8,8,1,1,128]{7,4,3,2,1,0,6,5:T(8,128)}, u32[]{:S(2)}) copy-start(f32[1,1,8,8,8,1,1,128]{7,4,3,2,1,0,6,5:T(8,128)} %copy-done.18) | copy-start | bytes 786436
  216.4 13.5 %copy-start.21 = (f32[8,8,8]{0,2,1:T(8,128)S(1)}, f32[8,8,8]{0,2,1:T(8,128)}, u32[]{:S(2)}) copy-start(f32[8,8,8]{0,2,1:T(8,128)} %copy-done.20) | copy-start | bytes 6148
  216.4 13.5 %copy-start.27 = (f32[8,8,8,128]{3,2,1,0:T(8,128)S(1)}, f32[8,8,8,128]{3,2,1,0:T(8,128)}, u32[]{:S(2)}) copy-start(f32[8,8,8,128]{3,2,1,0:T(8,128)} %get-tuple-element.72) | copy-start | bytes 786436
  216.5 13.5 %copy-start.57 = (f32[128]{0:T(128)S(1)}, f32[128]{0:T(128)}, u32[]{:S(2)}) copy-start(f32[128]{0:T(128)} %copy-done.55) | copy-start | bytes 1540
  216.5 16.3 %copy-start.50 = (s32[2048]{0:T(1024)S(1)}, s32[2048]{0:T(1024)}, u32[]{:S(2)}) copy-start(s32[2048]{0:T(1024)} %copy-done.49) | copy-start | bytes 24580
  221.5 31.9 %all-to-all-start.2 = ((f32[128,1,32]{2,1,0:T(1,128)}), f32[128,1,32]{2,1,0:T(1,128)}, u32[]{:S(2)}, u32[]{:S(2)}) async-start(f32[128,1,32]{2,1,0:T(1,128)} %bitcast.134), calls=%async_computation.2 | async-start | bytes 131072 | tf_op jit(solution)/shard_map/all_to_all | solution.py:154
  289.9 26.4 %copy-start.5 = (f32[8,8,1,1]{1,0,3,2:T(8,128)S(1)}, f32[8,8,1,1]{1,0,3,2:T(8,128)}, u32[]{:S(2)}) copy-start(f32[8,8,1,1]{1,0,3,2:T(8,128)} %constant.408) | copy-start | bytes 772
  289.9 28.9 %copy-start.22 = (f32[8,8,8]{0,2,1:T(8,128)S(1)}, f32[8,8,8]{0,2,1:T(8,128)}, u32[]{:S(2)}) copy-start(f32[8,8,8]{0,2,1:T(8,128)} %copy-done.20) | copy-start | bytes 6148
  290.0 28.9 %copy-start.54 = (f32[128]{0:T(128)S(1)}, f32[128]{0:T(128)}, u32[]{:S(2)}) copy-start(f32[128]{0:T(128)} %copy-done.52) | copy-start | bytes 1540
  290.0 28.9 %copy-start.58 = (f32[128]{0:T(128)S(1)}, f32[128]{0:T(128)}, u32[]{:S(2)}) copy-start(f32[128]{0:T(128)} %copy-done.55) | copy-start | bytes 1540
  290.0 6.5 %collective-permute-start.9 = (f32[2,1,8,8,1,1,128]{6,1,3,2,5,4,0:T(1,128)S(1)}, f32[2,1,8,8,1,1,128]{6,1,3,2,5,4,0:T(1,128)S(1)}, u32[]{:S(2)}, u32[]{:S(2)}) collective-permute-start(f32[2,1,8,8,1,1,128]{6,1,3,2,5,4,0:T(1,128)S(1)} %bitcast.575), channel_id=1, source_target_pairs={{4,0},{8,4},{12,8},{16,12},{20,16},{24,20},{28,24},{32,28},{36,32}... | collective-permute-start | bytes 196616 | tf_op jit(solution)/shard_map/ppermute | solution.py:16
  294.3 7.7 %collective-permute-start.8 = (f32[2,1,8,8,1,1,128]{6,1,3,2,5,4,0:T(1,128)S(1)}, f32[2,1,8,8,1,1,128]{6,1,3,2,5,4,0:T(1,128)S(1)}, u32[]{:S(2)}, u32[]{:S(2)}) collective-permute-start(f32[2,1,8,8,1,1,128]{6,1,3,2,5,4,0:T(1,128)S(1)} %bitcast.579), channel_id=1, source_target_pairs={{0,4},{4,8},{8,12},{12,16},{16,20},{20,24},{24,28},{28,32},{32,36}... | collective-permute-start | bytes 196616 | tf_op jit(solution)/shard_map/ppermute | solution.py:16
  296.2 27.5 %copy-start.10 = (f32[1,1,8,8,8,1,1,128]{7,4,3,2,1,0,6,5:T(8,128)S(1)}, f32[1,1,8,8,8,1,1,128]{7,4,3,2,1,0,6,5:T(8,128)}, u32[]{:S(2)}) copy-start(f32[1,1,8,8,8,1,1,128]{7,4,3,2,1,0,6,5:T(8,128)} %copy-done.9) | copy-start | bytes 786436
  296.2 27.5 %copy-start.17 = (f32[8,8,8,1,1,128]{5,0,2,1,4,3:T(8,128)S(1)}, f32[8,8,8,1,1,128]{5,0,2,1,4,3:T(8,128)}, u32[]{:S(2)}) copy-start(f32[8,8,8,1,1,128]{5,0,2,1,4,3:T(8,128)} %copy-done.15) | copy-start | bytes 786436
  302.1 6.2 %collective-permute-start.10 = (f32[2,8,1,8,1,1,128]{6,1,3,2,5,4,0:T(8,128)S(1)}, f32[2,8,1,8,1,1,128]{6,1,3,2,5,4,0:T(8,128)S(1)}, u32[]{:S(2)}, u32[]{:S(2)}) collective-permute-start(f32[2,8,1,8,1,1,128]{6,1,3,2,5,4,0:T(8,128)S(1)} %pad_maximum_fusion.6), channel_id=1, source_target_pairs={{0,1},{1,2},{2,3},{4,5},{5,6},{6,7},{8,9},{9,10},{10,11},{12,13},{... | collective-permute-start | bytes 196616 | tf_op jit(solution)/shard_map/ppermute | solution.py:16
  308.3 6.2 %collective-permute-start.11 = (f32[2,8,1,8,1,1,128]{6,1,3,2,5,4,0:T(8,128)S(1)}, f32[2,8,1,8,1,1,128]{6,1,3,2,5,4,0:T(8,128)S(1)}, u32[]{:S(2)}, u32[]{:S(2)}) collective-permute-start(f32[2,8,1,8,1,1,128]{6,1,3,2,5,4,0:T(8,128)S(1)} %get-tuple-element.57), channel_id=1, source_target_pairs={{1,0},{2,1},{3,2},{5,4},{6,5},{7,6},{9,8},{10,9},{11,10},{13,12},{... | collective-permute-start | bytes 196616 | tf_op jit(solution)/shard_map/ppermute | solution.py:16
  314.4 13.3 %copy-start.8 = (f32[2,512,128]{2,1,0:T(8,128)S(1)}, f32[2,512,128]{2,1,0:T(8,128)}, u32[]{:S(2)}) copy-start(f32[2,512,128]{2,1,0:T(8,128)} %copy-done.7) | copy-start | bytes 1572868
  361.0 16.2 %copy-start.51 = (s32[2048]{0:T(1024)S(1)}, s32[2048]{0:T(1024)}, u32[]{:S(2)}) copy-start(s32[2048]{0:T(1024)} %copy-done.49) | copy-start | bytes 24580
  361.8 27.3 %all-to-all-start.3 = ((f32[128,1,32]{2,1,0:T(1,128)}), f32[128,1,32]{2,1,0:T(1,128)}, u32[]{:S(2)}, u32[]{:S(2)}) async-start(f32[128,1,32]{2,1,0:T(1,128)} %bitcast.182), calls=%async_computation.3 | async-start | bytes 131072 | tf_op jit(solution)/shard_map/all_to_all | solution.py:154
  370.2 20.6 %copy-start.48 = (s32[2048]{0:T(1024)S(1)}, s32[2048]{0:T(1024)}, u32[]{:S(2)}) copy-start(s32[2048]{0:T(1024)} %copy-done.47) | copy-start | bytes 24580
  377.3 25.3 %copy-start.46 = (f32[2048]{0:T(1024)S(1)}, f32[2048]{0:T(1024)}, u32[]{:S(2)}) copy-start(f32[2048]{0:T(1024)} %copy-done.45) | copy-start | bytes 24580
  377.3 25.3 %copy-start.44 = (s32[2048]{0:T(1024)S(1)}, s32[2048]{0:T(1024)}, u32[]{:S(2)}) copy-start(s32[2048]{0:T(1024)} %copy-done.43) | copy-start | bytes 24580
  414.4 26.0 %copy-start.2 = (f32[2,8,8,8,1,1,128]{6,3,2,1,0,5,4:T(8,128)S(1)}, f32[2,8,8,8,1,1,128]{6,3,2,1,0,5,4:T(8,128)}, u32[]{:S(2)}) copy-start(f32[2,8,8,8,1,1,128]{6,3,2,1,0,5,4:T(8,128)} %copy-done.1) | copy-start | bytes 1572868
  414.4 6.6 %collective-permute-start.13 = (f32[2,1,8,8,1,1,128]{6,1,3,2,5,4,0:T(1,128)S(1)}, f32[2,1,8,8,1,1,128]{6,1,3,2,5,4,0:T(1,128)S(1)}, u32[]{:S(2)}, u32[]{:S(2)}) collective-permute-start(f32[2,1,8,8,1,1,128]{6,1,3,2,5,4,0:T(1,128)S(1)} %bitcast.577), channel_id=1, source_target_pairs={{4,0},{8,4},{12,8},{16,12},{20,16},{24,20},{28,24},{32,28},{36,32}... | collective-permute-start | bytes 196616 | tf_op jit(solution)/shard_map/ppermute | solution.py:16
  418.8 7.7 %collective-permute-start.12 = (f32[2,1,8,8,1,1,128]{6,1,3,2,5,4,0:T(1,128)S(1)}, f32[2,1,8,8,1,1,128]{6,1,3,2,5,4,0:T(1,128)S(1)}, u32[]{:S(2)}, u32[]{:S(2)}) collective-permute-start(f32[2,1,8,8,1,1,128]{6,1,3,2,5,4,0:T(1,128)S(1)} %bitcast.581), channel_id=1, source_target_pairs={{0,4},{4,8},{8,12},{12,16},{16,20},{20,24},{24,28},{28,32},{32,36}... | collective-permute-start | bytes 196616 | tf_op jit(solution)/shard_map/ppermute | solution.py:16
  426.6 6.2 %collective-permute-start.14 = (f32[2,8,1,8,1,1,128]{6,1,3,2,5,4,0:T(8,128)S(1)}, f32[2,8,1,8,1,1,128]{6,1,3,2,5,4,0:T(8,128)S(1)}, u32[]{:S(2)}, u32[]{:S(2)}) collective-permute-start(f32[2,8,1,8,1,1,128]{6,1,3,2,5,4,0:T(8,128)S(1)} %pad_maximum_fusion.4), channel_id=1, source_target_pairs={{0,1},{1,2},{2,3},{4,5},{5,6},{6,7},{8,9},{9,10},{10,11},{12,13},{... | collective-permute-start | bytes 196616 | tf_op jit(solution)/shard_map/ppermute | solution.py:16
  432.8 6.2 %collective-permute-start.15 = (f32[2,8,1,8,1,1,128]{6,1,3,2,5,4,0:T(8,128)S(1)}, f32[2,8,1,8,1,1,128]{6,1,3,2,5,4,0:T(8,128)S(1)}, u32[]{:S(2)}, u32[]{:S(2)}) collective-permute-start(f32[2,8,1,8,1,1,128]{6,1,3,2,5,4,0:T(8,128)S(1)} %get-tuple-element.46), channel_id=1, source_target_pairs={{1,0},{2,1},{3,2},{5,4},{6,5},{7,6},{9,8},{10,9},{11,10},{13,12},{... | collective-permute-start | bytes 196616 | tf_op jit(solution)/shard_map/ppermute | solution.py:16
  (20 other events, 151.3 us)
where the time goes:
time: 448 us; the launch traced here: 442 us
  local copies, waits for them, and re-layouts  211 us (47%)
  starting transfers between devices  81.8 us (18%)
  other arithmetic  79.4 us (18%)
  waiting for transfers between devices  36.1 us (8%)
  matrix products  31.2 us (7%)
    gather x6, local copies, waits for them, and re-layouts, one_block(): element_values = element_rows[ids].reshape(-1, 8, 8, 8)  78.8 us
    ppermute x16, starting transfers between devices, passed_along(): lax.ppermute(value, axis, [(source, source + steps) for source in range(l...  46 us
    gather x3, local copies, waits for them, and re-layouts, rate(): donor_values = replies[target]  44.2 us
    gather x3, local copies, waits for them, and re-layouts, rate(): current = values.reshape(-1)[flat_index]  44.1 us
    scatter-add x3, other arithmetic, rate(): local = local.reshape(-1).at[flat_index].add(added).reshape(shape_full)  35.5 us
    ppermute x16, waiting for transfers between devices, passed_along(): lax.ppermute(value, axis, [(source, source + steps) for source in range(l...  33.7 us
    all_to_all x3, starting transfers between devices, send_answers(): lax.all_to_all(answers.reshape(devices, capacity), ('gx', 'gy'), split_ax...  24.3 us
    gather x1, local copies, waits for them, and re-layouts, body(): point_mass = volume_factor * cube_flat[point_q]  13.2 us
  transfers between devices with their start and end apart: 20, of which 10 were waited for; matrix products, arithmetic and copies ran while one was open for 37% of the time, Pallas kernels for 0%

commit v1 on v0

v1 whole, which is shorter than its diff:
```python
import jax
import jax.numpy as jnp
import numpy as np
from jax import lax
from jax.experimental import pallas as pl
from jax.experimental.pallas import tpu as pltpu
from jax.sharding import PartitionSpec as P

time_step = 0.01
penalty_rate = 50.0
metric = 2.0
volume_factor = 0.125
node_inner = [0.8717401485096066, 0.5917001814331423, 0.20929921790247888]
f32 = jnp.float32
bf16 = jnp.bfloat16
i32 = jnp.int32


def legendre_seven(point):
    before, current = (1.0, point)
    for order in range(1, 7):
        before, current = (
            current,
            ((2 * order + 1) * point * current - order * before) / (order + 1),
        )
    return current


def gll_tables():
    degree = 7
    gll_nodes = [-1.0] + [-v for v in node_inner] + node_inner[::-1] + [1.0]
    end_values = [legendre_seven(v) for v in gll_nodes]
    weights = [2.0 / (degree * (degree + 1) * v * v) for v in end_values]
    derivative = [[0.0] * 8 for _ in range(8)]
    for a in range(8):
        for b in range(8):
            if a != b:
                derivative[a][b] = end_values[a] / (end_values[b] * (gll_nodes[a] - gll_nodes[b]))
    derivative[0][0] = -degree * (degree + 1) / 4.0
    derivative[7][7] = degree * (degree + 1) / 4.0
    return (gll_nodes, weights, derivative)


NODES, WEIGHTS, DERIV = gll_tables()
DERIV_T = [[DERIV[b][a] for b in range(8)] for a in range(8)]


def split_two(x):
    hi = x.astype(bf16)
    lo = (x - hi.astype(f32)).astype(bf16)
    return hi, lo


def block_matrix(table):
    full = np.kron(np.eye(16), np.asarray(table, np.float64)).astype(np.float32)
    hi = full.astype(jnp.bfloat16)
    lo = (full - hi.astype(np.float32)).astype(jnp.bfloat16)
    return np.concatenate([hi, lo, hi], axis=1)


def apply_table(table, pieces):
    even = [pieces[b] + pieces[7 - b] for b in range(4)]
    odd = [pieces[b] - pieces[7 - b] for b in range(4)]
    outs = [None] * 8
    for a in range(4):
        s = None
        d = None
        for b in range(4):
            cs = 0.5 * (table[a][b] - table[a][7 - b])
            cd = 0.5 * (table[a][b] + table[a][7 - b])
            s = cs * odd[b] if s is None else s + cs * odd[b]
            d = cd * even[b] if d is None else d + cd * even[b]
        outs[a] = d + s
        outs[7 - a] = s - d
    return outs


def dot_nn(a, b):
    return lax.dot_general(a, b, (((1,), (0,)), ((), ())), preferred_element_type=f32)


def dot_nt(a, b):
    return lax.dot_general(a, b, (((1,), (1,)), ((), ())), preferred_element_type=f32)


def one_hot_rows(row, count, dtype=bf16):
    ids = lax.broadcasted_iota(i32, (count, row.shape[-1]), 0)
    return jnp.where(ids == row, 1.0, 0.0).astype(dtype)


def weight_rows():
    k = lax.broadcasted_iota(i32, (8, 128), 0)
    out = jnp.zeros((8, 128), f32)
    for j in range(8):
        out = jnp.where(k == j, WEIGHTS[j], out)
    return out


def query_kernel(owner_ref, donor_ref, coords_ref, payload_ref, rank_ref):
    rows = owner_ref.shape[1]
    half = rows // 2
    owner = owner_ref[...]
    step = 256
    before = (
        lax.broadcasted_iota(i32, (step, step), 0) < lax.broadcasted_iota(i32, (step, step), 1)
    )
    before = jnp.where(before, 1.0, 0.0).astype(bf16)
    total = jnp.zeros((128, 1), f32)
    acc = [jnp.zeros((128, 128), f32) for _ in range(3)]
    for c in range(rows // step):
        sl = slice(c * step, (c + 1) * step)
        oh = one_hot_rows(owner[:, sl], 128)
        ohf = oh.astype(f32)
        cum = dot_nn(oh, before) + total
        rank = jnp.sum(cum * ohf, axis=0, keepdims=True)
        total = total + jnp.sum(ohf, axis=1, keepdims=True)
        rank_i = rank.astype(i32)
        rank_ref[:, sl] = rank_i
        pick = lax.broadcasted_iota(i32, (32, step), 0) == rank_i
        col = lax.broadcasted_iota(i32, (1, step), 1) + c * step
        ident = (jnp.where(col < half, 128, 0) + donor_ref[:, sl]).astype(f32)
        parts = [[], [], []]
        for v in range(3):
            x = coords_ref[v : v + 1, sl]
            hi = x.astype(bf16).astype(f32)
            rest = x - hi
            mid = rest.astype(bf16).astype(f32)
            for p, val in enumerate((hi, mid, rest - mid)):
                parts[p].append(jnp.where(pick, val, 0.0).astype(bf16))
        zero = jnp.zeros((32, step), bf16)
        parts[0].append(jnp.where(pick, ident, 0.0).astype(bf16))
        parts[1].append(zero)
        parts[2].append(zero)
        for p in range(3):
            acc[p] = acc[p] + dot_nt(oh, jnp.concatenate(parts[p], axis=0))
    payload_ref[...] = acc[0] + (acc[1] + acc[2])


def prepare_kernel(flags_ref, point_ref, load_ref, inv_ref):
    half = point_ref.shape[1] // 2
    wk = weight_rows()
    for m in range(2):
        point = point_ref[:, m * half : (m + 1) * half]
        q = lax.shift_right_logical(point, 7)
        e = lax.bitwise_and(point, 127)
        count = dot_nt(one_hot_rows(q, 512), one_hot_rows(e, 128))
        for ij in range(64):
            c = penalty_rate * volume_factor * WEIGHTS[ij // 8] * WEIGHTS[ij % 8]
            load_ref[m, ij * 8 : ij * 8 + 8, :] = (c * wk) * count[ij * 8 : ij * 8 + 8, :]
    k = lax.broadcasted_iota(i32, (8, 128), 0)
    e = lax.broadcasted_iota(i32, (8, 128), 1)
    shared = ((k == 0) & (e > 0)) | ((k == 7) & (e < 127))
    base = time_step / (volume_factor * wk * jnp.where(shared, 2.0, 1.0))
    for ij in range(64):
        i, j = ij // 8, ij % 8
        val = base * (1.0 / (WEIGHTS[i] * WEIGHTS[j]))
        if i == 0:
            val = val * flags_ref[0]
        if i == 7:
            val = val * flags_ref[1]
        if j == 0:
            val = val * flags_ref[2]
        if j == 7:
            val = val * flags_ref[3]
        inv_ref[ij * 8 : ij * 8 + 8, :] = val


def local_kernel(u_ref, vel_ref, nu_ref, load_ref, dz_ref, dzt_ref, out_ref, ax_ref, ay_ref, fz_ref):
    wk = weight_rows()

    def depth(table, pick):
        chunks = []
        for c in range(4):
            rows = slice(c * 128, (c + 1) * 128)
            hi, lo = split_two(jnp.concatenate([pick(0, rows), pick(1, rows)], axis=1))
            chunks.append(dot_nn(table, jnp.concatenate([hi, hi, lo], axis=0)))
        return chunks

    az = depth(dz_ref[...], lambda m, rows: u_ref[m, rows, :])
    for m in range(2):
        for j in range(8):
            outs = apply_table(DERIV, [u_ref[m, i * 64 + j * 8 : i * 64 + j * 8 + 8, :] for i in range(8)])
            for i in range(8):
                ax_ref[m, i * 64 + j * 8 : i * 64 + j * 8 + 8, :] = outs[i]
        wnu = 4.0 * volume_factor * wk * nu_ref[m : m + 1, :]
        wad = 2.0 * volume_factor * wk
        for i in range(8):
            outs = apply_table(DERIV, [u_ref[m, i * 64 + j * 8 : i * 64 + j * 8 + 8, :] for j in range(8)])
            fluxes = []
            for j in range(8):
                ij = i * 8 + j
                rows = slice(ij * 8, ij * 8 + 8)
                c = WEIGHTS[i] * WEIGHTS[j]
                gx = ax_ref[m, rows, :]
                gy = outs[j]
                gz = az[ij // 16][(ij % 16) * 8 : (ij % 16) * 8 + 8, m * 128 : (m + 1) * 128]
                adv = vel_ref[0, m, rows, :] * gx + vel_ref[1, m, rows, :] * gy + vel_ref[2, m, rows, :] * gz
                out_ref[m, rows, :] = -((c * wad) * adv) - load_ref[m, rows, :] * u_ref[m, rows, :]
                flux = c * wnu
                ax_ref[m, rows, :] = flux * gx
                fz_ref[m, rows, :] = flux * gz
                fluxes.append(flux * gy)
            outs = apply_table(DERIV_T, fluxes)
            for j in range(8):
                rows = slice(i * 64 + j * 8, i * 64 + j * 8 + 8)
                out_ref[m, rows, :] = out_ref[m, rows, :] - outs[j]
    bz = depth(dzt_ref[...], lambda m, rows: fz_ref[m, rows, :])
    for m in range(2):
        for j in range(8):
            outs = apply_table(DERIV_T, [ax_ref[m, i * 64 + j * 8 : i * 64 + j * 8 + 8, :] for i in range(8)])
            for i in range(8):
                ij = i * 8 + j
                rows = slice(ij * 8, ij * 8 + 8)
                gz = bz[ij // 16][(ij % 16) * 8 : (ij % 16) * 8 + 8, m * 128 : (m + 1) * 128]
                out_ref[m, rows, :] = (out_ref[m, rows, :] - outs[i]) - gz


def interpolate(u, received_ref, ans_ref, wx_ref, wy_ref, wz_ref):
    parts = [split_two(v) for v in u]
    cat = jnp.concatenate([parts[0][0], parts[1][0], parts[0][1], parts[1][1]], axis=1)
    turned = received_ref[...].T
    for v, ref in enumerate((wx_ref, wy_ref, wz_ref)):
        x = turned[v * 32 : v * 32 + 32, :]
        diff = [x - NODES[m] for m in range(8)]
        pre = [None] * 8
        suf = [None] * 8
        for m in range(1, 8):
            pre[m] = diff[m - 1] if pre[m - 1] is None else pre[m - 1] * diff[m - 1]
        for m in range(6, -1, -1):
            suf[m] = diff[m + 1] if suf[m + 1] is None else suf[m + 1] * diff[m + 1]
        for j in range(8):
            c = 1.0
            for m in range(8):
                if m != j:
                    c = c / (NODES[j] - NODES[m])
            w = suf[j] if pre[j] is None else (pre[j] if suf[j] is None else pre[j] * suf[j])
            w = w * c
            if ref is wz_ref:
                ref[:, j, :] = w
            else:
                ref[j] = w
    ids = turned[96:128, :].astype(i32)
    rows = []
    for g in range(16):
        hot = [one_hot_rows(ids[s : s + 1, :], 256) for s in (2 * g, 2 * g + 1)]
        hot = jnp.concatenate(hot, axis=1)
        got = dot_nn(cat, jnp.concatenate([hot, hot], axis=0))
        for b in range(2):
            s = 2 * g + b
            total = None
            for j in range(8):
                acc = None
                for i in range(8):
                    term = wx_ref[i, s : s + 1, :] * got[i * 64 + j * 8 : i * 64 + j * 8 + 8, b * 128 : (b + 1) * 128]
                    acc = term if acc is None else acc + term
                acc = acc * wy_ref[j, s : s + 1, :]
                total = acc if total is None else total + acc
            rows.append(jnp.sum(total * wz_ref[s], axis=0, keepdims=True))
    answers = jnp.concatenate(rows + [jnp.zeros((96, 128), f32)], axis=0)
    ans_ref[...] = answers.T


def first_kernel(u_ref, received_ref, ans_ref, wx_ref, wy_ref, wz_ref):
    interpolate([u_ref[0], u_ref[1]], received_ref, ans_ref, wx_ref, wy_ref, wz_ref)


def penalty_kernel(replies_ref, owner_ref, rank_ref, point_ref, local_ref, out_ref, xl_ref, xr_ref, yl_ref, yr_ref):
    half = point_ref.shape[1] // 2
    hi, lo = split_two(replies_ref[...].T[0:32, :])
    lhs = jnp.concatenate([hi, lo], axis=1)
    wk = weight_rows()
    for m in range(2):
        sl = slice(m * half, (m + 1) * half)
        oh = one_hot_rows(owner_ref[:, sl], 128)
        got = dot_nn(lhs, jnp.concatenate([oh, oh], axis=0))
        pick = lax.broadcasted_iota(i32, (32, half), 0) == rank_ref[:, sl]
        g = jnp.sum(jnp.where(pick, got, 0.0), axis=0, keepdims=True)
        ghi = g.astype(bf16).astype(f32)
        glo = g - ghi
        point = point_ref[:, sl]
        q = lax.shift_right_logical(point, 7)
        e = lax.bitwise_and(point, 127)
        at = lax.broadcasted_iota(i32, (128, half), 0) == e
        rhs = jnp.concatenate(
            [jnp.where(at, ghi, 0.0).astype(bf16), jnp.where(at, glo, 0.0).astype(bf16)], axis=0
        )
        both = dot_nt(one_hot_rows(q, 512), rhs)
        summed = both[:, 0:128] + both[:, 128:256]
        for ij in range(64):
            rows = slice(ij * 8, ij * 8 + 8)
            i, j = ij // 8, ij % 8
            c = penalty_rate * volume_factor * WEIGHTS[i] * WEIGHTS[j]
            val = local_ref[m, rows, :] + (c * wk) * summed[rows, :]
            out_ref[m, rows, :] = val
            if i == 0:
                xl_ref[m, j * 8 : j * 8 + 8, :] = val
            if i == 7:
                xr_ref[m, j * 8 : j * 8 + 8, :] = val
            if j == 0:
                yl_ref[m, i * 8 : i * 8 + 8, :] = val
            if j == 7:
                yr_ref[m, i * 8 : i * 8 + 8, :] = val


def edge_kernel(yl_ref, yr_ref, xn_ref, xp_ref, yl_out, yr_out):
    for m in range(2):
        for src, dst, j in ((yl_ref, yl_out, 0), (yr_ref, yr_out, 7)):
            dst[m, 8:56, :] = src[m, 8:56, :]
            dst[m, 0:8, :] = src[m, 0:8, :] + xp_ref[m, j * 8 : j * 8 + 8, :]
            dst[m, 56:64, :] = src[m, 56:64, :] + xn_ref[m, j * 8 : j * 8 + 8, :]


def finish(blend, v_ref, xn_ref, xp_ref, yn_ref, yp_ref, inv_ref, start_ref, u_ref, new_ref, work_ref):
    lane = lax.broadcasted_iota(i32, (64, 128), 1)
    for m in range(2):
        for ij in range(64):
            rows = slice(ij * 8, ij * 8 + 8)
            i, j = ij // 8, ij % 8
            val = v_ref[m, rows, :]
            if j == 0:
                val = val + yp_ref[m, i * 8 : i * 8 + 8, :]
            elif j == 7:
                val = val + yn_ref[m, i * 8 : i * 8 + 8, :]
            if i == 0 and j not in (0, 7):
                val = val + xp_ref[m, j * 8 : j * 8 + 8, :]
            elif i == 7 and j not in (0, 7):
                val = val + xn_ref[m, j * 8 : j * 8 + 8, :]
            elif i == 0:
                val = val + xp_ref[m, j * 8 : j * 8 + 8, :]
            elif i == 7:
                val = val + xn_ref[m, j * 8 : j * 8 + 8, :]
            work_ref[m, rows, :] = val
        left = work_ref[m, pl.ds(0, 64, stride=8), :]
        right = work_ref[m, pl.ds(7, 64, stride=8), :]
        work_ref[m, pl.ds(0, 64, stride=8), :] = left + jnp.where(lane > 0, pltpu.roll(right, 1, 1), 0.0)
        work_ref[m, pl.ds(7, 64, stride=8), :] = right + jnp.where(lane < 127, pltpu.roll(left, 127, 1), 0.0)
        new = u_ref[m] + inv_ref[...] * work_ref[m]
        if blend is not None:
            new = blend[0] * start_ref[m] + blend[1] * new
        new_ref[m] = new


def step_kernel(blend, v_ref, xn_ref, xp_ref, yn_ref, yp_ref, inv_ref, start_ref, u_ref, received_ref,
                new_ref, ans_ref, work_ref, wx_ref, wy_ref, wz_ref):
    finish(blend, v_ref, xn_ref, xp_ref, yn_ref, yp_ref, inv_ref, start_ref, u_ref, new_ref, work_ref)
    interpolate([new_ref[0], new_ref[1]], received_ref, ans_ref, wx_ref, wy_ref, wz_ref)


def last_kernel(blend, v_ref, xn_ref, xp_ref, yn_ref, yp_ref, inv_ref, start_ref, u_ref, new_ref, work_ref):
    finish(blend, v_ref, xn_ref, xp_ref, yn_ref, yp_ref, inv_ref, start_ref, u_ref, new_ref, work_ref)


def call(kernel, outs, ins, scratch=(), smem_first=False):
    specs = [pl.BlockSpec(memory_space=pltpu.VMEM)] * len(ins)
    if smem_first:
        specs[0] = pl.BlockSpec(memory_space=pltpu.SMEM)
    return pl.pallas_call(
        kernel,
        out_shape=[jax.ShapeDtypeStruct(s, d) for s, d in outs],
        in_specs=specs,
        out_specs=[pl.BlockSpec(memory_space=pltpu.VMEM)] * len(outs),
        scratch_shapes=list(scratch),
        compiler_params=pltpu.CompilerParams(vmem_limit_bytes=24 << 20),
    )(*ins)


def passed_along(value, axis, steps):
    count = lax.axis_size(axis)
    leading, last = (max(0, -steps), min(count, count - steps))
    return lax.ppermute(value, axis, [(source, source + steps) for source in range(leading, last)])


def exchange(x):
    return lax.all_to_all(x, ("gx", "gy"), split_axis=0, concat_axis=0, tiled=True)


def body(scalar, velocity, diffusivity, recv_owner, donor_elem, recv_point, recv_coords):
    rows = recv_owner.shape[0]
    field = (2, 512, 128)
    face = (2, 64, 128)
    start = scalar.reshape(field)
    flow = velocity.reshape((3,) + field)
    nu = diffusivity.reshape(2, 128)
    owner = recv_owner.reshape(1, rows)
    donor = donor_elem.reshape(1, rows)
    point = recv_point.reshape(1, rows)
    deep = jnp.asarray(block_matrix(DERIV))
    deep_t = jnp.asarray(block_matrix(DERIV_T))

    payload, rank = call(
        query_kernel, [((128, 128), f32), ((1, rows), i32)], (owner, donor, recv_coords)
    )
    received = exchange(payload)

    ix, iy = lax.axis_index("gx"), lax.axis_index("gy")
    inside = [ix > 0, ix < lax.axis_size("gx") - 1, iy > 0, iy < lax.axis_size("gy") - 1]
    flags = jnp.where(jnp.stack(inside), 0.5, 1.0).astype(f32)
    load, inv = call(
        prepare_kernel, [(field, f32), ((512, 128), f32)], (flags, point), smem_first=True
    )
    weights_scratch = [pltpu.VMEM((8, 32, 128), f32), pltpu.VMEM((8, 32, 128), f32), pltpu.VMEM((32, 8, 128), f32)]

    def local(u):
        return call(
            local_kernel,
            [(field, f32)],
            (u, flow, nu, load, deep, deep_t),
            [pltpu.VMEM(field, f32)] * 3,
        )[0]

    def gather_faces(replies, loc):
        v, xl, xr, yl, yr = call(
            penalty_kernel,
            [(field, f32)] + [(face, f32)] * 4,
            (replies, owner, rank, point, loc),
        )
        xn = passed_along(xl, "gx", -1)
        xp = passed_along(xr, "gx", 1)
        yl, yr = call(edge_kernel, [(face, f32)] * 2, (yl, yr, xn, xp))
        yn = passed_along(yl, "gy", -1)
        yp = passed_along(yr, "gy", 1)
        return v, xn, xp, yn, yp

    u = start
    loc = local(u)
    answers = call(first_kernel, [((128, 128), f32)], (u, received), weights_scratch)[0]
    for blend in (None, (0.75, 0.25)):
        replies = exchange(answers)
        parts = gather_faces(replies, loc)
        u, answers = call(
            lambda *refs, blend=blend: step_kernel(blend, *refs),
            [(field, f32), ((128, 128), f32)],
            parts + (inv, start, u, received),
            [pltpu.VMEM(field, f32)] + weights_scratch,
        )
        loc = local(u)
    replies = exchange(answers)
    parts = gather_faces(replies, loc)
    third = call(
        lambda *refs: last_kernel((1.0 / 3.0, 2.0 / 3.0), *refs),
        [(field, f32)],
        parts + (inv, start, u),
        [pltpu.VMEM(field, f32)],
    )[0]
    return third.reshape(scalar.shape)


def solution(mesh):
    return jax.shard_map(
        body,
        mesh=mesh,
        in_specs=(
            P(None, None, "gx", "gy", None),
            P(None, None, None, "gx", "gy", None),
            P(None, "gx", "gy", None),
            P(("gx", "gy"), None),
            P(("gx", "gy")),
            P(("gx", "gy")),
            P(None, ("gx", "gy")),
        ),
        out_specs=P(None, None, "gx", "gy", None),
        check_vma=False,
    )
```

time: 448 us -> 149 us (0.33); the launches traced: 442 us -> 147 us
  local copies, waits for them, and re-layouts: 211 us -> 19.7 us
  other arithmetic: 79.4 us -> 0.08 us
  matrix products: 31.2 us -> 0 us
  Pallas kernels: 0 us -> 22 us
  starting transfers between devices: 81.8 us -> 62.9 us
  waiting for transfers between devices: 36.1 us -> 42.2 us
    gather x13 -> x0, local copies, waits for them, and re-layouts: 180 us -> none  [the longest x6 78.8 us: one_block(): element_values = element_rows[ids].reshape(-1, 8, 8, 8)]
    scatter-add x3 -> x0, other arithmetic: 35.5 us -> none  [rate(): local = local.reshape(-1).at[flat_index].add(added).reshape(shape_full)]
    dot_general x36 -> x0, matrix products: 31.2 us -> none  [the longest x6 12.6 us: element_rate(): jnp.einsum('ai,ajkxyz->ijkxyz', derivative, scaled * grad_x, precision=hi...]
    pallas_call x0 -> x15, Pallas kernels: none -> 22 us  [call(): pl.pallas_call(kernel, out_shape=[jax.ShapeDtypeStruct(s, d) for s, d in...]
    unnamed x137 -> x58, local copies, waits for them, and re-layouts: 3.53 us -> 19.7 us
    dot_general x6 -> x0, other arithmetic: 12.7 us -> none  [one_block(): jnp.einsum('nijk,ni,nj,nk->n', element_values, wx, wy, wz, precision=lax....]
    all_to_all x4, waiting for transfers between devices: 2.31 us -> 14.9 us  [exchange(): lax.all_to_all(x, ('gx', 'gy'), split_axis=0, concat_axis=0, tiled=True)]
    ppermute x16 -> x12, starting transfers between devices: 46 us -> 34 us  [passed_along(): lax.ppermute(value, axis, [(source, source + steps) for source in range(l...]
  transfers between devices with their start and end apart: 20 -> 16, of which waited for: 10 -> 12; matrix products, arithmetic and copies ran while one was open for 37% -> 0% of each run, Pallas kernels for 0% -> 3%
where the time goes in v1:
time: 149 us; the launch traced here: 147 us
  starting transfers between devices  62.9 us (42%)
  waiting for transfers between devices  42.2 us (28%)
  Pallas kernels  22 us (15%)
  local copies, waits for them, and re-layouts  19.7 us (13%)
    ppermute x12, starting transfers between devices, passed_along(): lax.ppermute(value, axis, [(source, source + steps) for source in range(l...  34 us
    all_to_all x4, starting transfers between devices, exchange(): lax.all_to_all(x, ('gx', 'gy'), split_axis=0, concat_axis=0, tiled=True)  29 us
    ppermute x12, waiting for transfers between devices, passed_along(): lax.ppermute(value, axis, [(source, source + steps) for source in range(l...  27.3 us
    pallas_call x15, Pallas kernels, call(): pl.pallas_call(kernel, out_shape=[jax.ShapeDtypeStruct(s, d) for s, d in...  22 us
    unnamed x58, local copies, waits for them, and re-layouts  19.7 us
    all_to_all x4, waiting for transfers between devices, exchange(): lax.all_to_all(x, ('gx', 'gy'), split_axis=0, concat_axis=0, tiled=True)  14.9 us
  transfers between devices with their start and end apart: 16, of which 12 were waited for; matrix products, arithmetic and copies ran while one was open for 0% of the time, Pallas kernels for 3%

profile of v1, /device:TPU:34, one launch (start us, length us, event | category | flops | bytes accessed | tf_op | source)
XLA Modules:
  0.0 147.3 jit_solution(3377840427407301142)
XLA Ops:
  0.0 0.7 copy-done.16
  0.7 0.8 copy-done.24
  1.5 0.7 copy-done.28
  2.2 2.2 %shard_map.91 = (f32[128,128]{1,0:T(8,128)}, s32[1,2048]{1,0:T(1,128)S(1)}) custom-call(s32[1,2048]{1,0:T(1,128)S(1)} %bitcast.44, s32[1,2048]{1,0:T(1,128)S(1)} %bitcast.55, f32[3,2048]{1,0:T(4,128)S(1)} %copy-done.24), custom_call_target="tpu_custom_call" | custom-call | tf_op jit(solution)/shard_map/pallas_call | solution.py:357
  4.3 0.6 copy-done.20
  4.9 10.2 %all-to-all-start = ((f32[128,1,128]{2,1,0:T(1,128)}), f32[128,1,128]{2,1,0:T(1,128)S(1)}, u32[]{:S(2)}, u32[]{:S(2)}) async-start(f32[128,1,128]{2,1,0:T(1,128)} %bitcast.4), calls=%async_computation | async-start | bytes 131072 | tf_op jit(solution)/shard_map/all_to_all | solution.py:374
  15.2 7.8 %all-to-all-done = f32[128,1,128]{2,1,0:T(1,128)S(1)} async-done(((f32[128,1,128]{2,1,0:T(1,128)}), f32[128,1,128]{2,1,0:T(1,128)S(1)}, u32[]{:S(2)}, u32[]{:S(2)}) %all-to-all-start) | async-done | bytes 65568 | tf_op jit(solution)/shard_map/all_to_all | solution.py:374
  22.9 1.0 copy-done
  24.0 3.5 %shard_map.92 = f32[128,128]{1,0:T(8,128)} custom-call(f32[2,512,128]{2,1,0:T(8,128)S(1)} %bitcast.29, f32[128,128]{1,0:T(8,128)S(1)} %bitcast.38), custom_call_target="tpu_custom_call" | custom-call | tf_op jit(solution)/shard_map/pallas_call | solution.py:357
  27.4 6.1 %all-to-all-start.1 = ((f32[128,1,128]{2,1,0:T(1,128)}), f32[128,1,128]{2,1,0:T(1,128)S(1)}, u32[]{:S(2)}, u32[]{:S(2)}) async-start(f32[128,1,128]{2,1,0:T(1,128)} %bitcast.7), calls=%async_computation.1 | async-start | bytes 131072 | tf_op jit(solution)/shard_map/all_to_all | solution.py:374
  33.5 0.1 add_select_fusion.flags_ref
  33.6 0.7 copy-done.18
  34.3 1.3 shard_map.93
  35.6 1.0 copy-done.1
  36.6 1.4 copy-done.3
  38.0 0.9 copy-done.10
  38.9 0.9 copy-done.13
  39.8 0.7 copy-done.25
  40.5 1.2 shard_map.94.local_ref
  41.8 0.7 copy-done.21
  42.5 1.1 shard_map.95
  43.5 4.3 %collective-permute-start = (f32[2,64,128]{2,1,0:T(8,128)S(1)}, f32[2,64,128]{2,1,0:T(8,128)S(1)}, u32[]{:S(2)}, u32[]{:S(2)}) collective-permute-start(f32[2,64,128]{2,1,0:T(8,128)S(1)} %get-tuple-element.38), channel_id=1, source_target_pairs={{4,0},{8,4},{12,8},{16,12},{20,16},{24,20},{28,24},{32,28},{36,32}... | collective-permute-start | bytes 196616 | tf_op jit(solution)/shard_map/ppermute | solution.py:370
  47.8 1.9 %collective-permute-start.1 = (f32[2,64,128]{2,1,0:T(8,128)S(1)}, f32[2,64,128]{2,1,0:T(8,128)S(1)}, u32[]{:S(2)}, u32[]{:S(2)}) collective-permute-start(f32[2,64,128]{2,1,0:T(8,128)S(1)} %get-tuple-element.39), channel_id=1, source_target_pairs={{0,4},{4,8},{8,12},{12,16},{16,20},{20,24},{24,28},{28,32},{32,36}... | collective-permute-start | bytes 196616 | tf_op jit(solution)/shard_map/ppermute | solution.py:370
  49.8 5.8 %collective-permute-done.1.xp_ref.refs_2_ = f32[2,64,128]{2,1,0:T(8,128)S(1)} collective-permute-done((f32[2,64,128]{2,1,0:T(8,128)S(1)}, f32[2,64,128]{2,1,0:T(8,128)S(1)}, u32[]{:S(2)}, u32[]{:S(2)}) %collective-permute-start.1) | collective-permute-done | bytes 65568 | tf_op jit(solution)/shard_map/ppermute | solution.py:370
  55.5 2.5 %collective-permute-start.2 = (f32[2,64,128]{2,1,0:T(8,128)S(1)}, f32[2,64,128]{2,1,0:T(8,128)S(1)}, u32[]{:S(2)}, u32[]{:S(2)}) collective-permute-start(f32[2,64,128]{2,1,0:T(8,128)S(1)} %get-tuple-element.42), channel_id=1, source_target_pairs={{1,0},{2,1},{3,2},{5,4},{6,5},{7,6},{9,8},{10,9},{11,10},{13,12},{... | collective-permute-start | bytes 196616 | tf_op jit(solution)/shard_map/ppermute | solution.py:370
  58.0 3.4 %collective-permute-start.3 = (f32[2,64,128]{2,1,0:T(8,128)S(1)}, f32[2,64,128]{2,1,0:T(8,128)S(1)}, u32[]{:S(2)}, u32[]{:S(2)}) collective-permute-start(f32[2,64,128]{2,1,0:T(8,128)S(1)} %get-tuple-element.43), channel_id=1, source_target_pairs={{0,1},{1,2},{2,3},{4,5},{5,6},{6,7},{8,9},{9,10},{10,11},{12,13},{... | collective-permute-start | bytes 196616 | tf_op jit(solution)/shard_map/ppermute | solution.py:370
  61.4 0.3 collective-permute-done.2.refs_3_
  61.7 2.5 %collective-permute-done.3.refs_4_ = f32[2,64,128]{2,1,0:T(8,128)S(1)} collective-permute-done((f32[2,64,128]{2,1,0:T(8,128)S(1)}, f32[2,64,128]{2,1,0:T(8,128)S(1)}, u32[]{:S(2)}, u32[]{:S(2)}) %collective-permute-start.3) | collective-permute-done | bytes 65568 | tf_op jit(solution)/shard_map/ppermute | solution.py:370
  64.2 3.5 %shard_map.97 = (f32[2,512,128]{2,1,0:T(8,128)S(1)}, f32[128,128]{1,0:T(8,128)}) custom-call(f32[2,512,128]{2,1,0:T(8,128)S(1)} %get-tuple-element.37.refs_0_, f32[2,64,128]{2,1,0:T(8,128)S(1)} %collective-permute-done.xn_ref.refs_1_, f32[2,64,128]{2,1,0:T(8,128)S(1)} %collective-permute-done.1.xp_ref.refs_2_, ...), custom_call_target="tpu_custom_call" | custom-call | tf_op jit(solution)/shard_map/pallas_call | solution.py:357
  67.7 0.8 copy-done.7
  68.5 7.5 %all-to-all-start.2 = ((f32[128,1,128]{2,1,0:T(1,128)}), f32[128,1,128]{2,1,0:T(1,128)S(1)}, u32[]{:S(2)}, u32[]{:S(2)}) async-start(f32[128,1,128]{2,1,0:T(1,128)} %bitcast.17), calls=%async_computation.2 | async-start | bytes 131072 | tf_op jit(solution)/shard_map/all_to_all | solution.py:374
  76.0 1.0 copy-done.8
  77.1 0.9 copy-done.11
  78.0 0.9 copy-done.14
  78.9 0.7 copy-done.26
  79.5 1.2 shard_map.98.local_ref
  80.8 3.1 %all-to-all-done.2 = f32[128,1,128]{2,1,0:T(1,128)S(1)} async-done(((f32[128,1,128]{2,1,0:T(1,128)}), f32[128,1,128]{2,1,0:T(1,128)S(1)}, u32[]{:S(2)}, u32[]{:S(2)}) %all-to-all-start.2) | async-done | bytes 65568 | tf_op jit(solution)/shard_map/all_to_all | solution.py:374
  83.9 0.7 copy-done.22
  84.6 1.1 shard_map.99
  85.6 3.2 %collective-permute-start.4 = (f32[2,64,128]{2,1,0:T(8,128)S(1)}, f32[2,64,128]{2,1,0:T(8,128)S(1)}, u32[]{:S(2)}, u32[]{:S(2)}) collective-permute-start(f32[2,64,128]{2,1,0:T(8,128)S(1)} %get-tuple-element.48), channel_id=1, source_target_pairs={{4,0},{8,4},{12,8},{16,12},{20,16},{24,20},{28,24},{32,28},{36,32}... | collective-permute-start | bytes 196616 | tf_op jit(solution)/shard_map/ppermute | solution.py:370
  88.9 1.9 %collective-permute-start.5 = (f32[2,64,128]{2,1,0:T(8,128)S(1)}, f32[2,64,128]{2,1,0:T(8,128)S(1)}, u32[]{:S(2)}, u32[]{:S(2)}) collective-permute-start(f32[2,64,128]{2,1,0:T(8,128)S(1)} %get-tuple-element.49), channel_id=1, source_target_pairs={{0,4},{4,8},{8,12},{12,16},{16,20},{20,24},{24,28},{28,32},{32,36}... | collective-permute-start | bytes 196616 | tf_op jit(solution)/shard_map/ppermute | solution.py:370
  90.8 5.8 %collective-permute-done.5.xp_ref.refs_2_ = f32[2,64,128]{2,1,0:T(8,128)S(1)} collective-permute-done((f32[2,64,128]{2,1,0:T(8,128)S(1)}, f32[2,64,128]{2,1,0:T(8,128)S(1)}, u32[]{:S(2)}, u32[]{:S(2)}) %collective-permute-start.5) | collective-permute-done | bytes 65568 | tf_op jit(solution)/shard_map/ppermute | solution.py:370
  96.6 3.3 %collective-permute-start.6 = (f32[2,64,128]{2,1,0:T(8,128)S(1)}, f32[2,64,128]{2,1,0:T(8,128)S(1)}, u32[]{:S(2)}, u32[]{:S(2)}) collective-permute-start(f32[2,64,128]{2,1,0:T(8,128)S(1)} %get-tuple-element.52), channel_id=1, source_target_pairs={{1,0},{2,1},{3,2},{5,4},{6,5},{7,6},{9,8},{10,9},{11,10},{13,12},{... | collective-permute-start | bytes 196616 | tf_op jit(solution)/shard_map/ppermute | solution.py:370
  99.9 2.5 %collective-permute-start.7 = (f32[2,64,128]{2,1,0:T(8,128)S(1)}, f32[2,64,128]{2,1,0:T(8,128)S(1)}, u32[]{:S(2)}, u32[]{:S(2)}) collective-permute-start(f32[2,64,128]{2,1,0:T(8,128)S(1)} %get-tuple-element.53), channel_id=1, source_target_pairs={{0,1},{1,2},{2,3},{4,5},{5,6},{6,7},{8,9},{9,10},{10,11},{12,13},{... | collective-permute-start | bytes 196616 | tf_op jit(solution)/shard_map/ppermute | solution.py:370
  102.4 0.3 collective-permute-done.6.refs_3_
  102.7 3.4 %collective-permute-done.7.refs_4_ = f32[2,64,128]{2,1,0:T(8,128)S(1)} collective-permute-done((f32[2,64,128]{2,1,0:T(8,128)S(1)}, f32[2,64,128]{2,1,0:T(8,128)S(1)}, u32[]{:S(2)}, u32[]{:S(2)}) %collective-permute-start.7) | collective-permute-done | bytes 65568 | tf_op jit(solution)/shard_map/ppermute | solution.py:370
  106.1 1.0 copy-done.9
  107.1 3.6 %shard_map.101 = (f32[2,512,128]{2,1,0:T(8,128)S(1)}, f32[128,128]{1,0:T(8,128)}) custom-call(f32[2,512,128]{2,1,0:T(8,128)S(1)} %get-tuple-element.47.refs_0_, f32[2,64,128]{2,1,0:T(8,128)S(1)} %collective-permute-done.4.xn_ref.refs_1_, f32[2,64,128]{2,1,0:T(8,128)S(1)} %collective-permute-done.5.xp_ref.refs_2_, ...), custom_call_target="tpu_custom_call" | custom-call | tf_op jit(solution)/shard_map/pallas_call | solution.py:357
  110.7 5.1 %all-to-all-start.3 = ((f32[128,1,128]{2,1,0:T(1,128)}), f32[128,1,128]{2,1,0:T(1,128)S(1)}, u32[]{:S(2)}, u32[]{:S(2)}) async-start(f32[128,1,128]{2,1,0:T(1,128)} %bitcast.20), calls=%async_computation.3 | async-start | bytes 131072 | tf_op jit(solution)/shard_map/all_to_all | solution.py:374
  115.9 0.9 copy-done.12
  116.8 0.9 copy-done.15
  117.7 1.2 shard_map.102.local_ref
  118.9 0.8 copy-done.5
  119.7 4.0 %all-to-all-done.3 = f32[128,1,128]{2,1,0:T(1,128)S(1)} async-done(((f32[128,1,128]{2,1,0:T(1,128)}), f32[128,1,128]{2,1,0:T(1,128)S(1)}, u32[]{:S(2)}, u32[]{:S(2)}) %all-to-all-start.3) | async-done | bytes 65568 | tf_op jit(solution)/shard_map/all_to_all | solution.py:374
  123.7 1.0 copy-done.6
  124.7 1.1 shard_map.103
  125.8 3.2 %collective-permute-start.8 = (f32[2,64,128]{2,1,0:T(8,128)S(1)}, f32[2,64,128]{2,1,0:T(8,128)S(1)}, u32[]{:S(2)}, u32[]{:S(2)}) collective-permute-start(f32[2,64,128]{2,1,0:T(8,128)S(1)} %get-tuple-element.57), channel_id=1, source_target_pairs={{4,0},{8,4},{12,8},{16,12},{20,16},{24,20},{28,24},{32,28},{36,32}... | collective-permute-start | bytes 196616 | tf_op jit(solution)/shard_map/ppermute | solution.py:370
  129.0 1.9 %collective-permute-start.9 = (f32[2,64,128]{2,1,0:T(8,128)S(1)}, f32[2,64,128]{2,1,0:T(8,128)S(1)}, u32[]{:S(2)}, u32[]{:S(2)}) collective-permute-start(f32[2,64,128]{2,1,0:T(8,128)S(1)} %get-tuple-element.58), channel_id=1, source_target_pairs={{0,4},{4,8},{8,12},{12,16},{16,20},{20,24},{24,28},{28,32},{32,36}... | collective-permute-start | bytes 196616 | tf_op jit(solution)/shard_map/ppermute | solution.py:370
  131.0 5.8 %collective-permute-done.9.xp_ref.refs_2_ = f32[2,64,128]{2,1,0:T(8,128)S(1)} collective-permute-done((f32[2,64,128]{2,1,0:T(8,128)S(1)}, f32[2,64,128]{2,1,0:T(8,128)S(1)}, u32[]{:S(2)}, u32[]{:S(2)}) %collective-permute-start.9) | collective-permute-done | bytes 65568 | tf_op jit(solution)/shard_map/ppermute | solution.py:370
  136.7 3.3 %collective-permute-start.10 = (f32[2,64,128]{2,1,0:T(8,128)S(1)}, f32[2,64,128]{2,1,0:T(8,128)S(1)}, u32[]{:S(2)}, u32[]{:S(2)}) collective-permute-start(f32[2,64,128]{2,1,0:T(8,128)S(1)} %get-tuple-element.61), channel_id=1, source_target_pairs={{1,0},{2,1},{3,2},{5,4},{6,5},{7,6},{9,8},{10,9},{11,10},{13,12},{... | collective-permute-start | bytes 196616 | tf_op jit(solution)/shard_map/ppermute | solution.py:370
  140.1 2.5 %collective-permute-start.11 = (f32[2,64,128]{2,1,0:T(8,128)S(1)}, f32[2,64,128]{2,1,0:T(8,128)S(1)}, u32[]{:S(2)}, u32[]{:S(2)}) collective-permute-start(f32[2,64,128]{2,1,0:T(8,128)S(1)} %get-tuple-element.62), channel_id=1, source_target_pairs={{0,1},{1,2},{2,3},{4,5},{5,6},{6,7},{8,9},{9,10},{10,11},{12,13},{... | collective-permute-start | bytes 196616 | tf_op jit(solution)/shard_map/ppermute | solution.py:370
  142.6 0.3 collective-permute-done.10.refs_3_
  142.9 3.3 %collective-permute-done.11.refs_4_ = f32[2,64,128]{2,1,0:T(8,128)S(1)} collective-permute-done((f32[2,64,128]{2,1,0:T(8,128)S(1)}, f32[2,64,128]{2,1,0:T(8,128)S(1)}, u32[]{:S(2)}, u32[]{:S(2)}) %collective-permute-start.11) | collective-permute-done | bytes 65568 | tf_op jit(solution)/shard_map/ppermute | solution.py:370
  146.3 1.0 shard_map.105
  (42 shorter events, 0.1 us)
Async XLA Ops:
  0.0 0.7 copy-start.16
  0.7 0.8 copy-start.24
  1.5 0.7 copy-start.28
  4.3 0.6 copy-start.20
  4.9 18.0 %all-to-all-start = ((f32[128,1,128]{2,1,0:T(1,128)}), f32[128,1,128]{2,1,0:T(1,128)S(1)}, u32[]{:S(2)}, u32[]{:S(2)}) async-start(f32[128,1,128]{2,1,0:T(1,128)} %bitcast.4), calls=%async_computation | async-start | bytes 131072 | tf_op jit(solution)/shard_map/all_to_all | solution.py:374
  22.9 1.0 copy-start
  27.4 14.3 %all-to-all-start.1 = ((f32[128,1,128]{2,1,0:T(1,128)}), f32[128,1,128]{2,1,0:T(1,128)S(1)}, u32[]{:S(2)}, u32[]{:S(2)}) async-start(f32[128,1,128]{2,1,0:T(1,128)} %bitcast.7), calls=%async_computation.1 | async-start | bytes 131072 | tf_op jit(solution)/shard_map/all_to_all | solution.py:374
  33.6 0.7 copy-start.18
  35.6 1.0 copy-start.1
  36.6 1.4 copy-start.3
  38.0 0.9 copy-start.10
  38.9 0.9 copy-start.13
  39.8 0.7 copy-start.25
  40.5 1.2 copy-start.17
  40.5 1.3 copy-start.19
  40.5 23.6 %copy-start.2 = (f32[2,512,1,1,128]{4,3,2,1,0:T(1,128)S(1)}, f32[2,512,1,1,128]{4,3,2,1,0:T(1,128)}, u32[]{:S(2)}) copy-start(f32[2,512,1,1,128]{4,3,2,1,0:T(1,128)} %param.9) | copy-start | bytes 1572868
  41.8 0.7 copy-start.21
  42.5 33.5 %copy-start.4 = (f32[3,2,512,1,1,128]{5,4,3,2,1,0:T(1,128)S(1)}, f32[3,2,512,1,1,128]{5,4,3,2,1,0:T(1,128)}, u32[]{:S(2)}) copy-start(f32[3,2,512,1,1,128]{5,4,3,2,1,0:T(1,128)} %param.10) | copy-start | bytes 4718596
  43.5 6.2 %collective-permute-start = (f32[2,64,128]{2,1,0:T(8,128)S(1)}, f32[2,64,128]{2,1,0:T(8,128)S(1)}, u32[]{:S(2)}, u32[]{:S(2)}) collective-permute-start(f32[2,64,128]{2,1,0:T(8,128)S(1)} %get-tuple-element.38), channel_id=1, source_target_pairs={{4,0},{8,4},{12,8},{16,12},{20,16},{24,20},{28,24},{32,28},{36,32}... | collective-permute-start | bytes 196616 | tf_op jit(solution)/shard_map/ppermute | solution.py:370
  47.8 7.7 %collective-permute-start.1 = (f32[2,64,128]{2,1,0:T(8,128)S(1)}, f32[2,64,128]{2,1,0:T(8,128)S(1)}, u32[]{:S(2)}, u32[]{:S(2)}) collective-permute-start(f32[2,64,128]{2,1,0:T(8,128)S(1)} %get-tuple-element.39), channel_id=1, source_target_pairs={{0,4},{4,8},{8,12},{12,16},{16,20},{20,24},{24,28},{28,32},{32,36}... | collective-permute-start | bytes 196616 | tf_op jit(solution)/shard_map/ppermute | solution.py:370
  55.5 6.2 %collective-permute-start.2 = (f32[2,64,128]{2,1,0:T(8,128)S(1)}, f32[2,64,128]{2,1,0:T(8,128)S(1)}, u32[]{:S(2)}, u32[]{:S(2)}) collective-permute-start(f32[2,64,128]{2,1,0:T(8,128)S(1)} %get-tuple-element.42), channel_id=1, source_target_pairs={{1,0},{2,1},{3,2},{5,4},{6,5},{7,6},{9,8},{10,9},{11,10},{13,12},{... | collective-permute-start | bytes 196616 | tf_op jit(solution)/shard_map/ppermute | solution.py:370
  58.0 6.2 %collective-permute-start.3 = (f32[2,64,128]{2,1,0:T(8,128)S(1)}, f32[2,64,128]{2,1,0:T(8,128)S(1)}, u32[]{:S(2)}, u32[]{:S(2)}) collective-permute-start(f32[2,64,128]{2,1,0:T(8,128)S(1)} %get-tuple-element.43), channel_id=1, source_target_pairs={{0,1},{1,2},{2,3},{4,5},{5,6},{6,7},{8,9},{9,10},{10,11},{12,13},{... | collective-permute-start | bytes 196616 | tf_op jit(solution)/shard_map/ppermute | solution.py:370
  67.7 0.8 copy-start.7
  68.5 15.4 %all-to-all-start.2 = ((f32[128,1,128]{2,1,0:T(1,128)}), f32[128,1,128]{2,1,0:T(1,128)S(1)}, u32[]{:S(2)}, u32[]{:S(2)}) async-start(f32[128,1,128]{2,1,0:T(1,128)} %bitcast.17), calls=%async_computation.2 | async-start | bytes 131072 | tf_op jit(solution)/shard_map/all_to_all | solution.py:374
  76.0 1.0 copy-start.8
  77.1 0.9 copy-start.11
  78.0 0.9 copy-start.14
  78.8 0.7 copy-start.26
  83.9 0.7 copy-start.22
  85.6 30.2 %copy-start.27 = (f32[2,1,1,128]{3,2,1,0:T(1,128)S(1)}, f32[2,1,1,128]{3,2,1,0:T(1,128)}, u32[]{:S(2)}) copy-start(f32[2,1,1,128]{3,2,1,0:T(1,128)} %param.11) | copy-start | bytes 3076
  85.6 5.2 %collective-permute-start.4 = (f32[2,64,128]{2,1,0:T(8,128)S(1)}, f32[2,64,128]{2,1,0:T(8,128)S(1)}, u32[]{:S(2)}, u32[]{:S(2)}) collective-permute-start(f32[2,64,128]{2,1,0:T(8,128)S(1)} %get-tuple-element.48), channel_id=1, source_target_pairs={{4,0},{8,4},{12,8},{16,12},{20,16},{24,20},{28,24},{32,28},{36,32}... | collective-permute-start | bytes 196616 | tf_op jit(solution)/shard_map/ppermute | solution.py:370
  88.9 7.7 %collective-permute-start.5 = (f32[2,64,128]{2,1,0:T(8,128)S(1)}, f32[2,64,128]{2,1,0:T(8,128)S(1)}, u32[]{:S(2)}, u32[]{:S(2)}) collective-permute-start(f32[2,64,128]{2,1,0:T(8,128)S(1)} %get-tuple-element.49), channel_id=1, source_target_pairs={{0,4},{4,8},{8,12},{12,16},{16,20},{20,24},{24,28},{28,32},{32,36}... | collective-permute-start | bytes 196616 | tf_op jit(solution)/shard_map/ppermute | solution.py:370
  96.6 6.2 %collective-permute-start.6 = (f32[2,64,128]{2,1,0:T(8,128)S(1)}, f32[2,64,128]{2,1,0:T(8,128)S(1)}, u32[]{:S(2)}, u32[]{:S(2)}) collective-permute-start(f32[2,64,128]{2,1,0:T(8,128)S(1)} %get-tuple-element.52), channel_id=1, source_target_pairs={{1,0},{2,1},{3,2},{5,4},{6,5},{7,6},{9,8},{10,9},{11,10},{13,12},{... | collective-permute-start | bytes 196616 | tf_op jit(solution)/shard_map/ppermute | solution.py:370
  99.9 6.2 %collective-permute-start.7 = (f32[2,64,128]{2,1,0:T(8,128)S(1)}, f32[2,64,128]{2,1,0:T(8,128)S(1)}, u32[]{:S(2)}, u32[]{:S(2)}) collective-permute-start(f32[2,64,128]{2,1,0:T(8,128)S(1)} %get-tuple-element.53), channel_id=1, source_target_pairs={{0,1},{1,2},{2,3},{4,5},{5,6},{6,7},{8,9},{9,10},{10,11},{12,13},{... | collective-permute-start | bytes 196616 | tf_op jit(solution)/shard_map/ppermute | solution.py:370
  106.1 1.0 copy-start.9
  110.7 13.0 %all-to-all-start.3 = ((f32[128,1,128]{2,1,0:T(1,128)}), f32[128,1,128]{2,1,0:T(1,128)S(1)}, u32[]{:S(2)}, u32[]{:S(2)}) async-start(f32[128,1,128]{2,1,0:T(1,128)} %bitcast.20), calls=%async_computation.3 | async-start | bytes 131072 | tf_op jit(solution)/shard_map/all_to_all | solution.py:374
  115.9 0.9 copy-start.12
  116.8 0.9 copy-start.15
  117.7 6.1 %copy-start.23 = (s32[1,2048]{1,0:T(1,128)S(1)}, s32[1,2048]{1,0:T(1,128)}, u32[]{:S(2)}) copy-start(s32[1,2048]{1,0:T(1,128)} %copy-done.20) | copy-start | bytes 24580
  118.9 0.8 copy-start.5
  123.7 1.0 copy-start.6
  125.8 5.2 %collective-permute-start.8 = (f32[2,64,128]{2,1,0:T(8,128)S(1)}, f32[2,64,128]{2,1,0:T(8,128)S(1)}, u32[]{:S(2)}, u32[]{:S(2)}) collective-permute-start(f32[2,64,128]{2,1,0:T(8,128)S(1)} %get-tuple-element.57), channel_id=1, source_target_pairs={{4,0},{8,4},{12,8},{16,12},{20,16},{24,20},{28,24},{32,28},{36,32}... | collective-permute-start | bytes 196616 | tf_op jit(solution)/shard_map/ppermute | solution.py:370
  129.0 7.7 %collective-permute-start.9 = (f32[2,64,128]{2,1,0:T(8,128)S(1)}, f32[2,64,128]{2,1,0:T(8,128)S(1)}, u32[]{:S(2)}, u32[]{:S(2)}) collective-permute-start(f32[2,64,128]{2,1,0:T(8,128)S(1)} %get-tuple-element.58), channel_id=1, source_target_pairs={{0,4},{4,8},{8,12},{12,16},{16,20},{20,24},{24,28},{28,32},{32,36}... | collective-permute-start | bytes 196616 | tf_op jit(solution)/shard_map/ppermute | solution.py:370
  136.7 6.2 %collective-permute-start.10 = (f32[2,64,128]{2,1,0:T(8,128)S(1)}, f32[2,64,128]{2,1,0:T(8,128)S(1)}, u32[]{:S(2)}, u32[]{:S(2)}) collective-permute-start(f32[2,64,128]{2,1,0:T(8,128)S(1)} %get-tuple-element.61), channel_id=1, source_target_pairs={{1,0},{2,1},{3,2},{5,4},{6,5},{7,6},{9,8},{10,9},{11,10},{13,12},{... | collective-permute-start | bytes 196616 | tf_op jit(solution)/shard_map/ppermute | solution.py:370
  140.1 6.2 %collective-permute-start.11 = (f32[2,64,128]{2,1,0:T(8,128)S(1)}, f32[2,64,128]{2,1,0:T(8,128)S(1)}, u32[]{:S(2)}, u32[]{:S(2)}) collective-permute-start(f32[2,64,128]{2,1,0:T(8,128)S(1)} %get-tuple-element.62), channel_id=1, source_target_pairs={{0,1},{1,2},{2,3},{4,5},{5,6},{6,7},{8,9},{9,10},{10,11},{12,13},{... | collective-permute-start | bytes 196616 | tf_op jit(solution)/shard_map/ppermute | solution.py:370

commit v2 on v1

--- a/solution.py
+++ b/solution.py
@@ -96,7 +96,18 @@
     return out
 
 
-def query_kernel(owner_ref, donor_ref, coords_ref, payload_ref, rank_ref):
+def start_copies(pairs, sems):
+    copies = [pltpu.make_async_copy(src, dst, sems.at[n]) for n, (src, dst) in enumerate(pairs)]
+    for copy in copies:
+        copy.start()
+    return copies
+
+
+def query_kernel(owner_any, donor_any, coords_any, payload_ref, rank_any, owner_ref, donor_ref, coords_ref, rank_ref, sems):
+    copies = start_copies(
+        [(owner_any, owner_ref), (donor_any, donor_ref), (coords_any, coords_ref)], sems
+    )
+    copies[0].wait()
     rows = owner_ref.shape[1]
     half = rows // 2
     owner = owner_ref[...]
@@ -106,17 +117,26 @@
     )
     before = jnp.where(before, 1.0, 0.0).astype(bf16)
     total = jnp.zeros((128, 1), f32)
-    acc = [jnp.zeros((128, 128), f32) for _ in range(3)]
+    hots = []
+    ranks = []
     for c in range(rows // step):
         sl = slice(c * step, (c + 1) * step)
         oh = one_hot_rows(owner[:, sl], 128)
         ohf = oh.astype(f32)
         cum = dot_nn(oh, before) + total
-        rank = jnp.sum(cum * ohf, axis=0, keepdims=True)
         total = total + jnp.sum(ohf, axis=1, keepdims=True)
-        rank_i = rank.astype(i32)
-        rank_ref[:, sl] = rank_i
-        pick = lax.broadcasted_iota(i32, (32, step), 0) == rank_i
+        rank = jnp.sum(cum * ohf, axis=0, keepdims=True).astype(i32)
+        rank_ref[:, sl] = rank
+        hots.append(oh)
+        ranks.append(rank)
+    out = pltpu.make_async_copy(rank_ref, rank_any, sems.at[3])
+    out.start()
+    copies[1].wait()
+    copies[2].wait()
+    acc = [jnp.zeros((128, 128), f32) for _ in range(3)]
+    for c in range(rows // step):
+        sl = slice(c * step, (c + 1) * step)
+        pick = lax.broadcasted_iota(i32, (32, step), 0) == ranks[c]
         col = lax.broadcasted_iota(i32, (1, step), 1) + c * step
         ident = (jnp.where(col < half, 128, 0) + donor_ref[:, sl]).astype(f32)
         parts = [[], [], []]
@@ -132,11 +152,21 @@
         parts[1].append(zero)
         parts[2].append(zero)
         for p in range(3):
-            acc[p] = acc[p] + dot_nt(oh, jnp.concatenate(parts[p], axis=0))
+            acc[p] = acc[p] + dot_nt(hots[c], jnp.concatenate(parts[p], axis=0))
     payload_ref[...] = acc[0] + (acc[1] + acc[2])
-
-
-def prepare_kernel(flags_ref, point_ref, load_ref, inv_ref):
+    out.wait()
+
+
+def prepare_kernel(flags_ref, owner_any, rank_any, point_any, load_any, inv_any, table_any, mask_any,
+                   load_ref, inv_ref, table_ref, mask_ref, sems):
+    copies = start_copies(
+        [(owner_any, table_ref.at[0]), (rank_any, table_ref.at[1]), (point_any, table_ref.at[2])], sems
+    )
+    for n in range(4):
+        mask_ref[n] = jnp.full((8, 128), 2.0 - 2.0 * flags_ref[n], f32)
+    for copy in copies:
+        copy.wait()
+    point_ref = table_ref.at[2]
     half = point_ref.shape[1] // 2
     wk = weight_rows()
     for m in range(2):
@@ -163,10 +193,23 @@
         if j == 7:
             val = val * flags_ref[3]
         inv_ref[ij * 8 : ij * 8 + 8, :] = val
-
-
-def local_kernel(u_ref, vel_ref, nu_ref, load_ref, dz_ref, dzt_ref, out_ref, ax_ref, ay_ref, fz_ref):
+    copies = start_copies(
+        [(load_ref, load_any), (inv_ref, inv_any), (table_ref, table_any), (mask_ref, mask_any)], sems
+    )
+    for copy in copies:
+        copy.wait()
+
+
+def local_kernel(u_any, vel_any, nu_any, load_any, deep_any, table_any, mask_any, out_ref, table_ref, mask_ref, u_ref, vel_ref, nu_ref, load_ref, deep_ref,
+                 ax_ref, ay_ref, fz_ref, sems):
+    copies = start_copies(
+        [(u_any, u_ref), (deep_any, deep_ref), (nu_any, nu_ref), (vel_any, vel_ref), (load_any, load_ref),
+         (table_any, table_ref), (mask_any, mask_ref)],
+        sems,
+    )
     wk = weight_rows()
+    copies[0].wait()
+    copies[1].wait()
 
     def depth(table, pick):
         chunks = []
@@ -176,12 +219,15 @@
             chunks.append(dot_nn(table, jnp.concatenate([hi, hi, lo], axis=0)))
         return chunks
 
-    az = depth(dz_ref[...], lambda m, rows: u_ref[m, rows, :])
+    az = depth(deep_ref[0], lambda m, rows: u_ref[m, rows, :])
     for m in range(2):
         for j in range(8):
             outs = apply_table(DERIV, [u_ref[m, i * 64 + j * 8 : i * 64 + j * 8 + 8, :] for i in range(8)])
             for i in range(8):
                 ax_ref[m, i * 64 + j * 8 : i * 64 + j * 8 + 8, :] = outs[i]
+    for copy in copies[2:]:
+        copy.wait()
+    for m in range(2):
         wnu = 4.0 * volume_factor * wk * nu_ref[m : m + 1, :]
         wad = 2.0 * volume_factor * wk
         for i in range(8):
@@ -204,7 +250,7 @@
             for j in range(8):
                 rows = slice(i * 64 + j * 8, i * 64 + j * 8 + 8)
                 out_ref[m, rows, :] = out_ref[m, rows, :] - outs[j]
-    bz = depth(dzt_ref[...], lambda m, rows: fz_ref[m, rows, :])
+    bz = depth(deep_ref[1], lambda m, rows: fz_ref[m, rows, :])
     for m in range(2):
         for j in range(8):
             outs = apply_table(DERIV_T, [ax_ref[m, i * 64 + j * 8 : i * 64 + j * 8 + 8, :] for i in range(8)])
@@ -260,11 +306,14 @@
     ans_ref[...] = answers.T
 
 
-def first_kernel(u_ref, received_ref, ans_ref, wx_ref, wy_ref, wz_ref):
+def first_kernel(u_any, received_ref, ans_ref, u_ref, wx_ref, wy_ref, wz_ref, sems):
+    copies = start_copies([(u_any, u_ref)], sems)
+    copies[0].wait()
     interpolate([u_ref[0], u_ref[1]], received_ref, ans_ref, wx_ref, wy_ref, wz_ref)
 
 
-def penalty_kernel(replies_ref, owner_ref, rank_ref, point_ref, local_ref, out_ref, xl_ref, xr_ref, yl_ref, yr_ref):
+def penalty_kernel(replies_ref, table_ref, mask_ref, local_ref, out_ref, xl_ref, xr_ref, yl_ref, yr_ref):
+    owner_ref, rank_ref, point_ref = table_ref.at[0], table_ref.at[1], table_ref.at[2]
     half = point_ref.shape[1] // 2
     hi, lo = split_two(replies_ref[...].T[0:32, :])
     lhs = jnp.concatenate([hi, lo], axis=1)
@@ -293,24 +342,29 @@
             val = local_ref[m, rows, :] + (c * wk) * summed[rows, :]
             out_ref[m, rows, :] = val
             if i == 0:
-                xl_ref[m, j * 8 : j * 8 + 8, :] = val
+                xl_ref[m, j * 8 : j * 8 + 8, :] = val * mask_ref[0]
             if i == 7:
-                xr_ref[m, j * 8 : j * 8 + 8, :] = val
+                xr_ref[m, j * 8 : j * 8 + 8, :] = val * mask_ref[1]
             if j == 0:
                 yl_ref[m, i * 8 : i * 8 + 8, :] = val
             if j == 7:
                 yr_ref[m, i * 8 : i * 8 + 8, :] = val
 
 
-def edge_kernel(yl_ref, yr_ref, xn_ref, xp_ref, yl_out, yr_out):
+def edge_kernel(yl_ref, yr_ref, xn_ref, xp_ref, mask_ref, yl_out, yr_out):
     for m in range(2):
         for src, dst, j in ((yl_ref, yl_out, 0), (yr_ref, yr_out, 7)):
-            dst[m, 8:56, :] = src[m, 8:56, :]
-            dst[m, 0:8, :] = src[m, 0:8, :] + xp_ref[m, j * 8 : j * 8 + 8, :]
-            dst[m, 56:64, :] = src[m, 56:64, :] + xn_ref[m, j * 8 : j * 8 + 8, :]
-
-
-def finish(blend, v_ref, xn_ref, xp_ref, yn_ref, yp_ref, inv_ref, start_ref, u_ref, new_ref, work_ref):
+            mask = mask_ref[2 if j == 0 else 3]
+            for i in range(8):
+                val = src[m, i * 8 : i * 8 + 8, :]
+                if i == 0:
+                    val = val + xp_ref[m, j * 8 : j * 8 + 8, :]
+                if i == 7:
+                    val = val + xn_ref[m, j * 8 : j * 8 + 8, :]
+                dst[m, i * 8 : i * 8 + 8, :] = val * mask
+
+
+def finish(blend, v_ref, xn_ref, xp_ref, yn_ref, yp_ref, start_ref, u_ref, inv_ref, new_ref, work_ref, copies):
     lane = lax.broadcasted_iota(i32, (64, 128), 1)
     for m in range(2):
         for ij in range(64):
@@ -321,11 +375,7 @@
                 val = val + yp_ref[m, i * 8 : i * 8 + 8, :]
             elif j == 7:
                 val = val + yn_ref[m, i * 8 : i * 8 + 8, :]
-            if i == 0 and j not in (0, 7):
-                val = val + xp_ref[m, j * 8 : j * 8 + 8, :]
-            elif i == 7 and j not in (0, 7):
-                val = val + xn_ref[m, j * 8 : j * 8 + 8, :]
-            elif i == 0:
+            if i == 0:
                 val = val + xp_ref[m, j * 8 : j * 8 + 8, :]
             elif i == 7:
                 val = val + xn_ref[m, j * 8 : j * 8 + 8, :]
@@ -334,40 +384,53 @@
         right = work_ref[m, pl.ds(7, 64, stride=8), :]
         work_ref[m, pl.ds(0, 64, stride=8), :] = left + jnp.where(lane > 0, pltpu.roll(right, 1, 1), 0.0)
         work_ref[m, pl.ds(7, 64, stride=8), :] = right + jnp.where(lane < 127, pltpu.roll(left, 127, 1), 0.0)
+    for copy in copies:
+        copy.wait()
+    for m in range(2):
         new = u_ref[m] + inv_ref[...] * work_ref[m]
         if blend is not None:
             new = blend[0] * start_ref[m] + blend[1] * new
         new_ref[m] = new
 
 
-def step_kernel(blend, v_ref, xn_ref, xp_ref, yn_ref, yp_ref, inv_ref, start_ref, u_ref, received_ref,
-                new_ref, ans_ref, work_ref, wx_ref, wy_ref, wz_ref):
-    finish(blend, v_ref, xn_ref, xp_ref, yn_ref, yp_ref, inv_ref, start_ref, u_ref, new_ref, work_ref)
+def step_kernel(blend, v_ref, xn_ref, xp_ref, yn_ref, yp_ref, start_any, u_any, inv_any, received_any,
+                new_any, ans_ref, work_ref, start_ref, u_ref, inv_ref, received_ref, new_ref,
+                wx_ref, wy_ref, wz_ref, sems):
+    pairs = [(u_any, u_ref), (inv_any, inv_ref), (received_any, received_ref)]
+    if blend is not None:
+        pairs.append((start_any, start_ref))
+    copies = start_copies(pairs, sems)
+    finish(blend, v_ref, xn_ref, xp_ref, yn_ref, yp_ref, start_ref, u_ref, inv_ref, new_ref, work_ref, copies)
+    out = pltpu.make_async_copy(new_ref, new_any, sems.at[4])
+    out.start()
     interpolate([new_ref[0], new_ref[1]], received_ref, ans_ref, wx_ref, wy_ref, wz_ref)
-
-
-def last_kernel(blend, v_ref, xn_ref, xp_ref, yn_ref, yp_ref, inv_ref, start_ref, u_ref, new_ref, work_ref):
-    finish(blend, v_ref, xn_ref, xp_ref, yn_ref, yp_ref, inv_ref, start_ref, u_ref, new_ref, work_ref)
-
-
-def call(kernel, outs, ins, scratch=(), smem_first=False):
-    specs = [pl.BlockSpec(memory_space=pltpu.VMEM)] * len(ins)
-    if smem_first:
-        specs[0] = pl.BlockSpec(memory_space=pltpu.SMEM)
+    out.wait()
+
+
+def last_kernel(blend, v_ref, xn_ref, xp_ref, yn_ref, yp_ref, start_any, u_any, inv_any, new_ref,
+                work_ref, start_ref, u_ref, inv_ref, sems):
+    copies = start_copies([(u_any, u_ref), (inv_any, inv_ref), (start_any, start_ref)], sems)
+    finish(blend, v_ref, xn_ref, xp_ref, yn_ref, yp_ref, start_ref, u_ref, inv_ref, new_ref, work_ref, copies)
+
+
+PINNED = "a"
+SPACES = {"v": pltpu.VMEM, "a": pltpu.HBM, "s": pltpu.SMEM}
+
+
+def call(kernel, outs, ins, scratch=(), spaces="", out_spaces=""):
     return pl.pallas_call(
         kernel,
-        out_shape=[jax.ShapeDtypeStruct(s, d) for s, d in outs],
-        in_specs=specs,
-        out_specs=[pl.BlockSpec(memory_space=pltpu.VMEM)] * len(outs),
+        out_shape=[SPACES[c](s, d) if c in PINNED else jax.ShapeDtypeStruct(s, d) for (s, d), c in zip(outs, out_spaces)],
+        in_specs=[pl.BlockSpec(memory_space=SPACES[c]) for c in spaces],
+        out_specs=[pl.BlockSpec(memory_space=SPACES[c]) for c in out_spaces],
         scratch_shapes=list(scratch),
         compiler_params=pltpu.CompilerParams(vmem_limit_bytes=24 << 20),
-    )(*ins)
-
-
-def passed_along(value, axis, steps):
+    )(*[pltpu.with_memory_space_constraint(x, SPACES[c]) if c in PINNED else x for x, c in zip(ins, spaces)])
+
+
+def passed_around(value, axis, steps):
     count = lax.axis_size(axis)
-    leading, last = (max(0, -steps), min(count, count - steps))
-    return lax.ppermute(value, axis, [(source, source + steps) for source in range(leading, last)])
+    return lax.ppermute(value, axis, [(n, (n + steps) % count) for n in range(count)])
 
 
 def exchange(x):
@@ -384,63 +447,99 @@
     owner = recv_owner.reshape(1, rows)
     donor = donor_elem.reshape(1, rows)
     point = recv_point.reshape(1, rows)
-    deep = jnp.asarray(block_matrix(DERIV))
-    deep_t = jnp.asarray(block_matrix(DERIV_T))
+    deep = jnp.asarray(np.stack([block_matrix(DERIV), block_matrix(DERIV_T)]))
+
+    def vmem(shape, dtype=f32):
+        return pltpu.VMEM(shape, dtype)
+
+    def dma(count):
+        return pltpu.SemaphoreType.DMA((count,))
+
+    line = vmem((1, rows), i32)
+    weights_scratch = [vmem((8, 32, 128)), vmem((8, 32, 128)), vmem((32, 8, 128))]
 
     payload, rank = call(
-        query_kernel, [((128, 128), f32), ((1, rows), i32)], (owner, donor, recv_coords)
+        query_kernel,
+        [((128, 128), f32), ((1, rows), i32)],
+        (owner, donor, recv_coords),
+        [line, line, vmem((3, rows)), line, dma(4)],
+        "aaa",
+        "va",
     )
     received = exchange(payload)
 
     ix, iy = lax.axis_index("gx"), lax.axis_index("gy")
     inside = [ix > 0, ix < lax.axis_size("gx") - 1, iy > 0, iy < lax.axis_size("gy") - 1]
     flags = jnp.where(jnp.stack(inside), 0.5, 1.0).astype(f32)
-    load, inv = call(
-        prepare_kernel, [(field, f32), ((512, 128), f32)], (flags, point), smem_first=True
-    )
-    weights_scratch = [pltpu.VMEM((8, 32, 128), f32), pltpu.VMEM((8, 32, 128), f32), pltpu.VMEM((32, 8, 128), f32)]
+    load, inv, table, mask = call(
+        prepare_kernel,
+        [(field, f32), ((512, 128), f32), ((3, 1, rows), i32), ((4, 8, 128), f32)],
+        (flags, owner, rank, point),
+        [vmem(field), vmem((512, 128)), vmem((3, 1, rows), i32), vmem((4, 8, 128)), dma(4)],
+        "saaa",
+        "aaaa",
+    )
 
     def local(u):
         return call(
             local_kernel,
-            [(field, f32)],
-            (u, flow, nu, load, deep, deep_t),
-            [pltpu.VMEM(field, f32)] * 3,
-        )[0]
-
-    def gather_faces(replies, loc):
+            [(field, f32), ((3, 1, rows), i32), ((4, 8, 128), f32)],
+            (u, flow, nu, load, deep, table, mask),
+            [vmem(field), vmem((3,) + field), vmem((2, 128)), vmem(field), vmem((2, 128, 384), bf16)]
+            + [vmem(field)] * 3
+            + [dma(7)],
+            "aaaaaaa",
+            "vvv",
+        )
+
+    def gather_faces(replies, loc, table, mask):
         v, xl, xr, yl, yr = call(
             penalty_kernel,
             [(field, f32)] + [(face, f32)] * 4,
-            (replies, owner, rank, point, loc),
+            (replies, table, mask, loc),
+            (),
+            "vvvv",
+            "vvvvv",
         )
-        xn = passed_along(xl, "gx", -1)
-        xp = passed_along(xr, "gx", 1)
-        yl, yr = call(edge_kernel, [(face, f32)] * 2, (yl, yr, xn, xp))
-        yn = passed_along(yl, "gy", -1)
-        yp = passed_along(yr, "gy", 1)
+        xn = passed_around(xl, "gx", -1)
+        xp = passed_around(xr, "gx", 1)
+        yl, yr = call(edge_kernel, [(face, f32)] * 2, (yl, yr, xn, xp, mask), (), "vvvvv", "vv")
+        yn = passed_around(yl, "gy", -1)
+        yp = passed_around(yr, "gy", 1)
         return v, xn, xp, yn, yp
 
     u = start
     loc = local(u)
-    answers = call(first_kernel, [((128, 128), f32)], (u, received), weights_scratch)[0]
+    received, loc = lax.optimization_barrier((received, loc))
+    answers = call(
+        first_kernel,
+        [((128, 128), f32)],
+        (u, received),
+        [vmem(field)] + weights_scratch + [dma(1)],
+        "av",
+        "v",
+    )[0]
     for blend in (None, (0.75, 0.25)):
         replies = exchange(answers)
-        parts = gather_faces(replies, loc)
+        parts = gather_faces(replies, *loc)
         u, answers = call(
             lambda *refs, blend=blend: step_kernel(blend, *refs),
             [(field, f32), ((128, 128), f32)],
-            parts + (inv, start, u, received),
-            [pltpu.VMEM(field, f32)] + weights_scratch,
+            parts + (start, u, inv, received),
+            [vmem(field)] * 3 + [vmem((512, 128)), vmem((128, 128)), vmem(field)] + weights_scratch + [dma(5)],
+            "vvvvvaaaa",
+            "av",
         )
         loc = local(u)
     replies = exchange(answers)
-    parts = gather_faces(replies, loc)
+    parts = gather_faces(replies, *loc)
     third = call(
         lambda *refs: last_kernel((1.0 / 3.0, 2.0 / 3.0), *refs),
         [(field, f32)],
-        parts + (inv, start, u),
-        [pltpu.VMEM(field, f32)],
+        parts + (start, u, inv),
+        [vmem(field)] * 3 + [vmem((512, 128)), dma(3)],
+        "vvvvvaaa",
+        "v",
     )[0]
     return third.reshape(scalar.shape)
 

time: 149 us -> 130 us (0.87)
  the two profiles are of different devices: /device:TPU:34 before, /device:TPU:0 now
where the time goes in v2:
time: 130 us; the launch traced here: 129 us
  waiting for transfers between devices  52 us (40%)
  Pallas kernels  32.8 us (25%)
  starting transfers between devices  28.6 us (22%)
  blocking collectives  15.4 us (12%)
    ppermute x12, waiting for transfers between devices, passed_around(): lax.ppermute(value, axis, [(n, (n + steps) % count) for n in range(count)])  35.4 us
    pallas_call x15, Pallas kernels, call(): pl.pallas_call(kernel, out_shape=[SPACES[c](s, d) if c in PINNED else jax...  32.8 us
    all_to_all x3, starting transfers between devices, exchange(): lax.all_to_all(x, ('gx', 'gy'), split_axis=0, concat_axis=0, tiled=True)  20.6 us
    all_to_all x3, waiting for transfers between devices, exchange(): lax.all_to_all(x, ('gx', 'gy'), split_axis=0, concat_axis=0, tiled=True)  16.6 us
    all_to_all x1, blocking collectives, exchange(): lax.all_to_all(x, ('gx', 'gy'), split_axis=0, concat_axis=0, tiled=True)  15.4 us
    ppermute x12, starting transfers between devices, passed_around(): lax.ppermute(value, axis, [(n, (n + steps) % count) for n in range(count)])  8.02 us
  transfers between devices with their start and end apart: 15, of which 15 were waited for; matrix products, arithmetic and copies ran while one was open for 0% of the time, Pallas kernels for 9%

profile of v2, /device:TPU:0, one launch (start us, length us, event | category | flops | bytes accessed | tf_op | source)
XLA Modules:
  0.0 129.2 jit_solution(6450270916693470174)
XLA Ops:
  0.0 2.6 %shard_map.82 = (f32[128,128]{1,0:T(8,128)}, s32[1,2048]{1,0:T(1,128)}) custom-call(s32[1,2048]{1,0:T(1,128)} %bitcast.45, s32[1,2048]{1,0:T(1,128)} %bitcast.51, f32[3,2048]{1,0:T(4,128)} %coords_any.1), custom_call_target="tpu_custom_call" | custom-call | tf_op jit(solution)/shard_map/pallas_call | solution.py:421
  2.6 11.2 %all-to-all-start = ((f32[128,1,128]{2,1,0:T(1,128)}), f32[128,1,128]{2,1,0:T(1,128)S(1)}, u32[]{:S(2)}, u32[]{:S(2)}) async-start(f32[128,1,128]{2,1,0:T(1,128)} %bitcast.4), calls=%async_computation | async-start | bytes 131072 | tf_op jit(solution)/shard_map/all_to_all | solution.py:437
  13.8 0.1 add_select_fusion.flags_ref
  13.8 2.9 %shard_map.83 = (f32[2,512,128]{2,1,0:T(8,128)}, f32[512,128]{1,0:T(8,128)}, s32[3,1,2048]{2,1,0:T(1,128)}, f32[4,8,128]{2,1,0:T(8,128)}) custom-call(f32[4]{0:T(128)S(1)} %add_select_fusion.flags_ref, s32[1,2048]{1,0:T(1,128)} %bitcast.46, s32[1,2048]{1,0:T(1,128)} %get-tuple-element.50.rank_any, s32[1,2048]{1,0:T(1,128)} %bitcast.50), custom_call_target="tpu_custom_call" | custom-call | tf_op jit(solution)/shard_map/pallas_call | solution.py:421
  16.7 2.8 %shard_map.84 = (f32[2,512,128]{2,1,0:T(8,128)S(1)}, s32[3,1,2048]{2,1,0:T(1,128)S(1)}, f32[4,8,128]{2,1,0:T(8,128)S(1)}) custom-call(f32[2,512,128]{2,1,0:T(8,128)} %bitcast.36, f32[3,2,512,128]{3,2,1,0:T(8,128)} %bitcast.42, f32[2,128]{1,0:T(2,128)} %bitcast.47, f32[2,512,128]{2,1,0:T(8,128)} %get-tuple-element.51.load_any, ...), custom_call_target="tpu_custom_call" | custom-call | tf_op jit(solution)/shard_map/pallas_call | solution.py:421
  19.5 3.5 %all-to-all-done = f32[128,1,128]{2,1,0:T(1,128)S(1)} async-done(((f32[128,1,128]{2,1,0:T(1,128)}), f32[128,1,128]{2,1,0:T(1,128)S(1)}, u32[]{:S(2)}, u32[]{:S(2)}) %all-to-all-start) | async-done | bytes 65568 | tf_op jit(solution)/shard_map/all_to_all | solution.py:437
  23.0 0.0 copy-start
  23.0 3.9 %shard_map.85 = f32[128,128]{1,0:T(8,128)S(1)} custom-call(f32[2,512,128]{2,1,0:T(8,128)} %bitcast.37, f32[128,128]{1,0:T(8,128)S(1)} %bitcast.29), custom_call_target="tpu_custom_call" | custom-call | tf_op jit(solution)/shard_map/pallas_call | solution.py:421
  27.0 15.4 %all_to_all.45 = f32[128,1,128]{2,1,0:T(1,128)S(1)} all-to-all(f32[128,1,128]{2,1,0:T(1,128)S(1)} %bitcast.35), channel_id=1, replica_groups=mesh['gx'=32,'gy'=4] {'gx','gy'}, dimensions={0} | all-to-all | bytes 131072 | tf_op jit(solution)/shard_map/all_to_all | solution.py:437
  42.3 1.1 shard_map.86
  43.4 0.5 collective-permute-start
  43.8 0.1 collective-permute-start.1
  44.0 1.8 %collective-permute-done.xn_ref.refs_1_ = f32[2,64,128]{2,1,0:T(8,128)S(1)} collective-permute-done((f32[2,64,128]{2,1,0:T(8,128)S(1)}, f32[2,64,128]{2,1,0:T(8,128)S(1)}, u32[]{:S(2)}, u32[]{:S(2)}) %collective-permute-start) | collective-permute-done | bytes 65568 | tf_op jit(solution)/shard_map/ppermute | solution.py:433
  45.7 5.1 %collective-permute-done.1.xp_ref.refs_2_ = f32[2,64,128]{2,1,0:T(8,128)S(1)} collective-permute-done((f32[2,64,128]{2,1,0:T(8,128)S(1)}, f32[2,64,128]{2,1,0:T(8,128)S(1)}, u32[]{:S(2)}, u32[]{:S(2)}) %collective-permute-start.1) | collective-permute-done | bytes 65568 | tf_op jit(solution)/shard_map/ppermute | solution.py:433
  50.9 1.5 %collective-permute-start.2 = (f32[2,64,128]{2,1,0:T(8,128)S(1)}, f32[2,64,128]{2,1,0:T(8,128)S(1)}, u32[]{:S(2)}, u32[]{:S(2)}) collective-permute-start(f32[2,64,128]{2,1,0:T(8,128)S(1)} %get-tuple-element.66), channel_id=1, source_target_pairs={{0,3},{1,0},{2,1},{3,2},{4,7},{5,4},{6,5},{7,6},{8,11},{9,8},{10,9... | collective-permute-start | bytes 196616 | tf_op jit(solution)/shard_map/ppermute | solution.py:433
  52.4 0.6 collective-permute-start.3
  53.0 2.2 %collective-permute-done.2.refs_3_ = f32[2,64,128]{2,1,0:T(8,128)S(1)} collective-permute-done((f32[2,64,128]{2,1,0:T(8,128)S(1)}, f32[2,64,128]{2,1,0:T(8,128)S(1)}, u32[]{:S(2)}, u32[]{:S(2)}) %collective-permute-start.2) | collective-permute-done | bytes 65568 | tf_op jit(solution)/shard_map/ppermute | solution.py:433
  55.2 2.7 %collective-permute-done.3.refs_4_ = f32[2,64,128]{2,1,0:T(8,128)S(1)} collective-permute-done((f32[2,64,128]{2,1,0:T(8,128)S(1)}, f32[2,64,128]{2,1,0:T(8,128)S(1)}, u32[]{:S(2)}, u32[]{:S(2)}) %collective-permute-start.3) | collective-permute-done | bytes 65568 | tf_op jit(solution)/shard_map/ppermute | solution.py:433
  57.9 0.0 copy-done
  57.9 4.7 %shard_map.88 = (f32[2,512,128]{2,1,0:T(8,128)}, f32[128,128]{1,0:T(8,128)}) custom-call(f32[2,512,128]{2,1,0:T(8,128)S(1)} %get-tuple-element.61.refs_0_, f32[2,64,128]{2,1,0:T(8,128)S(1)} %collective-permute-done.xn_ref.refs_1_, f32[2,64,128]{2,1,0:T(8,128)S(1)} %collective-permute-done.1.xp_ref.refs_2_, f32[2,64,128]{2,1,0:T(8,128)S(1)} %collective-permute-done.2.refs_3_, ...), custom_call_target="tpu_custom_call" | custom-call | tf_op jit(solution)/shard_map/pallas_call | solution.py:421
  62.6 4.8 %all-to-all-start.2 = ((f32[128,1,128]{2,1,0:T(1,128)}), f32[128,1,128]{2,1,0:T(1,128)S(1)}, u32[]{:S(2)}, u32[]{:S(2)}) async-start(f32[128,1,128]{2,1,0:T(1,128)} %bitcast.17), calls=%async_computation.2 | async-start | bytes 131072 | tf_op jit(solution)/shard_map/all_to_all | solution.py:437
  67.4 2.7 %shard_map.89 = (f32[2,512,128]{2,1,0:T(8,128)S(1)}, s32[3,1,2048]{2,1,0:T(1,128)S(1)}, f32[4,8,128]{2,1,0:T(8,128)S(1)}) custom-call(f32[2,512,128]{2,1,0:T(8,128)} %get-tuple-element.70.u_any.refs_6_, f32[3,2,512,128]{3,2,1,0:T(8,128)} %bitcast.43, f32[2,128]{1,0:T(2,128)} %bitcast.48, f32[2,512,128]{2,1,0:T(8,128)} %get-tuple-element.51.load_any, ...), custom_call_target="tpu_custom_call" | custom-call | tf_op jit(solution)/shard_map/pallas_call | solution.py:421
  70.2 6.5 %all-to-all-done.2 = f32[128,1,128]{2,1,0:T(1,128)S(1)} async-done(((f32[128,1,128]{2,1,0:T(1,128)}), f32[128,1,128]{2,1,0:T(1,128)S(1)}, u32[]{:S(2)}, u32[]{:S(2)}) %all-to-all-start.2) | async-done | bytes 65568 | tf_op jit(solution)/shard_map/all_to_all | solution.py:437
  76.7 1.1 shard_map.90
  77.8 0.5 collective-permute-start.4
  78.3 0.1 collective-permute-start.5
  78.4 1.8 %collective-permute-done.4.xn_ref.refs_1_ = f32[2,64,128]{2,1,0:T(8,128)S(1)} collective-permute-done((f32[2,64,128]{2,1,0:T(8,128)S(1)}, f32[2,64,128]{2,1,0:T(8,128)S(1)}, u32[]{:S(2)}, u32[]{:S(2)}) %collective-permute-start.4) | collective-permute-done | bytes 65568 | tf_op jit(solution)/shard_map/ppermute | solution.py:433
  80.2 5.1 %collective-permute-done.5.xp_ref.refs_2_ = f32[2,64,128]{2,1,0:T(8,128)S(1)} collective-permute-done((f32[2,64,128]{2,1,0:T(8,128)S(1)}, f32[2,64,128]{2,1,0:T(8,128)S(1)}, u32[]{:S(2)}, u32[]{:S(2)}) %collective-permute-start.5) | collective-permute-done | bytes 65568 | tf_op jit(solution)/shard_map/ppermute | solution.py:433
  85.3 1.5 %collective-permute-start.6 = (f32[2,64,128]{2,1,0:T(8,128)S(1)}, f32[2,64,128]{2,1,0:T(8,128)S(1)}, u32[]{:S(2)}, u32[]{:S(2)}) collective-permute-start(f32[2,64,128]{2,1,0:T(8,128)S(1)} %get-tuple-element.79), channel_id=1, source_target_pairs={{0,3},{1,0},{2,1},{3,2},{4,7},{5,4},{6,5},{7,6},{8,11},{9,8},{10,9... | collective-permute-start | bytes 196616 | tf_op jit(solution)/shard_map/ppermute | solution.py:433
  86.8 0.6 collective-permute-start.7
  87.4 2.2 %collective-permute-done.6.refs_3_ = f32[2,64,128]{2,1,0:T(8,128)S(1)} collective-permute-done((f32[2,64,128]{2,1,0:T(8,128)S(1)}, f32[2,64,128]{2,1,0:T(8,128)S(1)}, u32[]{:S(2)}, u32[]{:S(2)}) %collective-permute-start.6) | collective-permute-done | bytes 65568 | tf_op jit(solution)/shard_map/ppermute | solution.py:433
  89.6 2.7 %collective-permute-done.7.refs_4_ = f32[2,64,128]{2,1,0:T(8,128)S(1)} collective-permute-done((f32[2,64,128]{2,1,0:T(8,128)S(1)}, f32[2,64,128]{2,1,0:T(8,128)S(1)}, u32[]{:S(2)}, u32[]{:S(2)}) %collective-permute-start.7) | collective-permute-done | bytes 65568 | tf_op jit(solution)/shard_map/ppermute | solution.py:433
  92.3 4.9 %shard_map.92 = (f32[2,512,128]{2,1,0:T(8,128)}, f32[128,128]{1,0:T(8,128)}) custom-call(f32[2,512,128]{2,1,0:T(8,128)S(1)} %get-tuple-element.74.refs_0_, f32[2,64,128]{2,1,0:T(8,128)S(1)} %collective-permute-done.4.xn_ref.refs_1_, f32[2,64,128]{2,1,0:T(8,128)S(1)} %collective-permute-done.5.xp_ref.refs_2_, ...), custom_call_target="tpu_custom_call" | custom-call | tf_op jit(solution)/shard_map/pallas_call | solution.py:421
  97.2 4.6 %all-to-all-start.3 = ((f32[128,1,128]{2,1,0:T(1,128)}), f32[128,1,128]{2,1,0:T(1,128)S(1)}, u32[]{:S(2)}, u32[]{:S(2)}) async-start(f32[128,1,128]{2,1,0:T(1,128)} %bitcast.20), calls=%async_computation.3 | async-start | bytes 131072 | tf_op jit(solution)/shard_map/all_to_all | solution.py:437
  101.9 2.7 %shard_map.93 = (f32[2,512,128]{2,1,0:T(8,128)S(1)}, s32[3,1,2048]{2,1,0:T(1,128)S(1)}, f32[4,8,128]{2,1,0:T(8,128)S(1)}) custom-call(f32[2,512,128]{2,1,0:T(8,128)} %get-tuple-element.82.u_any.refs_6_, f32[3,2,512,128]{3,2,1,0:T(8,128)} %bitcast.44, f32[2,128]{1,0:T(2,128)} %bitcast.49, f32[2,512,128]{2,1,0:T(8,128)} %get-tuple-element.51.load_any, ...), custom_call_target="tpu_custom_call" | custom-call | tf_op jit(solution)/shard_map/pallas_call | solution.py:421
  104.6 6.5 %all-to-all-done.3 = f32[128,1,128]{2,1,0:T(1,128)S(1)} async-done(((f32[128,1,128]{2,1,0:T(1,128)}), f32[128,1,128]{2,1,0:T(1,128)S(1)}, u32[]{:S(2)}, u32[]{:S(2)}) %all-to-all-start.3) | async-done | bytes 65568 | tf_op jit(solution)/shard_map/all_to_all | solution.py:437
  111.2 1.1 shard_map.94
  112.2 0.5 collective-permute-start.8
  112.7 0.1 collective-permute-start.9
  112.8 1.8 %collective-permute-done.8.xn_ref.refs_1_ = f32[2,64,128]{2,1,0:T(8,128)S(1)} collective-permute-done((f32[2,64,128]{2,1,0:T(8,128)S(1)}, f32[2,64,128]{2,1,0:T(8,128)S(1)}, u32[]{:S(2)}, u32[]{:S(2)}) %collective-permute-start.8) | collective-permute-done | bytes 65568 | tf_op jit(solution)/shard_map/ppermute | solution.py:433
  114.6 5.1 %collective-permute-done.9.xp_ref.refs_2_ = f32[2,64,128]{2,1,0:T(8,128)S(1)} collective-permute-done((f32[2,64,128]{2,1,0:T(8,128)S(1)}, f32[2,64,128]{2,1,0:T(8,128)S(1)}, u32[]{:S(2)}, u32[]{:S(2)}) %collective-permute-start.9) | collective-permute-done | bytes 65568 | tf_op jit(solution)/shard_map/ppermute | solution.py:433
  119.7 1.5 %collective-permute-start.10 = (f32[2,64,128]{2,1,0:T(8,128)S(1)}, f32[2,64,128]{2,1,0:T(8,128)S(1)}, u32[]{:S(2)}, u32[]{:S(2)}) collective-permute-start(f32[2,64,128]{2,1,0:T(8,128)S(1)} %get-tuple-element.91), channel_id=1, source_target_pairs={{0,3},{1,0},{2,1},{3,2},{4,7},{5,4},{6,5},{7,6},{8,11},{9,8},{10,9... | collective-permute-start | bytes 196616 | tf_op jit(solution)/shard_map/ppermute | solution.py:433
  121.2 0.6 collective-permute-start.11
  121.8 2.2 %collective-permute-done.10.refs_3_ = f32[2,64,128]{2,1,0:T(8,128)S(1)} collective-permute-done((f32[2,64,128]{2,1,0:T(8,128)S(1)}, f32[2,64,128]{2,1,0:T(8,128)S(1)}, u32[]{:S(2)}, u32[]{:S(2)}) %collective-permute-start.10) | collective-permute-done | bytes 65568 | tf_op jit(solution)/shard_map/ppermute | solution.py:433
  124.0 2.7 %collective-permute-done.11.refs_4_ = f32[2,64,128]{2,1,0:T(8,128)S(1)} collective-permute-done((f32[2,64,128]{2,1,0:T(8,128)S(1)}, f32[2,64,128]{2,1,0:T(8,128)S(1)}, u32[]{:S(2)}, u32[]{:S(2)}) %collective-permute-start.11) | collective-permute-done | bytes 65568 | tf_op jit(solution)/shard_map/ppermute | solution.py:433
  126.7 2.3 %shard_map.96 = f32[2,512,128]{2,1,0:T(8,128)} custom-call(f32[2,512,128]{2,1,0:T(8,128)S(1)} %get-tuple-element.86.refs_0_, f32[2,64,128]{2,1,0:T(8,128)S(1)} %collective-permute-done.8.xn_ref.refs_1_, f32[2,64,128]{2,1,0:T(8,128)S(1)} %collective-permute-done.9.xp_ref.refs_2_, f32[2,64,128]{2,1,0:T(8,128)S(1)} %collective-permute-done.10.refs_3_, ...), custom_call_target="tpu_custom_call" | custom-call | tf_op jit(solution)/shard_map/pallas_call | solution.py:421
  (3 shorter events, 0.0 us)
Async XLA Ops:
  2.6 20.5 %all-to-all-start = ((f32[128,1,128]{2,1,0:T(1,128)}), f32[128,1,128]{2,1,0:T(1,128)S(1)}, u32[]{:S(2)}, u32[]{:S(2)}) async-start(f32[128,1,128]{2,1,0:T(1,128)} %bitcast.4), calls=%async_computation | async-start | bytes 131072 | tf_op jit(solution)/shard_map/all_to_all | solution.py:437
  23.0 34.8 %copy-start = (f32[128,1,128]{2,1,0:T(1,128)}, f32[128,1,128]{2,1,0:T(1,128)S(1)}, u32[]{:S(2)}) copy-start(f32[128,1,128]{2,1,0:T(1,128)S(1)} %all-to-all-done) | copy-start | bytes 196612
  43.4 2.4 %collective-permute-start = (f32[2,64,128]{2,1,0:T(8,128)S(1)}, f32[2,64,128]{2,1,0:T(8,128)S(1)}, u32[]{:S(2)}, u32[]{:S(2)}) collective-permute-start(f32[2,64,128]{2,1,0:T(8,128)S(1)} %get-tuple-element.62), channel_id=1, source_target_pairs={{0,124},{4,0},{8,4},{12,8},{16,12},{20,16},{24,20},{28,24},{32,28}... | collective-permute-start | bytes 196616 | tf_op jit(solution)/shard_map/ppermute | solution.py:433
  43.8 7.0 %collective-permute-start.1 = (f32[2,64,128]{2,1,0:T(8,128)S(1)}, f32[2,64,128]{2,1,0:T(8,128)S(1)}, u32[]{:S(2)}, u32[]{:S(2)}) collective-permute-start(f32[2,64,128]{2,1,0:T(8,128)S(1)} %get-tuple-element.63), channel_id=1, source_target_pairs={{0,4},{4,8},{8,12},{12,16},{16,20},{20,24},{24,28},{28,32},{32,36}... | collective-permute-start | bytes 196616 | tf_op jit(solution)/shard_map/ppermute | solution.py:433
  50.9 4.3 %collective-permute-start.2 = (f32[2,64,128]{2,1,0:T(8,128)S(1)}, f32[2,64,128]{2,1,0:T(8,128)S(1)}, u32[]{:S(2)}, u32[]{:S(2)}) collective-permute-start(f32[2,64,128]{2,1,0:T(8,128)S(1)} %get-tuple-element.66), channel_id=1, source_target_pairs={{0,3},{1,0},{2,1},{3,2},{4,7},{5,4},{6,5},{7,6},{8,11},{9,8},{10,9... | collective-permute-start | bytes 196616 | tf_op jit(solution)/shard_map/ppermute | solution.py:433
  52.4 5.5 %collective-permute-start.3 = (f32[2,64,128]{2,1,0:T(8,128)S(1)}, f32[2,64,128]{2,1,0:T(8,128)S(1)}, u32[]{:S(2)}, u32[]{:S(2)}) collective-permute-start(f32[2,64,128]{2,1,0:T(8,128)S(1)} %get-tuple-element.67), channel_id=1, source_target_pairs={{0,1},{1,2},{2,3},{3,0},{4,5},{5,6},{6,7},{7,4},{8,9},{9,10},{10,1... | collective-permute-start | bytes 196616 | tf_op jit(solution)/shard_map/ppermute | solution.py:433
  62.6 14.1 %all-to-all-start.2 = ((f32[128,1,128]{2,1,0:T(1,128)}), f32[128,1,128]{2,1,0:T(1,128)S(1)}, u32[]{:S(2)}, u32[]{:S(2)}) async-start(f32[128,1,128]{2,1,0:T(1,128)} %bitcast.17), calls=%async_computation.2 | async-start | bytes 131072 | tf_op jit(solution)/shard_map/all_to_all | solution.py:437
  77.8 2.4 %collective-permute-start.4 = (f32[2,64,128]{2,1,0:T(8,128)S(1)}, f32[2,64,128]{2,1,0:T(8,128)S(1)}, u32[]{:S(2)}, u32[]{:S(2)}) collective-permute-start(f32[2,64,128]{2,1,0:T(8,128)S(1)} %get-tuple-element.75), channel_id=1, source_target_pairs={{0,124},{4,0},{8,4},{12,8},{16,12},{20,16},{24,20},{28,24},{32,28}... | collective-permute-start | bytes 196616 | tf_op jit(solution)/shard_map/ppermute | solution.py:433
  78.3 7.0 %collective-permute-start.5 = (f32[2,64,128]{2,1,0:T(8,128)S(1)}, f32[2,64,128]{2,1,0:T(8,128)S(1)}, u32[]{:S(2)}, u32[]{:S(2)}) collective-permute-start(f32[2,64,128]{2,1,0:T(8,128)S(1)} %get-tuple-element.76), channel_id=1, source_target_pairs={{0,4},{4,8},{8,12},{12,16},{16,20},{20,24},{24,28},{28,32},{32,36}... | collective-permute-start | bytes 196616 | tf_op jit(solution)/shard_map/ppermute | solution.py:433
  85.3 4.3 %collective-permute-start.6 = (f32[2,64,128]{2,1,0:T(8,128)S(1)}, f32[2,64,128]{2,1,0:T(8,128)S(1)}, u32[]{:S(2)}, u32[]{:S(2)}) collective-permute-start(f32[2,64,128]{2,1,0:T(8,128)S(1)} %get-tuple-element.79), channel_id=1, source_target_pairs={{0,3},{1,0},{2,1},{3,2},{4,7},{5,4},{6,5},{7,6},{8,11},{9,8},{10,9... | collective-permute-start | bytes 196616 | tf_op jit(solution)/shard_map/ppermute | solution.py:433
  86.8 5.5 %collective-permute-start.7 = (f32[2,64,128]{2,1,0:T(8,128)S(1)}, f32[2,64,128]{2,1,0:T(8,128)S(1)}, u32[]{:S(2)}, u32[]{:S(2)}) collective-permute-start(f32[2,64,128]{2,1,0:T(8,128)S(1)} %get-tuple-element.80), channel_id=1, source_target_pairs={{0,1},{1,2},{2,3},{3,0},{4,5},{5,6},{6,7},{7,4},{8,9},{9,10},{10,1... | collective-permute-start | bytes 196616 | tf_op jit(solution)/shard_map/ppermute | solution.py:433
  97.2 13.9 %all-to-all-start.3 = ((f32[128,1,128]{2,1,0:T(1,128)}), f32[128,1,128]{2,1,0:T(1,128)S(1)}, u32[]{:S(2)}, u32[]{:S(2)}) async-start(f32[128,1,128]{2,1,0:T(1,128)} %bitcast.20), calls=%async_computation.3 | async-start | bytes 131072 | tf_op jit(solution)/shard_map/all_to_all | solution.py:437
  112.2 2.4 %collective-permute-start.8 = (f32[2,64,128]{2,1,0:T(8,128)S(1)}, f32[2,64,128]{2,1,0:T(8,128)S(1)}, u32[]{:S(2)}, u32[]{:S(2)}) collective-permute-start(f32[2,64,128]{2,1,0:T(8,128)S(1)} %get-tuple-element.87), channel_id=1, source_target_pairs={{0,124},{4,0},{8,4},{12,8},{16,12},{20,16},{24,20},{28,24},{32,28}... | collective-permute-start | bytes 196616 | tf_op jit(solution)/shard_map/ppermute | solution.py:433
  112.7 7.0 %collective-permute-start.9 = (f32[2,64,128]{2,1,0:T(8,128)S(1)}, f32[2,64,128]{2,1,0:T(8,128)S(1)}, u32[]{:S(2)}, u32[]{:S(2)}) collective-permute-start(f32[2,64,128]{2,1,0:T(8,128)S(1)} %get-tuple-element.88), channel_id=1, source_target_pairs={{0,4},{4,8},{8,12},{12,16},{16,20},{20,24},{24,28},{28,32},{32,36}... | collective-permute-start | bytes 196616 | tf_op jit(solution)/shard_map/ppermute | solution.py:433
  119.7 4.3 %collective-permute-start.10 = (f32[2,64,128]{2,1,0:T(8,128)S(1)}, f32[2,64,128]{2,1,0:T(8,128)S(1)}, u32[]{:S(2)}, u32[]{:S(2)}) collective-permute-start(f32[2,64,128]{2,1,0:T(8,128)S(1)} %get-tuple-element.91), channel_id=1, source_target_pairs={{0,3},{1,0},{2,1},{3,2},{4,7},{5,4},{6,5},{7,6},{8,11},{9,8},{10,9... | collective-permute-start | bytes 196616 | tf_op jit(solution)/shard_map/ppermute | solution.py:433
  121.2 5.5 %collective-permute-start.11 = (f32[2,64,128]{2,1,0:T(8,128)S(1)}, f32[2,64,128]{2,1,0:T(8,128)S(1)}, u32[]{:S(2)}, u32[]{:S(2)}) collective-permute-start(f32[2,64,128]{2,1,0:T(8,128)S(1)} %get-tuple-element.92), channel_id=1, source_target_pairs={{0,1},{1,2},{2,3},{3,0},{4,5},{5,6},{6,7},{7,4},{8,9},{9,10},{10,1... | collective-permute-start | bytes 196616 | tf_op jit(solution)/shard_map/ppermute | solution.py:433

commit v3 on v2

--- a/solution.py
+++ b/solution.py
@@ -84,8 +84,8 @@
 
 
 def one_hot_rows(row, count, dtype=bf16):
-    ids = lax.broadcasted_iota(i32, (count, row.shape[-1]), 0)
-    return jnp.where(ids == row, 1.0, 0.0).astype(dtype)
+    ids = lax.broadcasted_iota(jnp.int16, (count, row.shape[-1]), 0)
+    return jnp.where(ids == row.astype(jnp.int16), jnp.ones((), dtype), jnp.zeros((), dtype))
 
 
 def weight_rows():
@@ -157,20 +157,22 @@
     out.wait()
 
 
-def prepare_kernel(flags_ref, owner_any, rank_any, point_any, load_any, inv_any, table_any, mask_any,
-                   load_ref, inv_ref, table_ref, mask_ref, sems):
+def prepare_kernel(flags_ref, owner_any, rank_any, point_any, load_any, inv_any, table_any, mask_any, low_any, high_any,
+                   load_ref, inv_ref, table_ref, mask_ref, low_ref, high_ref, sems):
     copies = start_copies(
-        [(owner_any, table_ref.at[0]), (rank_any, table_ref.at[1]), (point_any, table_ref.at[2])], sems
+        [(owner_any, table_ref.at[0:1]), (rank_any, table_ref.at[1:2]), (point_any, table_ref.at[2:3])], sems
     )
     for n in range(4):
-        mask_ref[n] = jnp.full((8, 128), 2.0 - 2.0 * flags_ref[n], f32)
+        mask_ref[n] = jnp.full((8, 128), flags_ref[n], i32).astype(f32)
     for copy in copies:
         copy.wait()
-    point_ref = table_ref.at[2]
-    half = point_ref.shape[1] // 2
+    for n, ref in enumerate((low_ref, high_ref)):
+        ref[0:2, :] = table_ref[0:2, :]
+        ref[2:3, :] = (table_ref[2:3, :] + 1) * flags_ref[n + 2] - 1
+    half = table_ref.shape[1] // 2
     wk = weight_rows()
     for m in range(2):
-        point = point_ref[:, m * half : (m + 1) * half]
+        point = table_ref[2:3, m * half : (m + 1) * half]
         q = lax.shift_right_logical(point, 7)
         e = lax.bitwise_and(point, 127)
         count = dot_nt(one_hot_rows(q, 512), one_hot_rows(e, 128))
@@ -184,32 +186,56 @@
     for ij in range(64):
         i, j = ij // 8, ij % 8
         val = base * (1.0 / (WEIGHTS[i] * WEIGHTS[j]))
-        if i == 0:
-            val = val * flags_ref[0]
-        if i == 7:
-            val = val * flags_ref[1]
-        if j == 0:
-            val = val * flags_ref[2]
-        if j == 7:
-            val = val * flags_ref[3]
+        if i in (0, 7):
+            val = val * (1.0 - 0.5 * mask_ref[0 if i == 0 else 1])
+        if j in (0, 7):
+            val = val * (1.0 - 0.5 * mask_ref[2 if j == 0 else 3])
         inv_ref[ij * 8 : ij * 8 + 8, :] = val
     copies = start_copies(
-        [(load_ref, load_any), (inv_ref, inv_any), (table_ref, table_any), (mask_ref, mask_any)], sems
+        [(load_ref, load_any), (inv_ref, inv_any), (table_ref, table_any), (mask_ref, mask_any),
+         (low_ref, low_any), (high_ref, high_any)],
+        sems,
     )
     for copy in copies:
         copy.wait()
 
 
-def local_kernel(u_any, vel_any, nu_any, load_any, deep_any, table_any, mask_any, out_ref, table_ref, mask_ref, u_ref, vel_ref, nu_ref, load_ref, deep_ref,
-                 ax_ref, ay_ref, fz_ref, sems):
-    copies = start_copies(
-        [(u_any, u_ref), (deep_any, deep_ref), (nu_any, nu_ref), (vel_any, vel_ref), (load_any, load_ref),
-         (table_any, table_ref), (mask_any, mask_ref)],
-        sems,
-    )
+def relay_kernel(flags_ref, own_ref, below_ref, above_ref, low_ref, high_ref):
+    for n, ref in ((0, low_ref), (1, high_ref)):
+        for t, src in enumerate((own_ref, below_ref, above_ref)):
+            ref[3 * t : 3 * t + 2, :] = src[0:2, :]
+            ref[3 * t + 2 : 3 * t + 3, :] = (src[2:3, :] + 1) * flags_ref[n] - 1
+
+
+GHOSTS = [(-1, 0), (1, 0), (0, -1), (0, 1), (-1, -1), (-1, 1), (1, -1), (1, 1)]
+
+
+def ghost_kernel(xp_ref, xn_ref, yp_ref, yn_ref, out_any, out_ref, sems):
+    for n, (dx, dy) in enumerate(GHOSTS):
+        if dx == 0:
+            src, base = (yp_ref, 0) if dy < 0 else (yn_ref, 0)
+        else:
+            src, base = (xp_ref if dx < 0 else xn_ref), {0: 0, -1: 3, 1: 6}[dy]
+        point = src[base + 2 : base + 3, :]
+        q = lax.shift_right_arithmetic(point, 7)
+        i = lax.shift_right_arithmetic(q, 6)
+        j = lax.bitwise_and(lax.shift_right_arithmetic(q, 3), 7)
+        k = lax.bitwise_and(q, 7)
+        good = point >= 0
+        if dx:
+            good = good & (i == (7 if dx < 0 else 0))
+        if dy:
+            good = good & (j == (7 if dy < 0 else 0))
+        row = k if dx and dy else (j * 8 + k if dx else i * 8 + k)
+        out_ref[n, 0:2, :] = src[base : base + 2, :]
+        out_ref[n, 2:3, :] = jnp.where(good, row, -1)
+        out_ref[n, 3:4, :] = lax.bitwise_and(point, 127)
+    copies = start_copies([(out_ref, out_any)], sems)
+    copies[0].wait()
+
+
+def local_rates(u_ref, vel_ref, nu_ref, load_ref, deep_ref, out_ref, ax_ref, ay_ref, fz_ref, copies):
     wk = weight_rows()
-    copies[0].wait()
-    copies[1].wait()
 
     def depth(table, pick):
         chunks = []
@@ -225,7 +251,7 @@
             outs = apply_table(DERIV, [u_ref[m, i * 64 + j * 8 : i * 64 + j * 8 + 8, :] for i in range(8)])
             for i in range(8):
                 ax_ref[m, i * 64 + j * 8 : i * 64 + j * 8 + 8, :] = outs[i]
-    for copy in copies[2:]:
+    for copy in copies:
         copy.wait()
     for m in range(2):
         wnu = 4.0 * volume_factor * wk * nu_ref[m : m + 1, :]
@@ -261,9 +287,35 @@
                 out_ref[m, rows, :] = (out_ref[m, rows, :] - outs[i]) - gz
 
 
-def interpolate(u, received_ref, ans_ref, wx_ref, wy_ref, wz_ref):
+def send_faces(loc_ref, mask_ref, xl_ref, xr_ref, yl_ref, yr_ref, keep_ref):
+    for m in range(2):
+        for n in range(8):
+            rows = slice(n * 8, n * 8 + 8)
+            xl_ref[m, rows, :] = loc_ref[m, rows, :]
+            xr_ref[m, rows, :] = loc_ref[m, 448 + n * 8 : 456 + n * 8, :]
+            yl_ref[m, rows, :] = loc_ref[m, n * 64 : n * 64 + 8, :] * mask_ref[2]
+            yr_ref[m, rows, :] = loc_ref[m, n * 64 + 56 : n * 64 + 64, :] * mask_ref[3]
+    keep_ref[...] = mask_ref[0:2]
+
+
+def local_kernel(u_any, vel_any, nu_any, load_any, deep_any, mask_any, loc_ref, xl_ref, xr_ref, yl_ref, yr_ref, keep_ref,
+                 u_ref, vel_ref, nu_ref, load_ref, deep_ref, mask_ref, ax_ref, ay_ref, fz_ref, sems):
+    copies = start_copies(
+        [(u_any, u_ref), (deep_any, deep_ref), (nu_any, nu_ref), (vel_any, vel_ref), (load_any, load_ref),
+         (mask_any, mask_ref)],
+        sems,
+    )
+    copies[0].wait()
+    copies[1].wait()
+    local_rates(u_ref, vel_ref, nu_ref, load_ref, deep_ref, loc_ref, ax_ref, ay_ref, fz_ref, copies[2:])
+    send_faces(loc_ref, mask_ref, xl_ref, xr_ref, yl_ref, yr_ref, keep_ref)
+
+
+def interpolate(u, received_ref, ans_ref, wx_ref, wy_ref, wz_ref, copies):
     parts = [split_two(v) for v in u]
     cat = jnp.concatenate([parts[0][0], parts[1][0], parts[0][1], parts[1][1]], axis=1)
+    for copy in copies:
+        copy.wait()
     turned = received_ref[...].T
     for v, ref in enumerate((wx_ref, wy_ref, wz_ref)):
         x = turned[v * 32 : v * 32 + 32, :]
@@ -302,31 +354,97 @@
                 acc = acc * wy_ref[j, s : s + 1, :]
                 total = acc if total is None else total + acc
             rows.append(jnp.sum(total * wz_ref[s], axis=0, keepdims=True))
-    answers = jnp.concatenate(rows + [jnp.zeros((96, 128), f32)], axis=0)
-    ans_ref[...] = answers.T
+    answers = jnp.concatenate(rows, axis=0)
+    blocks = [answers]
+    for dx, dy in GHOSTS:
+        blocks.append(pltpu.roll(answers, (-(4 * dx + dy)) % 128, 1))
+    for a in range(3):
+        group = blocks[4 * a : 4 * a + 4]
+        if len(group) < 4:
+            group = group + [jnp.zeros((32 * (4 - len(group)), 128), f32)]
+        ans_ref[:, a, :] = jnp.concatenate(group, axis=0).T
+    ans_ref[:, 3, :] = jnp.zeros((128, 128), f32)
+
+
+def answer_kernel(u_ref, received_any, ans_ref, received_ref, wx_ref, wy_ref, wz_ref, sems):
+    copies = start_copies([(received_any, received_ref)], sems)
+    interpolate([u_ref[0], u_ref[1]], received_ref, ans_ref, wx_ref, wy_ref, wz_ref, copies)
 
 
 def first_kernel(u_any, received_ref, ans_ref, u_ref, wx_ref, wy_ref, wz_ref, sems):
     copies = start_copies([(u_any, u_ref)], sems)
     copies[0].wait()
-    interpolate([u_ref[0], u_ref[1]], received_ref, ans_ref, wx_ref, wy_ref, wz_ref)
-
-
-def penalty_kernel(replies_ref, table_ref, mask_ref, local_ref, out_ref, xl_ref, xr_ref, yl_ref, yr_ref):
-    owner_ref, rank_ref, point_ref = table_ref.at[0], table_ref.at[1], table_ref.at[2]
-    half = point_ref.shape[1] // 2
-    hi, lo = split_two(replies_ref[...].T[0:32, :])
-    lhs = jnp.concatenate([hi, lo], axis=1)
+    interpolate([u_ref[0], u_ref[1]], received_ref, ans_ref, wx_ref, wy_ref, wz_ref, [])
+
+
+def edge_kernel(xl_ref, xr_ref, yn_ref, yp_ref, keep_ref, xl_out, xr_out):
+    for m in range(2):
+        for src, dst, i in ((xl_ref, xl_out, 0), (xr_ref, xr_out, 7)):
+            mask = keep_ref[0 if i == 0 else 1]
+            for j in range(8):
+                val = src[m, j * 8 : j * 8 + 8, :]
+                if j == 0:
+                    val = val + yp_ref[m, i * 8 : i * 8 + 8, :]
+                if j == 7:
+                    val = val + yn_ref[m, i * 8 : i * 8 + 8, :]
+                dst[m, j * 8 : j * 8 + 8, :] = val * mask
+
+
+def bring_kernel(after_ref, table_any, ghost_any, table_ref, ghost_ref, sems):
+    copies = start_copies([(table_any, table_ref), (ghost_any, ghost_ref)], sems)
+    for copy in copies:
+        copy.wait()
+
+
+def with_faces(parts, m, ij):
+    loc_ref, xn_ref, xp_ref, yn_ref, yp_ref = parts
+    i, j = ij // 8, ij % 8
+    val = loc_ref[m, ij * 8 : ij * 8 + 8, :]
+    if j == 0:
+        val = val + yp_ref[m, i * 8 : i * 8 + 8, :]
+    elif j == 7:
+        val = val + yn_ref[m, i * 8 : i * 8 + 8, :]
+    if i == 0:
+        val = val + xp_ref[m, j * 8 : j * 8 + 8, :]
+    elif i == 7:
+        val = val + xn_ref[m, j * 8 : j * 8 + 8, :]
+    return val
+
+
+def picked(block, owner, rank):
+    parts = []
+    for c in range(owner.shape[1] // 128):
+        sl = slice(c * 128, (c + 1) * 128)
+        index = jnp.broadcast_to(owner[:, sl], (32, 128))
+        got = jnp.take_along_axis(block, index, axis=1, mode="promise_in_bounds")
+        pick = lax.broadcasted_iota(i32, (32, 128), 0) == rank[:, sl]
+        parts.append(jnp.sum(jnp.where(pick, got, 0.0), axis=0, keepdims=True))
+    g = jnp.concatenate(parts, axis=1)
+    ghi = g.astype(bf16).astype(f32)
+    return ghi, g - ghi
+
+
+def add_replies(replies_ref, table_ref, ghost_ref, parts, work_ref):
+    half = table_ref.shape[1] // 2
     wk = weight_rows()
+    blocks = []
+    for a in range(3):
+        turned = replies_ref[:, a, :].T
+        for c in range(4):
+            if 4 * a + c < 9:
+                blocks.append(turned[c * 32 : c * 32 + 32, :])
     for m in range(2):
         sl = slice(m * half, (m + 1) * half)
-        oh = one_hot_rows(owner_ref[:, sl], 128)
-        got = dot_nn(lhs, jnp.concatenate([oh, oh], axis=0))
-        pick = lax.broadcasted_iota(i32, (32, half), 0) == rank_ref[:, sl]
-        g = jnp.sum(jnp.where(pick, got, 0.0), axis=0, keepdims=True)
-        ghi = g.astype(bf16).astype(f32)
-        glo = g - ghi
-        point = point_ref[:, sl]
+        faces = {}
+        for n, where in enumerate(GHOSTS):
+            ghi, glo = picked(blocks[n + 1], ghost_ref[n, 0:1, sl], ghost_ref[n, 1:2, sl])
+            size = 8 if where[0] and where[1] else 64
+            at = lax.broadcasted_iota(i32, (size, half), 0) == ghost_ref[n, 2:3, sl]
+            lhs = jnp.concatenate([jnp.where(at, ghi, 0.0), jnp.where(at, glo, 0.0)], axis=0).astype(bf16)
+            both = dot_nt(lhs, one_hot_rows(ghost_ref[n, 3:4, sl], 128))
+            faces[where] = both[0:size, :] + both[size : 2 * size, :]
+        ghi, glo = picked(blocks[0], table_ref[0:1, sl], table_ref[1:2, sl])
+        point = table_ref[2:3, sl]
         q = lax.shift_right_logical(point, 7)
         e = lax.bitwise_and(point, 127)
         at = lax.broadcasted_iota(i32, (128, half), 0) == e
@@ -338,83 +456,63 @@
         for ij in range(64):
             rows = slice(ij * 8, ij * 8 + 8)
             i, j = ij // 8, ij % 8
+            dx = {0: -1, 7: 1}.get(i, 0)
+            dy = {0: -1, 7: 1}.get(j, 0)
             c = penalty_rate * volume_factor * WEIGHTS[i] * WEIGHTS[j]
-            val = local_ref[m, rows, :] + (c * wk) * summed[rows, :]
-            out_ref[m, rows, :] = val
-            if i == 0:
-                xl_ref[m, j * 8 : j * 8 + 8, :] = val * mask_ref[0]
-            if i == 7:
-                xr_ref[m, j * 8 : j * 8 + 8, :] = val * mask_ref[1]
-            if j == 0:
-                yl_ref[m, i * 8 : i * 8 + 8, :] = val
-            if j == 7:
-                yr_ref[m, i * 8 : i * 8 + 8, :] = val
-
-
-def edge_kernel(yl_ref, yr_ref, xn_ref, xp_ref, mask_ref, yl_out, yr_out):
-    for m in range(2):
-        for src, dst, j in ((yl_ref, yl_out, 0), (yr_ref, yr_out, 7)):
-            mask = mask_ref[2 if j == 0 else 3]
-            for i in range(8):
-                val = src[m, i * 8 : i * 8 + 8, :]
-                if i == 0:
-                    val = val + xp_ref[m, j * 8 : j * 8 + 8, :]
-                if i == 7:
-                    val = val + xn_ref[m, j * 8 : j * 8 + 8, :]
-                dst[m, i * 8 : i * 8 + 8, :] = val * mask
-
-
-def finish(blend, v_ref, xn_ref, xp_ref, yn_ref, yp_ref, start_ref, u_ref, inv_ref, new_ref, work_ref, copies):
+            g = summed[rows, :]
+            if dx:
+                g = g + faces[(dx, 0)][j * 8 : j * 8 + 8, :]
+            if dy:
+                g = g + faces[(0, dy)][i * 8 : i * 8 + 8, :]
+            if dx and dy:
+                g = g + faces[(dx, dy)]
+            work_ref[m, rows, :] = with_faces(parts, m, ij) + (c * wk) * g
+
+
+def advance(blend, start_ref, u_ref, inv_ref, work_ref, new_ref):
     lane = lax.broadcasted_iota(i32, (64, 128), 1)
     for m in range(2):
-        for ij in range(64):
-            rows = slice(ij * 8, ij * 8 + 8)
-            i, j = ij // 8, ij % 8
-            val = v_ref[m, rows, :]
-            if j == 0:
-                val = val + yp_ref[m, i * 8 : i * 8 + 8, :]
-            elif j == 7:
-                val = val + yn_ref[m, i * 8 : i * 8 + 8, :]
-            if i == 0:
-                val = val + xp_ref[m, j * 8 : j * 8 + 8, :]
-            elif i == 7:
-                val = val + xn_ref[m, j * 8 : j * 8 + 8, :]
-            work_ref[m, rows, :] = val
         left = work_ref[m, pl.ds(0, 64, stride=8), :]
         right = work_ref[m, pl.ds(7, 64, stride=8), :]
         work_ref[m, pl.ds(0, 64, stride=8), :] = left + jnp.where(lane > 0, pltpu.roll(right, 1, 1), 0.0)
         work_ref[m, pl.ds(7, 64, stride=8), :] = right + jnp.where(lane < 127, pltpu.roll(left, 127, 1), 0.0)
-    for copy in copies:
-        copy.wait()
-    for m in range(2):
         new = u_ref[m] + inv_ref[...] * work_ref[m]
         if blend is not None:
             new = blend[0] * start_ref[m] + blend[1] * new
         new_ref[m] = new
 
 
-def step_kernel(blend, v_ref, xn_ref, xp_ref, yn_ref, yp_ref, start_any, u_any, inv_any, received_any,
-                new_any, ans_ref, work_ref, start_ref, u_ref, inv_ref, received_ref, new_ref,
-                wx_ref, wy_ref, wz_ref, sems):
-    pairs = [(u_any, u_ref), (inv_any, inv_ref), (received_any, received_ref)]
-    if blend is not None:
-        pairs.append((start_any, start_ref))
-    copies = start_copies(pairs, sems)
-    finish(blend, v_ref, xn_ref, xp_ref, yn_ref, yp_ref, start_ref, u_ref, inv_ref, new_ref, work_ref, copies)
-    out = pltpu.make_async_copy(new_ref, new_any, sems.at[4])
+def step_kernel(blend, replies_ref, table_ref, ghost_ref, old_ref, xn_ref, xp_ref, yn_ref, yp_ref, start_any, u_any, inv_any, vel_any, nu_any, load_any,
+                deep_any, mask_any, new_any, new_ref, loc_ref, xl_ref, xr_ref, yl_ref, yr_ref, keep_ref,
+                work_ref, start_ref, u_ref, inv_ref, vel_ref, nu_ref, load_ref, deep_ref, mask_ref,
+                ax_ref, ay_ref, fz_ref, sems):
+    copies = start_copies(
+        [(u_any, u_ref), (inv_any, inv_ref), (start_any, start_ref), (deep_any, deep_ref), (nu_any, nu_ref),
+         (vel_any, vel_ref), (load_any, load_ref), (mask_any, mask_ref)],
+        sems,
+    )
+    add_replies(replies_ref, table_ref, ghost_ref, (old_ref, xn_ref, xp_ref, yn_ref, yp_ref), work_ref)
+    for copy in copies[:4]:
+        copy.wait()
+    advance(blend, start_ref, u_ref, inv_ref, work_ref, new_ref)
+    out = pltpu.make_async_copy(new_ref, new_any, sems.at[8])
     out.start()
-    interpolate([new_ref[0], new_ref[1]], received_ref, ans_ref, wx_ref, wy_ref, wz_ref)
+    local_rates(new_ref, vel_ref, nu_ref, load_ref, deep_ref, loc_ref, ax_ref, ay_ref, fz_ref, copies[4:])
+    send_faces(loc_ref, mask_ref, xl_ref, xr_ref, yl_ref, yr_ref, keep_ref)
     out.wait()
 
 
-def last_kernel(blend, v_ref, xn_ref, xp_ref, yn_ref, yp_ref, start_any, u_any, inv_any, new_ref,
+def last_kernel(blend, replies_ref, table_ref, ghost_ref, old_ref, xn_ref, xp_ref, yn_ref, yp_ref, start_any, u_any, inv_any, new_ref,
                 work_ref, start_ref, u_ref, inv_ref, sems):
     copies = start_copies([(u_any, u_ref), (inv_any, inv_ref), (start_any, start_ref)], sems)
-    finish(blend, v_ref, xn_ref, xp_ref, yn_ref, yp_ref, start_ref, u_ref, inv_ref, new_ref, work_ref, copies)
-
-
-PINNED = "a"
-SPACES = {"v": pltpu.VMEM, "a": pltpu.HBM, "s": pltpu.SMEM}
+    add_replies(replies_ref, table_ref, ghost_ref, (old_ref, xn_ref, xp_ref, yn_ref, yp_ref), work_ref)
+    for copy in copies:
+        copy.wait()
+    advance(blend, start_ref, u_ref, inv_ref, work_ref, new_ref)
+
+
+PINNED = "ap"
+SPACES = {"p": pltpu.VMEM, "v": pltpu.VMEM, "a": pltpu.HBM, "s": pltpu.SMEM}
 
 
 def call(kernel, outs, ins, scratch=(), spaces="", out_spaces=""):
@@ -424,7 +522,7 @@
         in_specs=[pl.BlockSpec(memory_space=SPACES[c]) for c in spaces],
         out_specs=[pl.BlockSpec(memory_space=SPACES[c]) for c in out_spaces],
         scratch_shapes=list(scratch),
-        compiler_params=pltpu.CompilerParams(vmem_limit_bytes=24 << 20),
+        compiler_params=pltpu.CompilerParams(vmem_limit_bytes=28 << 20),
     )(*[pltpu.with_memory_space_constraint(x, SPACES[c]) if c in PINNED else x for x, c in zip(ins, spaces)])
 
 
@@ -457,6 +555,9 @@
 
     line = vmem((1, rows), i32)
     weights_scratch = [vmem((8, 32, 128)), vmem((8, 32, 128)), vmem((32, 8, 128))]
+    local_scratch = [vmem((3,) + field), vmem((2, 128)), vmem(field), vmem((2, 128, 384), bf16), vmem((4, 8, 128))]
+    local_scratch = local_scratch + [vmem(field)] * 3
+    tables = [((3, rows), i32)] * 2
 
     payload, rank = call(
         query_kernel,
@@ -470,75 +571,100 @@
 
     ix, iy = lax.axis_index("gx"), lax.axis_index("gy")
     inside = [ix > 0, ix < lax.axis_size("gx") - 1, iy > 0, iy < lax.axis_size("gy") - 1]
-    flags = jnp.where(jnp.stack(inside), 0.5, 1.0).astype(f32)
-    load, inv, table, mask = call(
+    flags = jnp.stack(inside).astype(i32)
+    load, inv, table, mask, low, high = call(
         prepare_kernel,
-        [(field, f32), ((512, 128), f32), ((3, 1, rows), i32), ((4, 8, 128), f32)],
+        [(field, f32), ((512, 128), f32), ((3, rows), i32), ((4, 8, 128), f32)] + tables,
         (flags, owner, rank, point),
-        [vmem(field), vmem((512, 128)), vmem((3, 1, rows), i32), vmem((4, 8, 128)), dma(4)],
+        [vmem(field), vmem((512, 128)), vmem((3, rows), i32), vmem((4, 8, 128))]
+        + [vmem((3, rows), i32)] * 2
+        + [dma(6)],
         "saaa",
-        "aaaa",
-    )
-
-    def local(u):
+        "aaaaaa",
+    )
+
+    def along_y(yl, yr):
+        return passed_around(yl, "gy", -1), passed_around(yr, "gy", 1)
+
+    def along_x(xl, xr, yn, yp, keep):
+        xl, xr = call(edge_kernel, [(face, f32)] * 2, (xl, xr, yn, yp, keep), (), "vvvvv", "vv")
+        return passed_around(xl, "gx", -1), passed_around(xr, "gx", 1)
+
+    def bring(after):
         return call(
-            local_kernel,
-            [(field, f32), ((3, 1, rows), i32), ((4, 8, 128), f32)],
-            (u, flow, nu, load, deep, table, mask),
-            [vmem(field), vmem((3,) + field), vmem((2, 128)), vmem(field), vmem((2, 128, 384), bf16)]
-            + [vmem(field)] * 3
-            + [dma(7)],
-            "aaaaaaa",
-            "vvv",
+            bring_kernel,
+            [((3, rows), i32), ((8, 4, rows), i32)],
+            (after, table, ghosts),
+            [dma(2)],
+            "vaa",
+            "vv",
         )
 
-    def gather_faces(replies, loc, table, mask):
-        v, xl, xr, yl, yr = call(
-            penalty_kernel,
-            [(field, f32)] + [(face, f32)] * 4,
-            (replies, table, mask, loc),
-            (),
-            "vvvv",
-            "vvvvv",
-        )
-        xn = passed_around(xl, "gx", -1)
-        xp = passed_around(xr, "gx", 1)
-        yl, yr = call(edge_kernel, [(face, f32)] * 2, (yl, yr, xn, xp, mask), (), "vvvvv", "vv")
-        yn = passed_around(yl, "gy", -1)
-        yp = passed_around(yr, "gy", 1)
-        return v, xn, xp, yn, yp
-
+    outs = [(field, f32)] + [(face, f32)] * 4 + [((2, 8, 128), f32)]
     u = start
-    loc = local(u)
-    received, loc = lax.optimization_barrier((received, loc))
+    loc, xl, xr, yl, yr, keep = call(
+        local_kernel,
+        outs,
+        (u, flow, nu, load, deep, mask),
+        [vmem(field)] + local_scratch + [dma(6)],
+        "aaaaaa",
+        "vvvvvv",
+    )
+    received, loc, yl, yr, low, high = lax.optimization_barrier((received, loc, yl, yr, low, high))
+    yn, yp = along_y(yl, yr)
+    table_n, table_p = along_y(low, high)
     answers = call(
         first_kernel,
-        [((128, 128), f32)],
+        [((128, 4, 128), f32)],
         (u, received),
         [vmem(field)] + weights_scratch + [dma(1)],
         "av",
-        "v",
+        "p",
     )[0]
+    answers, yn, yp, table_n, table_p = lax.optimization_barrier((answers, yn, yp, table_n, table_p))
+    replies = exchange(answers)
+    xn, xp = along_x(xl, xr, yn, yp, keep)
+    low, high = call(
+        relay_kernel, [((9, rows), i32)] * 2, (flags, table, table_p, table_n), (), "svvv", "vv"
+    )
+    tables_n, tables_p = passed_around(low, "gx", -1), passed_around(high, "gx", 1)
+    ghosts = call(
+        ghost_kernel,
+        [((8, 4, rows), i32)],
+        (tables_p, tables_n, table_p, table_n),
+        [vmem((8, 4, rows), i32), dma(1)],
+        "vvvv",
+        "a",
+    )[0]
+    own, near = bring(keep)
     for blend in (None, (0.75, 0.25)):
+        u, near_u, loc, xl, xr, yl, yr, keep = call(
+            lambda *refs, blend=blend: step_kernel(blend, *refs),
+            [(field, f32)] * 2 + outs,
+            (replies, own, near, loc, xn, xp, yn, yp, start, u, inv, flow, nu, load, deep, mask),
+            [vmem(field)] * 3 + [vmem((512, 128))] + local_scratch + [dma(9)],
+            "vvvvvvvvaaaaaaaa",
+            "avvvvvvv",
+        )
+        yn, yp = along_y(yl, yr)
+        answers = call(
+            answer_kernel,
+            [((128, 4, 128), f32)],
+            (near_u, received),
+            [vmem((128, 128))] + weights_scratch + [dma(1)],
+            "va",
+            "p",
+        )[0]
+        answers, yn, yp = lax.optimization_barrier((answers, yn, yp))
         replies = exchange(answers)
-        parts = gather_faces(replies, *loc)
-        u, answers = call(
-            lambda *refs, blend=blend: step_kernel(blend, *refs),
-            [(field, f32), ((128, 128), f32)],
-            parts + (start, u, inv, received),
-            [vmem(field)] * 3 + [vmem((512, 128)), vmem((128, 128)), vmem(field)] + weights_scratch + [dma(5)],
-            "vvvvvaaaa",
-            "av",
-        )
-        loc = local(u)
-    replies = exchange(answers)
-    parts = gather_faces(replies, *loc)
+        xn, xp = along_x(xl, xr, yn, yp, keep)
+        own, near = bring(keep)
     third = call(
         lambda *refs: last_kernel((1.0 / 3.0, 2.0 / 3.0), *refs),
         [(field, f32)],
-        parts + (start, u, inv),
+        (replies, own, near, loc, xn, xp, yn, yp, start, u, inv),
         [vmem(field)] * 3 + [vmem((512, 128)), dma(3)],
-        "vvvvvaaa",
+        "vvvvvvvvaaa",
         "v",
     )[0]
     return third.reshape(scalar.shape)

time: 130 us -> 119 us (0.915)
  waiting for transfers between devices: 52 us -> 23.3 us
  starting transfers between devices: 28.6 us -> 54.2 us
  blocking collectives: 15.4 us -> 0 us
  Pallas kernels: 32.8 us -> 40.3 us
    ppermute x12 -> x16, starting transfers between devices: 8.02 us -> 25.8 us  [passed_around(): lax.ppermute(value, axis, [(n, (n + steps) % count) for n in range(count)])]
    ppermute x12 -> x16, waiting for transfers between devices: 35.4 us -> 19.8 us  [passed_around(): lax.ppermute(value, axis, [(n, (n + steps) % count) for n in range(count)])]
    all_to_all x1 -> x0, blocking collectives: 15.4 us -> none  [exchange(): lax.all_to_all(x, ('gx', 'gy'), split_axis=0, concat_axis=0, tiled=True)]
    all_to_all x3 -> x4, waiting for transfers between devices: 16.6 us -> 3.51 us  [exchange(): lax.all_to_all(x, ('gx', 'gy'), split_axis=0, concat_axis=0, tiled=True)]
    all_to_all x3 -> x4, starting transfers between devices: 20.6 us -> 28.4 us  [exchange(): lax.all_to_all(x, ('gx', 'gy'), split_axis=0, concat_axis=0, tiled=True)]
    pallas_call x15 -> x17, Pallas kernels: 32.8 us -> 40.3 us  [call(): pl.pallas_call(kernel, out_shape=[SPACES[c](s, d) if c in PINNED else jax...]
  transfers between devices with their start and end apart: 15 -> 20, of which waited for: 15 -> 10; matrix products, arithmetic and copies ran while one was open for 0% -> 0% of each run, Pallas kernels for 9% -> 20%
where the time goes in v3:
time: 119 us; the launch traced here: 118 us
  starting transfers between devices  54.2 us (46%)
  Pallas kernels  40.3 us (34%)
  waiting for transfers between devices  23.3 us (20%)
    pallas_call x17, Pallas kernels, call(): pl.pallas_call(kernel, out_shape=[SPACES[c](s, d) if c in PINNED else jax...  40.3 us
    all_to_all x4, starting transfers between devices, exchange(): lax.all_to_all(x, ('gx', 'gy'), split_axis=0, concat_axis=0, tiled=True)  28.4 us
    ppermute x16, starting transfers between devices, passed_around(): lax.ppermute(value, axis, [(n, (n + steps) % count) for n in range(count)])  25.8 us
    ppermute x16, waiting for transfers between devices, passed_around(): lax.ppermute(value, axis, [(n, (n + steps) % count) for n in range(count)])  19.8 us
    all_to_all x4, waiting for transfers between devices, exchange(): lax.all_to_all(x, ('gx', 'gy'), split_axis=0, concat_axis=0, tiled=True)  3.51 us
  transfers between devices with their start and end apart: 20, of which 10 were waited for; matrix products, arithmetic and copies ran while one was open for 0% of the time, Pallas kernels for 20%

profile of v3, /device:TPU:0, one launch (start us, length us, event | category | flops | bytes accessed | tf_op | source)
XLA Modules:
  0.0 118.3 jit_solution(11425729446296436838)
XLA Ops:
  0.0 2.5 %shard_map.82 = (f32[128,128]{1,0:T(8,128)}, s32[1,2048]{1,0:T(1,128)}) custom-call(s32[1,2048]{1,0:T(1,128)} %bitcast.29, s32[1,2048]{1,0:T(1,128)} %bitcast.35, f32[3,2048]{1,0:T(4,128)} %coords_any.1), custom_call_target="tpu_custom_call" | custom-call | tf_op jit(solution)/shard_map/pallas_call | solution.py:519
  2.5 11.1 %all-to-all-start = ((f32[128,1,128]{2,1,0:T(1,128)}), f32[128,1,128]{2,1,0:T(1,128)S(1)}, u32[]{:S(2)}, u32[]{:S(2)}) async-start(f32[128,1,128]{2,1,0:T(1,128)} %bitcast.4), calls=%async_computation | async-start | bytes 131072 | tf_op jit(solution)/shard_map/all_to_all | solution.py:535
  13.7 0.1 add_convert_fusion.flags_ref
  13.8 2.9 %shard_map.83 = (f32[2,512,128]{2,1,0:T(8,128)}, f32[512,128]{1,0:T(8,128)}, s32[3,2048]{1,0:T(4,128)}, f32[4,8,128]{2,1,0:T(8,128)}, s32[3,2048]{1,0:T(4,128)}, /*index=5*/s32[3,2048]{1,0:T(4,128)}) custom-call(s32[4]{0:T(128)S(1)} %add_convert_fusion.flags_ref, s32[1,2048]{1,0:T(1,128)} %bitcast.30, s32[1,2048]{1,0:T(1,128)} %get-tuple-element.67.rank_any, ...), custom_call_target="tpu_custom_call" | custom-call | tf_op jit(solution)/shard_map/pallas_call | solution.py:519
  16.7 0.0 copy-start.3
  16.7 0.0 copy-start.2
  16.7 0.0 copy-start.1
  16.7 2.8 %shard_map.84 = (f32[2,512,128]{2,1,0:T(8,128)S(1)}, f32[2,64,128]{2,1,0:T(8,128)S(1)}, f32[2,64,128]{2,1,0:T(8,128)S(1)}, f32[2,64,128]{2,1,0:T(8,128)S(1)}, f3...) custom-call(f32[2,512,128]{2,1,0:T(8,128)} %bitcast.20, f32[3,2,512,128]{3,2,1,0:T(8,128)} %bitcast.26, ...), custom_call_target="tpu_custom_call" | custom-call | tf_op jit(solution)/shard_map/pallas_call | solution.py:519
  19.5 3.5 %all-to-all-done = f32[128,1,128]{2,1,0:T(1,128)S(1)} async-done(((f32[128,1,128]{2,1,0:T(1,128)}), f32[128,1,128]{2,1,0:T(1,128)S(1)}, u32[]{:S(2)}, u32[]{:S(2)}) %all-to-all-start) | async-done | bytes 65568 | tf_op jit(solution)/shard_map/all_to_all | solution.py:535
  23.0 0.0 copy-start
  23.0 1.2 collective-permute-start
  24.2 0.9 collective-permute-start.1
  25.0 0.0 copy-done.3
  25.0 2.4 %collective-permute-start.2 = (s32[3,2048]{1,0:T(4,128)S(1)}, s32[3,2048]{1,0:T(4,128)S(1)}, u32[]{:S(2)}, u32[]{:S(2)}) collective-permute-start(s32[3,2048]{1,0:T(4,128)S(1)} %copy-done.3), channel_id=1, source_target_pairs={{0,3},{1,0},{2,1},{3,2},{4,7},{5,4},{6,5},{7,6},{8,11},{9,8},{10,9... | collective-permute-start | bytes 73736 | tf_op jit(solution)/shard_map/ppermute | solution.py:531
  27.4 0.0 copy-done.2
  27.4 0.0 collective-permute-start.3
  27.4 4.6 %shard_map.85 = f32[128,4,128]{2,1,0:T(4,128)} custom-call(f32[2,512,128]{2,1,0:T(8,128)} %bitcast.21, f32[128,128]{1,0:T(8,128)S(1)} %bitcast.17), custom_call_target="tpu_custom_call" | custom-call | tf_op jit(solution)/shard_map/pallas_call | solution.py:519
  32.0 0.0 collective-permute-done.2.above_ref.yn_ref
  32.0 0.5 collective-permute-done.3.below_ref.yp_ref
  32.5 0.0 collective-permute-done.yn_ref.refs_6_
  32.5 0.0 collective-permute-done.1.yp_ref.refs_7_
  32.5 7.6 %all-to-all-start.1 = ((f32[128,4,128]{2,1,0:T(4,128)}), f32[128,4,128]{2,1,0:T(4,128)S(1)}, u32[]{:S(2)}, u32[]{:S(2)}) async-start(f32[128,4,128]{2,1,0:T(4,128)} %shard_map.85), calls=%async_computation.1 | async-start | bytes 524288 | tf_op jit(solution)/shard_map/all_to_all | solution.py:535
  40.2 0.0 copy-done.1
  40.2 0.6 shard_map.86
  40.8 0.1 collective-permute-start.4
  40.9 5.1 %collective-permute-start.5 = (s32[9,2048]{1,0:T(8,128)S(1)}, s32[9,2048]{1,0:T(8,128)S(1)}, u32[]{:S(2)}, u32[]{:S(2)}) collective-permute-start(s32[9,2048]{1,0:T(8,128)S(1)} %get-tuple-element.86), channel_id=1, source_target_pairs={{0,124},{4,0},{8,4},{12,8},{16,12},{20,16},{24,20},{28,24},{32,28}... | collective-permute-start | bytes 221192 | tf_op jit(solution)/shard_map/ppermute | solution.py:531
  45.9 0.4 collective-permute-start.6
  46.3 0.2 collective-permute-start.7
  46.5 3.9 %collective-permute-done.4.xp_ref = s32[9,2048]{1,0:T(8,128)S(1)} collective-permute-done((s32[9,2048]{1,0:T(8,128)S(1)}, s32[9,2048]{1,0:T(8,128)S(1)}, u32[]{:S(2)}, u32[]{:S(2)}) %collective-permute-start.4) | collective-permute-done | bytes 73760 | tf_op jit(solution)/shard_map/ppermute | solution.py:531
  50.4 0.0 collective-permute-done.5.xn_ref
  50.4 0.8 shard_map.87.ghost_any
  51.2 1.0 shard_map.88
  52.2 0.0 collective-permute-done.6.refs_4_
  52.2 1.1 collective-permute-done.7.refs_5_
  53.3 0.0 all-to-all-done.1.refs_0_
  53.3 5.0 %shard_map.90 = (f32[2,512,128]{2,1,0:T(8,128)}, f32[2,512,128]{2,1,0:T(8,128)S(1)}, f32[2,512,128]{2,1,0:T(8,128)S(1)}, f32[2,64,128]{2,1,0:T(8,128)S(1)}, f32[...) custom-call(f32[128,4,128]{2,1,0:T(4,128)S(1)} %all-to-all-done.1.refs_, ...), custom_call_target="tpu_custom_call" | custom-call | tf_op jit(solution)/shard_map/pallas_call | solution.py:519
  58.3 0.0 copy-done
  58.3 2.8 %collective-permute-start.8 = (f32[2,64,128]{2,1,0:T(8,128)S(1)}, f32[2,64,128]{2,1,0:T(8,128)S(1)}, u32[]{:S(2)}, u32[]{:S(2)}) collective-permute-start(f32[2,64,128]{2,1,0:T(8,128)S(1)} %get-tuple-element.98), channel_id=1, source_target_pairs={{0,3},{1,0},{2,1},{3,2},{4,7},{5,4},{6,5},{7,6},{8,11},{9,8},{10,9... | collective-permute-start | bytes 196616 | tf_op jit(solution)/shard_map/ppermute | solution.py:531
  61.1 0.0 collective-permute-start.9
  61.1 4.4 %shard_map.91 = f32[128,4,128]{2,1,0:T(4,128)} custom-call(f32[2,512,128]{2,1,0:T(8,128)S(1)} %get-tuple-element.97.u_ref, f32[128,128]{1,0:T(8,128)} %bitcast.18), custom_call_target="tpu_custom_call" | custom-call | tf_op jit(solution)/shard_map/pallas_call | solution.py:519
  65.5 0.0 collective-permute-done.8.yn_ref.refs_6_
  65.5 1.1 collective-permute-done.9.yp_ref.refs_7_
  66.6 5.0 %all-to-all-start.2 = ((f32[128,4,128]{2,1,0:T(4,128)}), f32[128,4,128]{2,1,0:T(4,128)S(1)}, u32[]{:S(2)}, u32[]{:S(2)}) async-start(f32[128,4,128]{2,1,0:T(4,128)} %shard_map.91), calls=%async_computation.2 | async-start | bytes 524288 | tf_op jit(solution)/shard_map/all_to_all | solution.py:535
  71.6 5.0 %collective-permute-start.10 = (f32[2,64,128]{2,1,0:T(8,128)S(1)}, f32[2,64,128]{2,1,0:T(8,128)S(1)}, u32[]{:S(2)}, u32[]{:S(2)}) collective-permute-start(f32[2,64,128]{2,1,0:T(8,128)S(1)} %get-tuple-element.109), channel_id=1, source_target_pairs={{0,124},{4,0},{8,4},{12,8},{16,12},{20,16},{24,20},{28,24},{32,28}... | collective-permute-start | bytes 196616 | tf_op jit(solution)/shard_map/ppermute | solution.py:531
  76.6 0.0 collective-permute-start.11
  76.6 1.0 shard_map.92
  77.6 0.9 collective-permute-done.10.refs_4_
  78.5 5.1 %collective-permute-done.11.refs_5_ = f32[2,64,128]{2,1,0:T(8,128)S(1)} collective-permute-done((f32[2,64,128]{2,1,0:T(8,128)S(1)}, f32[2,64,128]{2,1,0:T(8,128)S(1)}, u32[]{:S(2)}, u32[]{:S(2)}) %collective-permute-start.11) | collective-permute-done | bytes 65568 | tf_op jit(solution)/shard_map/ppermute | solution.py:531
  83.6 0.0 all-to-all-done.2.refs_0_
  83.6 5.0 %shard_map.94 = (f32[2,512,128]{2,1,0:T(8,128)}, f32[2,512,128]{2,1,0:T(8,128)S(1)}, f32[2,512,128]{2,1,0:T(8,128)S(1)}, f32[2,64,128]{2,1,0:T(8,128)S(1)}, f32[...) custom-call(f32[128,4,128]{2,1,0:T(4,128)S(1)} %all-to-all-done.2.refs_, ...), custom_call_target="tpu_custom_call" | custom-call | tf_op jit(solution)/shard_map/pallas_call | solution.py:519
  88.6 3.0 %collective-permute-start.12 = (f32[2,64,128]{2,1,0:T(8,128)S(1)}, f32[2,64,128]{2,1,0:T(8,128)S(1)}, u32[]{:S(2)}, u32[]{:S(2)}) collective-permute-start(f32[2,64,128]{2,1,0:T(8,128)S(1)} %get-tuple-element.113), channel_id=1, source_target_pairs={{0,3},{1,0},{2,1},{3,2},{4,7},{5,4},{6,5},{7,6},{8,11},{9,8},{10,9... | collective-permute-start | bytes 196616 | tf_op jit(solution)/shard_map/ppermute | solution.py:531
  91.6 0.0 collective-permute-start.13
  91.6 4.4 %shard_map.95 = f32[128,4,128]{2,1,0:T(4,128)} custom-call(f32[2,512,128]{2,1,0:T(8,128)S(1)} %get-tuple-element.112.u_ref, f32[128,128]{1,0:T(8,128)} %bitcast.19), custom_call_target="tpu_custom_call" | custom-call | tf_op jit(solution)/shard_map/pallas_call | solution.py:519
  96.0 0.0 collective-permute-done.12.yn_ref.refs_6_
  96.0 1.1 collective-permute-done.13.yp_ref.refs_7_
  97.1 4.6 %all-to-all-start.3 = ((f32[128,4,128]{2,1,0:T(4,128)}), f32[128,4,128]{2,1,0:T(4,128)S(1)}, u32[]{:S(2)}, u32[]{:S(2)}) async-start(f32[128,4,128]{2,1,0:T(4,128)} %shard_map.95), calls=%async_computation.3 | async-start | bytes 524288 | tf_op jit(solution)/shard_map/all_to_all | solution.py:535
  101.7 5.0 %collective-permute-start.14 = (f32[2,64,128]{2,1,0:T(8,128)S(1)}, f32[2,64,128]{2,1,0:T(8,128)S(1)}, u32[]{:S(2)}, u32[]{:S(2)}) collective-permute-start(f32[2,64,128]{2,1,0:T(8,128)S(1)} %get-tuple-element.124), channel_id=1, source_target_pairs={{0,124},{4,0},{8,4},{12,8},{16,12},{20,16},{24,20},{28,24},{32,28}... | collective-permute-start | bytes 196616 | tf_op jit(solution)/shard_map/ppermute | solution.py:531
  106.7 0.0 collective-permute-start.15
  106.7 1.0 shard_map.96
  107.7 0.9 collective-permute-done.14.refs_4_
  108.6 5.1 %collective-permute-done.15.refs_5_ = f32[2,64,128]{2,1,0:T(8,128)S(1)} collective-permute-done((f32[2,64,128]{2,1,0:T(8,128)S(1)}, f32[2,64,128]{2,1,0:T(8,128)S(1)}, u32[]{:S(2)}, u32[]{:S(2)}) %collective-permute-start.15) | collective-permute-done | bytes 65568 | tf_op jit(solution)/shard_map/ppermute | solution.py:531
  113.7 0.0 all-to-all-done.3.refs_0_
  113.7 4.4 %shard_map.98 = f32[2,512,128]{2,1,0:T(8,128)} custom-call(f32[128,4,128]{2,1,0:T(4,128)S(1)} %all-to-all-done.3.refs_0_, s32[3,2048]{1,0:T(4,128)S(1)} %get-tuple-element.117.refs_1_, s32[8,4,2048]{2,1,0:T(4,128)S(1)} %get-tuple-element.118.refs_2_, f32[2,512,128]{2,1,0:T(8,128)S(1)} %get-tuple-element.119.refs_3_, ...), custom_call_target="tpu_custom_call" | custom-call | tf_op jit(solution)/shard_map/pallas_call | solution.py:519
  (3 shorter events, 0.0 us)
Async XLA Ops:
  2.5 20.5 %all-to-all-start = ((f32[128,1,128]{2,1,0:T(1,128)}), f32[128,1,128]{2,1,0:T(1,128)S(1)}, u32[]{:S(2)}, u32[]{:S(2)}) async-start(f32[128,1,128]{2,1,0:T(1,128)} %bitcast.4), calls=%async_computation | async-start | bytes 131072 | tf_op jit(solution)/shard_map/all_to_all | solution.py:535
  16.7 8.3 %copy-start.3 = (s32[3,2048]{1,0:T(4,128)S(1)}, s32[3,2048]{1,0:T(4,128)}, u32[]{:S(2)}) copy-start(s32[3,2048]{1,0:T(4,128)} %get-tuple-element.78) | copy-start | bytes 73732
  16.7 10.7 %copy-start.2 = (s32[3,2048]{1,0:T(4,128)S(1)}, s32[3,2048]{1,0:T(4,128)}, u32[]{:S(2)}) copy-start(s32[3,2048]{1,0:T(4,128)} %get-tuple-element.79) | copy-start | bytes 73732
  16.7 23.5 %copy-start.1 = (s32[3,2048]{1,0:T(4,128)S(1)}, s32[3,2048]{1,0:T(4,128)}, u32[]{:S(2)}) copy-start(s32[3,2048]{1,0:T(4,128)} %get-tuple-element.82.own_ref.table_any) | copy-start | bytes 73732
  23.0 35.3 %copy-start = (f32[128,1,128]{2,1,0:T(1,128)}, f32[128,1,128]{2,1,0:T(1,128)S(1)}, u32[]{:S(2)}) copy-start(f32[128,1,128]{2,1,0:T(1,128)S(1)} %all-to-all-done) | copy-start | bytes 196612
  23.0 9.5 %collective-permute-start = (f32[2,64,128]{2,1,0:T(8,128)S(1)}, f32[2,64,128]{2,1,0:T(8,128)S(1)}, u32[]{:S(2)}, u32[]{:S(2)}) collective-permute-start(f32[2,64,128]{2,1,0:T(8,128)S(1)} %get-tuple-element.76), channel_id=1, source_target_pairs={{0,3},{1,0},{2,1},{3,2},{4,7},{5,4},{6,5},{7,6},{8,11},{9,8},{10,9... | collective-permute-start | bytes 196616 | tf_op jit(solution)/shard_map/ppermute | solution.py:531
  24.2 8.4 %collective-permute-start.1 = (f32[2,64,128]{2,1,0:T(8,128)S(1)}, f32[2,64,128]{2,1,0:T(8,128)S(1)}, u32[]{:S(2)}, u32[]{:S(2)}) collective-permute-start(f32[2,64,128]{2,1,0:T(8,128)S(1)} %get-tuple-element.77), channel_id=1, source_target_pairs={{0,1},{1,2},{2,3},{3,0},{4,5},{5,6},{6,7},{7,4},{8,9},{9,10},{10,1... | collective-permute-start | bytes 196616 | tf_op jit(solution)/shard_map/ppermute | solution.py:531
  25.0 7.0 %collective-permute-start.2 = (s32[3,2048]{1,0:T(4,128)S(1)}, s32[3,2048]{1,0:T(4,128)S(1)}, u32[]{:S(2)}, u32[]{:S(2)}) collective-permute-start(s32[3,2048]{1,0:T(4,128)S(1)} %copy-done.3), channel_id=1, source_target_pairs={{0,3},{1,0},{2,1},{3,2},{4,7},{5,4},{6,5},{7,6},{8,11},{9,8},{10,9... | collective-permute-start | bytes 73736 | tf_op jit(solution)/shard_map/ppermute | solution.py:531
  27.4 5.1 %collective-permute-start.3 = (s32[3,2048]{1,0:T(4,128)S(1)}, s32[3,2048]{1,0:T(4,128)S(1)}, u32[]{:S(2)}, u32[]{:S(2)}) collective-permute-start(s32[3,2048]{1,0:T(4,128)S(1)} %copy-done.2), channel_id=1, source_target_pairs={{0,1},{1,2},{2,3},{3,0},{4,5},{5,6},{6,7},{7,4},{8,9},{9,10},{10,1... | collective-permute-start | bytes 73736 | tf_op jit(solution)/shard_map/ppermute | solution.py:531
  32.5 20.8 %all-to-all-start.1 = ((f32[128,4,128]{2,1,0:T(4,128)}), f32[128,4,128]{2,1,0:T(4,128)S(1)}, u32[]{:S(2)}, u32[]{:S(2)}) async-start(f32[128,4,128]{2,1,0:T(4,128)} %shard_map.85), calls=%async_computation.1 | async-start | bytes 524288 | tf_op jit(solution)/shard_map/all_to_all | solution.py:535
  40.8 9.7 %collective-permute-start.4 = (s32[9,2048]{1,0:T(8,128)S(1)}, s32[9,2048]{1,0:T(8,128)S(1)}, u32[]{:S(2)}, u32[]{:S(2)}) collective-permute-start(s32[9,2048]{1,0:T(8,128)S(1)} %get-tuple-element.85), channel_id=1, source_target_pairs={{0,4},{4,8},{8,12},{12,16},{16,20},{20,24},{24,28},{28,32},{32,36}... | collective-permute-start | bytes 221192 | tf_op jit(solution)/shard_map/ppermute | solution.py:531
  40.9 9.6 %collective-permute-start.5 = (s32[9,2048]{1,0:T(8,128)S(1)}, s32[9,2048]{1,0:T(8,128)S(1)}, u32[]{:S(2)}, u32[]{:S(2)}) collective-permute-start(s32[9,2048]{1,0:T(8,128)S(1)} %get-tuple-element.86), channel_id=1, source_target_pairs={{0,124},{4,0},{8,4},{12,8},{16,12},{20,16},{24,20},{28,24},{32,28}... | collective-permute-start | bytes 221192 | tf_op jit(solution)/shard_map/ppermute | solution.py:531
  45.9 6.3 %collective-permute-start.6 = (f32[2,64,128]{2,1,0:T(8,128)S(1)}, f32[2,64,128]{2,1,0:T(8,128)S(1)}, u32[]{:S(2)}, u32[]{:S(2)}) collective-permute-start(f32[2,64,128]{2,1,0:T(8,128)S(1)} %get-tuple-element.94), channel_id=1, source_target_pairs={{0,124},{4,0},{8,4},{12,8},{16,12},{20,16},{24,20},{28,24},{32,28}... | collective-permute-start | bytes 196616 | tf_op jit(solution)/shard_map/ppermute | solution.py:531
  46.3 7.0 %collective-permute-start.7 = (f32[2,64,128]{2,1,0:T(8,128)S(1)}, f32[2,64,128]{2,1,0:T(8,128)S(1)}, u32[]{:S(2)}, u32[]{:S(2)}) collective-permute-start(f32[2,64,128]{2,1,0:T(8,128)S(1)} %get-tuple-element.95), channel_id=1, source_target_pairs={{0,4},{4,8},{8,12},{12,16},{16,20},{20,24},{24,28},{28,32},{32,36}... | collective-permute-start | bytes 196616 | tf_op jit(solution)/shard_map/ppermute | solution.py:531
  58.3 7.2 %collective-permute-start.8 = (f32[2,64,128]{2,1,0:T(8,128)S(1)}, f32[2,64,128]{2,1,0:T(8,128)S(1)}, u32[]{:S(2)}, u32[]{:S(2)}) collective-permute-start(f32[2,64,128]{2,1,0:T(8,128)S(1)} %get-tuple-element.98), channel_id=1, source_target_pairs={{0,3},{1,0},{2,1},{3,2},{4,7},{5,4},{6,5},{7,6},{8,11},{9,8},{10,9... | collective-permute-start | bytes 196616 | tf_op jit(solution)/shard_map/ppermute | solution.py:531
  61.1 5.5 %collective-permute-start.9 = (f32[2,64,128]{2,1,0:T(8,128)S(1)}, f32[2,64,128]{2,1,0:T(8,128)S(1)}, u32[]{:S(2)}, u32[]{:S(2)}) collective-permute-start(f32[2,64,128]{2,1,0:T(8,128)S(1)} %get-tuple-element.99), channel_id=1, source_target_pairs={{0,1},{1,2},{2,3},{3,0},{4,5},{5,6},{6,7},{7,4},{8,9},{9,10},{10,1... | collective-permute-start | bytes 196616 | tf_op jit(solution)/shard_map/ppermute | solution.py:531
  66.6 17.0 %all-to-all-start.2 = ((f32[128,4,128]{2,1,0:T(4,128)}), f32[128,4,128]{2,1,0:T(4,128)S(1)}, u32[]{:S(2)}, u32[]{:S(2)}) async-start(f32[128,4,128]{2,1,0:T(4,128)} %shard_map.91), calls=%async_computation.2 | async-start | bytes 524288 | tf_op jit(solution)/shard_map/all_to_all | solution.py:535
  71.6 6.9 %collective-permute-start.10 = (f32[2,64,128]{2,1,0:T(8,128)S(1)}, f32[2,64,128]{2,1,0:T(8,128)S(1)}, u32[]{:S(2)}, u32[]{:S(2)}) collective-permute-start(f32[2,64,128]{2,1,0:T(8,128)S(1)} %get-tuple-element.109), channel_id=1, source_target_pairs={{0,124},{4,0},{8,4},{12,8},{16,12},{20,16},{24,20},{28,24},{32,28}... | collective-permute-start | bytes 196616 | tf_op jit(solution)/shard_map/ppermute | solution.py:531
  76.6 7.0 %collective-permute-start.11 = (f32[2,64,128]{2,1,0:T(8,128)S(1)}, f32[2,64,128]{2,1,0:T(8,128)S(1)}, u32[]{:S(2)}, u32[]{:S(2)}) collective-permute-start(f32[2,64,128]{2,1,0:T(8,128)S(1)} %get-tuple-element.110), channel_id=1, source_target_pairs={{0,4},{4,8},{8,12},{12,16},{16,20},{20,24},{24,28},{28,32},{32,36}... | collective-permute-start | bytes 196616 | tf_op jit(solution)/shard_map/ppermute | solution.py:531
  88.6 7.4 %collective-permute-start.12 = (f32[2,64,128]{2,1,0:T(8,128)S(1)}, f32[2,64,128]{2,1,0:T(8,128)S(1)}, u32[]{:S(2)}, u32[]{:S(2)}) collective-permute-start(f32[2,64,128]{2,1,0:T(8,128)S(1)} %get-tuple-element.113), channel_id=1, source_target_pairs={{0,3},{1,0},{2,1},{3,2},{4,7},{5,4},{6,5},{7,6},{8,11},{9,8},{10,9... | collective-permute-start | bytes 196616 | tf_op jit(solution)/shard_map/ppermute | solution.py:531
  91.6 5.5 %collective-permute-start.13 = (f32[2,64,128]{2,1,0:T(8,128)S(1)}, f32[2,64,128]{2,1,0:T(8,128)S(1)}, u32[]{:S(2)}, u32[]{:S(2)}) collective-permute-start(f32[2,64,128]{2,1,0:T(8,128)S(1)} %get-tuple-element.114), channel_id=1, source_target_pairs={{0,1},{1,2},{2,3},{3,0},{4,5},{5,6},{6,7},{7,4},{8,9},{9,10},{10,1... | collective-permute-start | bytes 196616 | tf_op jit(solution)/shard_map/ppermute | solution.py:531
  97.1 16.6 %all-to-all-start.3 = ((f32[128,4,128]{2,1,0:T(4,128)}), f32[128,4,128]{2,1,0:T(4,128)S(1)}, u32[]{:S(2)}, u32[]{:S(2)}) async-start(f32[128,4,128]{2,1,0:T(4,128)} %shard_map.95), calls=%async_computation.3 | async-start | bytes 524288 | tf_op jit(solution)/shard_map/all_to_all | solution.py:535
  101.7 6.9 %collective-permute-start.14 = (f32[2,64,128]{2,1,0:T(8,128)S(1)}, f32[2,64,128]{2,1,0:T(8,128)S(1)}, u32[]{:S(2)}, u32[]{:S(2)}) collective-permute-start(f32[2,64,128]{2,1,0:T(8,128)S(1)} %get-tuple-element.124), channel_id=1, source_target_pairs={{0,124},{4,0},{8,4},{12,8},{16,12},{20,16},{24,20},{28,24},{32,28}... | collective-permute-start | bytes 196616 | tf_op jit(solution)/shard_map/ppermute | solution.py:531
  106.7 7.0 %collective-permute-start.15 = (f32[2,64,128]{2,1,0:T(8,128)S(1)}, f32[2,64,128]{2,1,0:T(8,128)S(1)}, u32[]{:S(2)}, u32[]{:S(2)}) collective-permute-start(f32[2,64,128]{2,1,0:T(8,128)S(1)} %get-tuple-element.125), channel_id=1, source_target_pairs={{0,4},{4,8},{8,12},{12,16},{16,20},{20,24},{24,28},{28,32},{32,36}... | collective-permute-start | bytes 196616 | tf_op jit(solution)/shard_map/ppermute | solution.py:531

commit v4 on v3

--- a/solution.py
+++ b/solution.py
@@ -162,7 +162,7 @@
     copies = start_copies(
         [(owner_any, table_ref.at[0:1]), (rank_any, table_ref.at[1:2]), (point_any, table_ref.at[2:3])], sems
     )
-    for n in range(4):
+    for n in range(5):
         mask_ref[n] = jnp.full((8, 128), flags_ref[n], i32).astype(f32)
     for copy in copies:
         copy.wait()
@@ -201,35 +201,41 @@
 
 
 def relay_kernel(flags_ref, own_ref, below_ref, above_ref, low_ref, high_ref):
-    for n, ref in ((0, low_ref), (1, high_ref)):
+    for there, ref in ((flags_ref[0], low_ref), (flags_ref[1], high_ref)):
         for t, src in enumerate((own_ref, below_ref, above_ref)):
             ref[3 * t : 3 * t + 2, :] = src[0:2, :]
-            ref[3 * t + 2 : 3 * t + 3, :] = (src[2:3, :] + 1) * flags_ref[n] - 1
+            ref[3 * t + 2 : 3 * t + 3, :] = (src[2:3, :] + 1) * there - 1
 
 
 GHOSTS = [(-1, 0), (1, 0), (0, -1), (0, 1), (-1, -1), (-1, 1), (1, -1), (1, 1)]
 
 
-def ghost_kernel(xp_ref, xn_ref, yp_ref, yn_ref, out_any, out_ref, sems):
-    for n, (dx, dy) in enumerate(GHOSTS):
-        if dx == 0:
-            src, base = (yp_ref, 0) if dy < 0 else (yn_ref, 0)
-        else:
-            src, base = (xp_ref if dx < 0 else xn_ref), {0: 0, -1: 3, 1: 6}[dy]
+def ghost_kernel(xp_ref, xn_ref, yp_ref, yn_ref, out_ref, out_any, sems):
+    def write(n, src, base, side_x, side_y):
         point = src[base + 2 : base + 3, :]
         q = lax.shift_right_arithmetic(point, 7)
         i = lax.shift_right_arithmetic(q, 6)
         j = lax.bitwise_and(lax.shift_right_arithmetic(q, 3), 7)
         k = lax.bitwise_and(q, 7)
         good = point >= 0
-        if dx:
-            good = good & (i == (7 if dx < 0 else 0))
-        if dy:
-            good = good & (j == (7 if dy < 0 else 0))
-        row = k if dx and dy else (j * 8 + k if dx else i * 8 + k)
+        row = k
+        if side_x is not None:
+            good = good & (i == side_x)
+        else:
+            row = i * 8 + k
+        if side_y is not None:
+            good = good & (j == side_y)
+        else:
+            row = j * 8 + k
         out_ref[n, 0:2, :] = src[base : base + 2, :]
         out_ref[n, 2:3, :] = jnp.where(good, row, -1)
         out_ref[n, 3:4, :] = lax.bitwise_and(point, 127)
+
+    write(2, yp_ref, 0, None, 7)
+    write(3, yn_ref, 0, None, 0)
+    for src, below in ((xp_ref, 1), (xn_ref, 0)):
+        for base, side_y, low, high in ((0, None, 0, 1), (3, 7, 4, 6), (6, 0, 5, 7)):
+            write(below * low + (1 - below) * high, src, base, 7 * below, side_y)
     copies = start_copies([(out_ref, out_any)], sems)
     copies[0].wait()
 
@@ -288,6 +294,21 @@
 
 
 def send_faces(loc_ref, mask_ref, xl_ref, xr_ref, yl_ref, yr_ref, keep_ref):
+    odd = mask_ref[4] > 0.5
+    for m in range(2):
+        for n in range(8):
+            rows = slice(n * 8, n * 8 + 8)
+            low = loc_ref[m, rows, :] * mask_ref[0]
+            high = loc_ref[m, 448 + n * 8 : 456 + n * 8, :] * mask_ref[1]
+            xl_ref[m, rows, :] = jnp.where(odd, low, high)
+            xr_ref[m, rows, :] = jnp.where(odd, high, low)
+            yl_ref[m, rows, :] = loc_ref[m, n * 64 : n * 64 + 8, :]
+            yr_ref[m, rows, :] = loc_ref[m, n * 64 + 56 : n * 64 + 64, :]
+    keep_ref[0:2] = mask_ref[2:4]
+    keep_ref[2] = mask_ref[4]
+
+
+def send_first_faces(loc_ref, mask_ref, xl_ref, xr_ref, yl_ref, yr_ref, keep_ref):
     for m in range(2):
         for n in range(8):
             rows = slice(n * 8, n * 8 + 8)
@@ -295,7 +316,21 @@
             xr_ref[m, rows, :] = loc_ref[m, 448 + n * 8 : 456 + n * 8, :]
             yl_ref[m, rows, :] = loc_ref[m, n * 64 : n * 64 + 8, :] * mask_ref[2]
             yr_ref[m, rows, :] = loc_ref[m, n * 64 + 56 : n * 64 + 64, :] * mask_ref[3]
-    keep_ref[...] = mask_ref[0:2]
+    keep_ref[0:2] = mask_ref[0:2]
+    keep_ref[2] = mask_ref[4]
+
+
+def first_edge_kernel(xl_ref, xr_ref, yn_ref, yp_ref, keep_ref, xl_out, xr_out):
+    for m in range(2):
+        for src, dst, i in ((xl_ref, xl_out, 0), (xr_ref, xr_out, 7)):
+            mask = keep_ref[0 if i == 0 else 1]
+            for j in range(8):
+                val = src[m, j * 8 : j * 8 + 8, :]
+                if j == 0:
+                    val = val + yp_ref[m, i * 8 : i * 8 + 8, :]
+                if j == 7:
+                    val = val + yn_ref[m, i * 8 : i * 8 + 8, :]
+                dst[m, j * 8 : j * 8 + 8, :] = val * mask
 
 
 def local_kernel(u_any, vel_any, nu_any, load_any, deep_any, mask_any, loc_ref, xl_ref, xr_ref, yl_ref, yr_ref, keep_ref,
@@ -308,14 +343,12 @@
     copies[0].wait()
     copies[1].wait()
     local_rates(u_ref, vel_ref, nu_ref, load_ref, deep_ref, loc_ref, ax_ref, ay_ref, fz_ref, copies[2:])
-    send_faces(loc_ref, mask_ref, xl_ref, xr_ref, yl_ref, yr_ref, keep_ref)
-
-
-def interpolate(u, received_ref, ans_ref, wx_ref, wy_ref, wz_ref, copies):
+    send_first_faces(loc_ref, mask_ref, xl_ref, xr_ref, yl_ref, yr_ref, keep_ref)
+
+
+def interpolate(u, received_ref, ans_ref, wx_ref, wy_ref, wz_ref):
     parts = [split_two(v) for v in u]
     cat = jnp.concatenate([parts[0][0], parts[1][0], parts[0][1], parts[1][1]], axis=1)
-    for copy in copies:
-        copy.wait()
     turned = received_ref[...].T
     for v, ref in enumerate((wx_ref, wy_ref, wz_ref)):
         x = turned[v * 32 : v * 32 + 32, :]
@@ -366,48 +399,59 @@
     ans_ref[:, 3, :] = jnp.zeros((128, 128), f32)
 
 
-def answer_kernel(u_ref, received_any, ans_ref, received_ref, wx_ref, wy_ref, wz_ref, sems):
-    copies = start_copies([(received_any, received_ref)], sems)
-    interpolate([u_ref[0], u_ref[1]], received_ref, ans_ref, wx_ref, wy_ref, wz_ref, copies)
+def answer_kernel(u_ref, received_ref, ans_ref, wx_ref, wy_ref, wz_ref):
+    interpolate([u_ref[0], u_ref[1]], received_ref, ans_ref, wx_ref, wy_ref, wz_ref)
 
 
 def first_kernel(u_any, received_ref, ans_ref, u_ref, wx_ref, wy_ref, wz_ref, sems):
     copies = start_copies([(u_any, u_ref)], sems)
     copies[0].wait()
-    interpolate([u_ref[0], u_ref[1]], received_ref, ans_ref, wx_ref, wy_ref, wz_ref, [])
-
-
-def edge_kernel(xl_ref, xr_ref, yn_ref, yp_ref, keep_ref, xl_out, xr_out):
-    for m in range(2):
-        for src, dst, i in ((xl_ref, xl_out, 0), (xr_ref, xr_out, 7)):
-            mask = keep_ref[0 if i == 0 else 1]
-            for j in range(8):
-                val = src[m, j * 8 : j * 8 + 8, :]
-                if j == 0:
-                    val = val + yp_ref[m, i * 8 : i * 8 + 8, :]
-                if j == 7:
-                    val = val + yn_ref[m, i * 8 : i * 8 + 8, :]
-                dst[m, j * 8 : j * 8 + 8, :] = val * mask
-
-
-def bring_kernel(after_ref, table_any, ghost_any, table_ref, ghost_ref, sems):
-    copies = start_copies([(table_any, table_ref), (ghost_any, ghost_ref)], sems)
+    interpolate([u_ref[0], u_ref[1]], received_ref, ans_ref, wx_ref, wy_ref, wz_ref)
+
+
+def edge_kernel(yl_ref, yr_ref, pair_ref, cross_ref, keep_ref, yl_out, yr_out):
+    odd = keep_ref[2] > 0.5
+    for m in range(2):
+        for src, dst, j in ((yl_ref, yl_out, 0), (yr_ref, yr_out, 7)):
+            mask = keep_ref[0 if j == 0 else 1]
+            pair = pair_ref[m, j * 8 : j * 8 + 8, :]
+            cross = cross_ref[m, j * 8 : j * 8 + 8, :]
+            for i in range(8):
+                val = src[m, i * 8 : i * 8 + 8, :]
+                if i == 0:
+                    val = val + jnp.where(odd, pair, cross)
+                if i == 7:
+                    val = val + jnp.where(odd, cross, pair)
+                dst[m, i * 8 : i * 8 + 8, :] = val * mask
+
+
+def bring_kernel(after_ref, table_any, ghost_any, received_any, table_ref, ghost_ref, received_ref, sems):
+    copies = start_copies([(table_any, table_ref), (ghost_any, ghost_ref), (received_any, received_ref)], sems)
     for copy in copies:
         copy.wait()
 
 
+def first_bring_kernel(after_ref, table_any, received_any, table_ref, received_ref, sems):
+    copies = start_copies([(table_any, table_ref), (received_any, received_ref)], sems)
+    for copy in copies:
+        copy.wait()
+
+
 def with_faces(parts, m, ij):
-    loc_ref, xn_ref, xp_ref, yn_ref, yp_ref = parts
+    loc_ref, pair_ref, cross_ref, yn_ref, yp_ref, keep_ref, ring = parts
     i, j = ij // 8, ij % 8
     val = loc_ref[m, ij * 8 : ij * 8 + 8, :]
     if j == 0:
         val = val + yp_ref[m, i * 8 : i * 8 + 8, :]
     elif j == 7:
         val = val + yn_ref[m, i * 8 : i * 8 + 8, :]
-    if i == 0:
-        val = val + xp_ref[m, j * 8 : j * 8 + 8, :]
-    elif i == 7:
-        val = val + xn_ref[m, j * 8 : j * 8 + 8, :]
+    if ring and i in (0, 7):
+        val = val + (cross_ref if i == 0 else pair_ref)[m, j * 8 : j * 8 + 8, :]
+    elif i in (0, 7):
+        pair = pair_ref[m, j * 8 : j * 8 + 8, :]
+        cross = cross_ref[m, j * 8 : j * 8 + 8, :]
+        odd = keep_ref[2] > 0.5
+        val = val + (jnp.where(odd, pair, cross) if i == 0 else jnp.where(odd, cross, pair))
     return val
 
 
@@ -420,8 +464,13 @@
         pick = lax.broadcasted_iota(i32, (32, 128), 0) == rank[:, sl]
         parts.append(jnp.sum(jnp.where(pick, got, 0.0), axis=0, keepdims=True))
     g = jnp.concatenate(parts, axis=1)
-    ghi = g.astype(bf16).astype(f32)
-    return ghi, g - ghi
+    return split_two(g)
+
+
+def placed(row, count, hi, lo):
+    at = lax.broadcasted_iota(jnp.int16, (count, row.shape[-1]), 0) == row.astype(jnp.int16)
+    zero = jnp.zeros((), bf16)
+    return jnp.concatenate([jnp.where(at, hi, zero), jnp.where(at, lo, zero)], axis=0)
 
 
 def add_replies(replies_ref, table_ref, ghost_ref, parts, work_ref):
@@ -439,19 +488,14 @@
         for n, where in enumerate(GHOSTS):
             ghi, glo = picked(blocks[n + 1], ghost_ref[n, 0:1, sl], ghost_ref[n, 1:2, sl])
             size = 8 if where[0] and where[1] else 64
-            at = lax.broadcasted_iota(i32, (size, half), 0) == ghost_ref[n, 2:3, sl]
-            lhs = jnp.concatenate([jnp.where(at, ghi, 0.0), jnp.where(at, glo, 0.0)], axis=0).astype(bf16)
+            lhs = placed(ghost_ref[n, 2:3, sl], size, ghi, glo)
             both = dot_nt(lhs, one_hot_rows(ghost_ref[n, 3:4, sl], 128))
             faces[where] = both[0:size, :] + both[size : 2 * size, :]
         ghi, glo = picked(blocks[0], table_ref[0:1, sl], table_ref[1:2, sl])
         point = table_ref[2:3, sl]
         q = lax.shift_right_logical(point, 7)
         e = lax.bitwise_and(point, 127)
-        at = lax.broadcasted_iota(i32, (128, half), 0) == e
-        rhs = jnp.concatenate(
-            [jnp.where(at, ghi, 0.0).astype(bf16), jnp.where(at, glo, 0.0).astype(bf16)], axis=0
-        )
-        both = dot_nt(one_hot_rows(q, 512), rhs)
+        both = dot_nt(one_hot_rows(q, 512), placed(e, 128, ghi, glo))
         summed = both[:, 0:128] + both[:, 128:256]
         for ij in range(64):
             rows = slice(ij * 8, ij * 8 + 8)
@@ -482,7 +526,7 @@
         new_ref[m] = new
 
 
-def step_kernel(blend, replies_ref, table_ref, ghost_ref, old_ref, xn_ref, xp_ref, yn_ref, yp_ref, start_any, u_any, inv_any, vel_any, nu_any, load_any,
+def step_kernel(blend, replies_ref, table_ref, ghost_ref, old_ref, xn_ref, xp_ref, yn_ref, yp_ref, kept_ref, start_any, u_any, inv_any, vel_any, nu_any, load_any,
                 deep_any, mask_any, new_any, new_ref, loc_ref, xl_ref, xr_ref, yl_ref, yr_ref, keep_ref,
                 work_ref, start_ref, u_ref, inv_ref, vel_ref, nu_ref, load_ref, deep_ref, mask_ref,
                 ax_ref, ay_ref, fz_ref, sems):
@@ -491,7 +535,7 @@
          (vel_any, vel_ref), (load_any, load_ref), (mask_any, mask_ref)],
         sems,
     )
-    add_replies(replies_ref, table_ref, ghost_ref, (old_ref, xn_ref, xp_ref, yn_ref, yp_ref), work_ref)
+    add_replies(replies_ref, table_ref, ghost_ref, (old_ref, xn_ref, xp_ref, yn_ref, yp_ref, kept_ref, blend is None), work_ref)
     for copy in copies[:4]:
         copy.wait()
     advance(blend, start_ref, u_ref, inv_ref, work_ref, new_ref)
@@ -502,10 +546,10 @@
     out.wait()
 
 
-def last_kernel(blend, replies_ref, table_ref, ghost_ref, old_ref, xn_ref, xp_ref, yn_ref, yp_ref, start_any, u_any, inv_any, new_ref,
+def last_kernel(blend, replies_ref, table_ref, ghost_ref, old_ref, xn_ref, xp_ref, yn_ref, yp_ref, kept_ref, start_any, u_any, inv_any, new_ref,
                 work_ref, start_ref, u_ref, inv_ref, sems):
     copies = start_copies([(u_any, u_ref), (inv_any, inv_ref), (start_any, start_ref)], sems)
-    add_replies(replies_ref, table_ref, ghost_ref, (old_ref, xn_ref, xp_ref, yn_ref, yp_ref), work_ref)
+    add_replies(replies_ref, table_ref, ghost_ref, (old_ref, xn_ref, xp_ref, yn_ref, yp_ref, kept_ref, blend is None), work_ref)
     for copy in copies:
         copy.wait()
     advance(blend, start_ref, u_ref, inv_ref, work_ref, new_ref)
@@ -529,6 +573,15 @@
 def passed_around(value, axis, steps):
     count = lax.axis_size(axis)
     return lax.ppermute(value, axis, [(n, (n + steps) % count) for n in range(count)])
+
+
+def swapped(pair, cross):
+    count = lax.axis_size("gx")
+    across = [min(max(((n + 1) ^ 1) - 1, 0), count - 1) for n in range(count)]
+    return (
+        lax.ppermute(pair, "gx", [(n, n ^ 1) for n in range(count)]),
+        lax.ppermute(cross, "gx", [(n, across[n]) for n in range(count)]),
+    )
 
 
 def exchange(x):
@@ -555,7 +608,7 @@
 
     line = vmem((1, rows), i32)
     weights_scratch = [vmem((8, 32, 128)), vmem((8, 32, 128)), vmem((32, 8, 128))]
-    local_scratch = [vmem((3,) + field), vmem((2, 128)), vmem(field), vmem((2, 128, 384), bf16), vmem((4, 8, 128))]
+    local_scratch = [vmem((3,) + field), vmem((2, 128)), vmem(field), vmem((2, 128, 384), bf16), vmem((5, 8, 128))]
     local_scratch = local_scratch + [vmem(field)] * 3
     tables = [((3, rows), i32)] * 2
 
@@ -571,12 +624,12 @@
 
     ix, iy = lax.axis_index("gx"), lax.axis_index("gy")
     inside = [ix > 0, ix < lax.axis_size("gx") - 1, iy > 0, iy < lax.axis_size("gy") - 1]
-    flags = jnp.stack(inside).astype(i32)
+    flags = jnp.stack(inside + [ix % 2 == 1]).astype(i32)
     load, inv, table, mask, low, high = call(
         prepare_kernel,
-        [(field, f32), ((512, 128), f32), ((3, rows), i32), ((4, 8, 128), f32)] + tables,
+        [(field, f32), ((512, 128), f32), ((3, rows), i32), ((5, 8, 128), f32)] + tables,
         (flags, owner, rank, point),
-        [vmem(field), vmem((512, 128)), vmem((3, rows), i32), vmem((4, 8, 128))]
+        [vmem(field), vmem((512, 128)), vmem((3, rows), i32), vmem((5, 8, 128))]
         + [vmem((3, rows), i32)] * 2
         + [dma(6)],
         "saaa",
@@ -586,21 +639,20 @@
     def along_y(yl, yr):
         return passed_around(yl, "gy", -1), passed_around(yr, "gy", 1)
 
-    def along_x(xl, xr, yn, yp, keep):
-        xl, xr = call(edge_kernel, [(face, f32)] * 2, (xl, xr, yn, yp, keep), (), "vvvvv", "vv")
-        return passed_around(xl, "gx", -1), passed_around(xr, "gx", 1)
+    def faces_along_y(yl, yr, xn, xp, keep):
+        return along_y(*call(edge_kernel, [(face, f32)] * 2, (yl, yr, xn, xp, keep), (), "vvvvv", "vv"))
 
     def bring(after):
         return call(
             bring_kernel,
-            [((3, rows), i32), ((8, 4, rows), i32)],
-            (after, table, ghosts),
-            [dma(2)],
-            "vaa",
-            "vv",
+            [((3, rows), i32), ((8, 4, rows), i32), ((128, 128), f32)],
+            (after, table, ghosts, received),
+            [dma(3)],
+            "vaaa",
+            "vvv",
         )
 
-    outs = [(field, f32)] + [(face, f32)] * 4 + [((2, 8, 128), f32)]
+    outs = [(field, f32)] + [(face, f32)] * 4 + [((3, 8, 128), f32)]
     u = start
     loc, xl, xr, yl, yr, keep = call(
         local_kernel,
@@ -623,48 +675,56 @@
     )[0]
     answers, yn, yp, table_n, table_p = lax.optimization_barrier((answers, yn, yp, table_n, table_p))
     replies = exchange(answers)
-    xn, xp = along_x(xl, xr, yn, yp, keep)
+    xl, xr = call(first_edge_kernel, [(face, f32)] * 2, (xl, xr, yn, yp, keep), (), "vvvvv", "vv")
+    xn, xp = passed_around(xl, "gx", -1), passed_around(xr, "gx", 1)
     low, high = call(
         relay_kernel, [((9, rows), i32)] * 2, (flags, table, table_p, table_n), (), "svvv", "vv"
     )
     tables_n, tables_p = passed_around(low, "gx", -1), passed_around(high, "gx", 1)
-    ghosts = call(
+    near, ghosts = call(
         ghost_kernel,
-        [((8, 4, rows), i32)],
+        [((8, 4, rows), i32)] * 2,
         (tables_p, tables_n, table_p, table_n),
-        [vmem((8, 4, rows), i32), dma(1)],
+        [dma(1)],
         "vvvv",
-        "a",
-    )[0]
-    own, near = bring(keep)
+        "va",
+    )
+    own, asked = call(
+        first_bring_kernel,
+        [((3, rows), i32), ((128, 128), f32)],
+        (table_n, table, received),
+        [dma(2)],
+        "vaa",
+        "vv",
+    )
     for blend in (None, (0.75, 0.25)):
         u, near_u, loc, xl, xr, yl, yr, keep = call(
             lambda *refs, blend=blend: step_kernel(blend, *refs),
             [(field, f32)] * 2 + outs,
-            (replies, own, near, loc, xn, xp, yn, yp, start, u, inv, flow, nu, load, deep, mask),
+            (replies, own, near, loc, xn, xp, yn, yp, keep, start, u, inv, flow, nu, load, deep, mask),
             [vmem(field)] * 3 + [vmem((512, 128))] + local_scratch + [dma(9)],
-            "vvvvvvvvaaaaaaaa",
+            "vvvvvvvvvaaaaaaaa",
             "avvvvvvv",
         )
-        yn, yp = along_y(yl, yr)
+        xn, xp = swapped(xl, xr)
         answers = call(
             answer_kernel,
             [((128, 4, 128), f32)],
-            (near_u, received),
-            [vmem((128, 128))] + weights_scratch + [dma(1)],
-            "va",
+            (near_u, asked),
+            weights_scratch,
+            "vv",
             "p",
         )[0]
-        answers, yn, yp = lax.optimization_barrier((answers, yn, yp))
+        answers, xn, xp = lax.optimization_barrier((answers, xn, xp))
         replies = exchange(answers)
-        xn, xp = along_x(xl, xr, yn, yp, keep)
-        own, near = bring(keep)
+        yn, yp = faces_along_y(yl, yr, xn, xp, keep)
+        own, near, asked = bring(keep)
     third = call(
         lambda *refs: last_kernel((1.0 / 3.0, 2.0 / 3.0), *refs),
         [(field, f32)],
-        (replies, own, near, loc, xn, xp, yn, yp, start, u, inv),
+        (replies, own, near, loc, xn, xp, yn, yp, keep, start, u, inv),
         [vmem(field)] * 3 + [vmem((512, 128)), dma(3)],
-        "vvvvvvvvaaa",
+        "vvvvvvvvvaaa",
         "v",
     )[0]
     return third.reshape(scalar.shape)

time: 119 us -> 118 us (level); the launches traced: 118 us -> 116 us
  starting transfers between devices: 54.2 us -> 52.7 us
  Pallas kernels: 40.3 us -> 39 us
    ppermute x16 -> x12, starting transfers between devices: 25.8 us -> 14.6 us  [passed_around(): lax.ppermute(value, axis, [(n, (n + steps) % count) for n in range(count)])]
    all_to_all x4, starting transfers between devices: 28.4 us -> 36.3 us  [exchange(): lax.all_to_all(x, ('gx', 'gy'), split_axis=0, concat_axis=0, tiled=True)]
    all_to_all x4, waiting for transfers between devices: 3.51 us -> 9.74 us  [exchange(): lax.all_to_all(x, ('gx', 'gy'), split_axis=0, concat_axis=0, tiled=True)]
    ppermute x16 -> x12, waiting for transfers between devices: 19.8 us -> 14 us  [passed_around(): lax.ppermute(value, axis, [(n, (n + steps) % count) for n in range(count)])]
    ppermute x0 -> x4, starting transfers between devices: none -> 1.86 us  [the longest x2 1.54 us: swapped(): lax.ppermute(cross, 'gx', [(n, across[n]) for n in range(count)])]
    pallas_call x17, Pallas kernels: 40.3 us -> 39 us  [call(): pl.pallas_call(kernel, out_shape=[SPACES[c](s, d) if c in PINNED else jax...]
  transfers between devices with their start and end apart: 20 -> 20, of which waited for: 10 -> 10; matrix products, arithmetic and copies ran while one was open for 0% -> 0% of each run, Pallas kernels for 20% -> 19%
where the time goes in v4:
time: 118 us; the launch traced here: 116 us
  starting transfers between devices  52.7 us (45%)
  Pallas kernels  39 us (33%)
  waiting for transfers between devices  23.7 us (20%)
    pallas_call x17, Pallas kernels, call(): pl.pallas_call(kernel, out_shape=[SPACES[c](s, d) if c in PINNED else jax...  39 us
    all_to_all x4, starting transfers between devices, exchange(): lax.all_to_all(x, ('gx', 'gy'), split_axis=0, concat_axis=0, tiled=True)  36.3 us
    ppermute x12, starting transfers between devices, passed_around(): lax.ppermute(value, axis, [(n, (n + steps) % count) for n in range(count)])  14.6 us
    ppermute x12, waiting for transfers between devices, passed_around(): lax.ppermute(value, axis, [(n, (n + steps) % count) for n in range(count)])  14 us
    all_to_all x4, waiting for transfers between devices, exchange(): lax.all_to_all(x, ('gx', 'gy'), split_axis=0, concat_axis=0, tiled=True)  9.74 us
  transfers between devices with their start and end apart: 20, of which 10 were waited for; matrix products, arithmetic and copies ran while one was open for 0% of the time, Pallas kernels for 19%

profile of v4, /device:TPU:0, one launch (start us, length us, event | category | flops | bytes accessed | tf_op | source)
XLA Modules:
  0.0 116.0 jit_solution(14154993816828474804)
XLA Ops:
  0.0 2.5 %shard_map.82 = (f32[128,128]{1,0:T(8,128)}, s32[1,2048]{1,0:T(1,128)}) custom-call(s32[1,2048]{1,0:T(1,128)} %bitcast.31, s32[1,2048]{1,0:T(1,128)} %bitcast.37, f32[3,2048]{1,0:T(4,128)} %coords_any.1), custom_call_target="tpu_custom_call" | custom-call | tf_op jit(solution)/shard_map/pallas_call | solution.py:563
  2.5 11.1 %all-to-all-start = ((f32[128,1,128]{2,1,0:T(1,128)}), f32[128,1,128]{2,1,0:T(1,128)S(1)}, u32[]{:S(2)}, u32[]{:S(2)}) async-start(f32[128,1,128]{2,1,0:T(1,128)} %bitcast.4), calls=%async_computation | async-start | bytes 131072 | tf_op jit(solution)/shard_map/all_to_all | solution.py:588
  13.7 0.1 stack.23
  13.8 2.9 %shard_map.83 = (f32[2,512,128]{2,1,0:T(8,128)}, f32[512,128]{1,0:T(8,128)}, s32[3,2048]{1,0:T(4,128)}, f32[5,8,128]{2,1,0:T(8,128)}, s32[3,2048]{1,0:T(4,128)}, /*index=5*/s32[3,2048]{1,0:T(4,128)}) custom-call(s32[5]{0:T(128)S(1)} %convert_element_type.3.flags_ref, s32[1,2048]{1,0:T(1,128)} %bitcast.32, s32[1,2048]{1,0:T(1,128)} %get-tuple-element.70.rank_any, ...), custom_call_target="tpu_custom_call" | custom-call | tf_op jit(solution)/shard_map/pallas_call | solution.py:563
  16.8 0.0 copy-start.3
  16.8 0.0 copy-start.2
  16.8 0.0 copy-start.1
  16.8 2.8 %shard_map.84 = (f32[2,512,128]{2,1,0:T(8,128)S(1)}, f32[2,64,128]{2,1,0:T(8,128)S(1)}, f32[2,64,128]{2,1,0:T(8,128)S(1)}, f32[2,64,128]{2,1,0:T(8,128)S(1)}, f3...) custom-call(f32[2,512,128]{2,1,0:T(8,128)} %bitcast.22, f32[3,2,512,128]{3,2,1,0:T(8,128)} %bitcast.28, ...), custom_call_target="tpu_custom_call" | custom-call | tf_op jit(solution)/shard_map/pallas_call | solution.py:563
  19.5 3.4 %all-to-all-done = f32[128,1,128]{2,1,0:T(1,128)S(1)} async-done(((f32[128,1,128]{2,1,0:T(1,128)}), f32[128,1,128]{2,1,0:T(1,128)S(1)}, u32[]{:S(2)}, u32[]{:S(2)}) %all-to-all-start) | async-done | bytes 65568 | tf_op jit(solution)/shard_map/all_to_all | solution.py:588
  23.0 0.0 copy-start
  23.0 1.2 collective-permute-start
  24.1 0.9 collective-permute-start.1
  25.0 0.0 copy-done.3
  25.0 2.4 %collective-permute-start.2 = (s32[3,2048]{1,0:T(4,128)S(1)}, s32[3,2048]{1,0:T(4,128)S(1)}, u32[]{:S(2)}, u32[]{:S(2)}) collective-permute-start(s32[3,2048]{1,0:T(4,128)S(1)} %copy-done.3), channel_id=1, source_target_pairs={{0,3},{1,0},{2,1},{3,2},{4,7},{5,4},{6,5},{7,6},{8,11},{9,8},{10,9... | collective-permute-start | bytes 73736 | tf_op jit(solution)/shard_map/ppermute | solution.py:575
  27.4 0.0 copy-done.2
  27.4 0.0 collective-permute-start.3
  27.4 4.6 %shard_map.85 = f32[128,4,128]{2,1,0:T(4,128)} custom-call(f32[2,512,128]{2,1,0:T(8,128)} %bitcast.23, f32[128,128]{1,0:T(8,128)S(1)} %bitcast.18), custom_call_target="tpu_custom_call" | custom-call | tf_op jit(solution)/shard_map/pallas_call | solution.py:563
  32.0 0.0 collective-permute-done.2.after_ref.above_ref.yn_ref
  32.0 0.5 collective-permute-done.3.below_ref.yp_ref
  32.5 0.0 collective-permute-done.yn_ref.refs_6_
  32.5 0.0 collective-permute-done.1.yp_ref.refs_7_
  32.5 7.7 %all-to-all-start.1 = ((f32[128,4,128]{2,1,0:T(4,128)}), f32[128,4,128]{2,1,0:T(4,128)S(1)}, u32[]{:S(2)}, u32[]{:S(2)}) async-start(f32[128,4,128]{2,1,0:T(4,128)} %shard_map.85), calls=%async_computation.1 | async-start | bytes 524288 | tf_op jit(solution)/shard_map/all_to_all | solution.py:588
  40.2 0.0 copy-done.1
  40.3 0.6 shard_map.87
  40.8 0.1 collective-permute-start.4
  40.9 5.1 %collective-permute-start.5 = (s32[9,2048]{1,0:T(8,128)S(1)}, s32[9,2048]{1,0:T(8,128)S(1)}, u32[]{:S(2)}, u32[]{:S(2)}) collective-permute-start(s32[9,2048]{1,0:T(8,128)S(1)} %get-tuple-element.89), channel_id=1, source_target_pairs={{0,124},{4,0},{8,4},{12,8},{16,12},{20,16},{24,20},{28,24},{32,28}... | collective-permute-start | bytes 221192 | tf_op jit(solution)/shard_map/ppermute | solution.py:575
  46.0 0.4 collective-permute-start.6
  46.4 0.2 collective-permute-start.7
  46.6 0.0 copy-done
  46.6 0.9 shard_map.86
  47.5 3.1 %collective-permute-done.4.xp_ref = s32[9,2048]{1,0:T(8,128)S(1)} collective-permute-done((s32[9,2048]{1,0:T(8,128)S(1)}, s32[9,2048]{1,0:T(8,128)S(1)}, u32[]{:S(2)}, u32[]{:S(2)}) %collective-permute-start.4) | collective-permute-done | bytes 73760 | tf_op jit(solution)/shard_map/ppermute | solution.py:575
  50.5 0.0 collective-permute-done.5.xn_ref
  50.5 0.8 shard_map.88
  51.3 0.0 collective-permute-done.6.refs_4_
  51.3 2.1 %collective-permute-done.7.refs_5_ = f32[2,64,128]{2,1,0:T(8,128)S(1)} collective-permute-done((f32[2,64,128]{2,1,0:T(8,128)S(1)}, f32[2,64,128]{2,1,0:T(8,128)S(1)}, u32[]{:S(2)}, u32[]{:S(2)}) %collective-permute-start.7) | collective-permute-done | bytes 65568 | tf_op jit(solution)/shard_map/ppermute | solution.py:575
  53.4 0.0 all-to-all-done.1.refs_0_
  53.4 4.9 %shard_map.90 = (f32[2,512,128]{2,1,0:T(8,128)}, f32[2,512,128]{2,1,0:T(8,128)S(1)}, f32[2,512,128]{2,1,0:T(8,128)S(1)}, f32[2,64,128]{2,1,0:T(8,128)S(1)}, f32[...) custom-call(f32[128,4,128]{2,1,0:T(4,128)S(1)} %all-to-all-done.1.refs_, ...), custom_call_target="tpu_custom_call" | custom-call | tf_op jit(solution)/shard_map/pallas_call | solution.py:563
  58.4 0.1 collective-permute-start.8
  58.5 0.7 collective-permute-start.9
  59.1 3.5 %shard_map.91 = f32[128,4,128]{2,1,0:T(4,128)} custom-call(f32[2,512,128]{2,1,0:T(8,128)S(1)} %get-tuple-element.100.u_ref, f32[128,128]{1,0:T(8,128)S(1)} %get-tuple-element.101.received_ref), custom_call_target="tpu_custom_call" | custom-call | tf_op jit(solution)/shard_map/pallas_call | solution.py:563
  62.7 0.0 collective-permute-done.8.pair_ref.refs_4_
  62.7 0.0 collective-permute-done.9.cross_ref.refs_5_
  62.7 9.2 %all-to-all-start.2 = ((f32[128,4,128]{2,1,0:T(4,128)}), f32[128,4,128]{2,1,0:T(4,128)S(1)}, u32[]{:S(2)}, u32[]{:S(2)}) async-start(f32[128,4,128]{2,1,0:T(4,128)} %shard_map.91), calls=%async_computation.2 | async-start | bytes 524288 | tf_op jit(solution)/shard_map/all_to_all | solution.py:588
  71.9 2.2 %collective-permute-start.10 = (f32[2,64,128]{2,1,0:T(8,128)S(1)}, f32[2,64,128]{2,1,0:T(8,128)S(1)}, u32[]{:S(2)}, u32[]{:S(2)}) collective-permute-start(f32[2,64,128]{2,1,0:T(8,128)S(1)} %get-tuple-element.114), channel_id=1, source_target_pairs={{0,3},{1,0},{2,1},{3,2},{4,7},{5,4},{6,5},{7,6},{8,11},{9,8},{10,9... | collective-permute-start | bytes 196616 | tf_op jit(solution)/shard_map/ppermute | solution.py:575
  74.2 0.0 collective-permute-start.11
  74.2 1.0 shard_map.92
  75.2 2.2 %collective-permute-done.10.refs_6_ = f32[2,64,128]{2,1,0:T(8,128)S(1)} collective-permute-done((f32[2,64,128]{2,1,0:T(8,128)S(1)}, f32[2,64,128]{2,1,0:T(8,128)S(1)}, u32[]{:S(2)}, u32[]{:S(2)}) %collective-permute-start.10) | collective-permute-done | bytes 65568 | tf_op jit(solution)/shard_map/ppermute | solution.py:575
  77.4 2.2 %collective-permute-done.11.refs_7_ = f32[2,64,128]{2,1,0:T(8,128)S(1)} collective-permute-done((f32[2,64,128]{2,1,0:T(8,128)S(1)}, f32[2,64,128]{2,1,0:T(8,128)S(1)}, u32[]{:S(2)}, u32[]{:S(2)}) %collective-permute-start.11) | collective-permute-done | bytes 65568 | tf_op jit(solution)/shard_map/ppermute | solution.py:575
  79.7 3.2 %all-to-all-done.2.refs_0_ = f32[128,4,128]{2,1,0:T(4,128)S(1)} async-done(((f32[128,4,128]{2,1,0:T(4,128)}), f32[128,4,128]{2,1,0:T(4,128)S(1)}, u32[]{:S(2)}, u32[]{:S(2)}) %all-to-all-start.2) | async-done | bytes 262176 | tf_op jit(solution)/shard_map/all_to_all | solution.py:588
  82.8 5.1 %shard_map.94 = (f32[2,512,128]{2,1,0:T(8,128)}, f32[2,512,128]{2,1,0:T(8,128)S(1)}, f32[2,512,128]{2,1,0:T(8,128)S(1)}, f32[2,64,128]{2,1,0:T(8,128)S(1)}, f32[...) custom-call(f32[128,4,128]{2,1,0:T(4,128)S(1)} %all-to-all-done.2.refs_, ...), custom_call_target="tpu_custom_call" | custom-call | tf_op jit(solution)/shard_map/pallas_call | solution.py:563
  87.9 0.2 collective-permute-start.12
  88.1 0.9 collective-permute-start.13
  89.0 3.5 %shard_map.95 = f32[128,4,128]{2,1,0:T(4,128)} custom-call(f32[2,512,128]{2,1,0:T(8,128)S(1)} %get-tuple-element.117.u_ref, f32[128,128]{1,0:T(8,128)S(1)} %get-tuple-element.118.received_ref), custom_call_target="tpu_custom_call" | custom-call | tf_op jit(solution)/shard_map/pallas_call | solution.py:563
  92.5 0.0 collective-permute-done.12.pair_ref.refs_4_
  92.5 0.0 collective-permute-done.13.cross_ref.refs_5_
  92.5 8.2 %all-to-all-start.3 = ((f32[128,4,128]{2,1,0:T(4,128)}), f32[128,4,128]{2,1,0:T(4,128)S(1)}, u32[]{:S(2)}, u32[]{:S(2)}) async-start(f32[128,4,128]{2,1,0:T(4,128)} %shard_map.95), calls=%async_computation.3 | async-start | bytes 524288 | tf_op jit(solution)/shard_map/all_to_all | solution.py:588
  100.7 2.2 %collective-permute-start.14 = (f32[2,64,128]{2,1,0:T(8,128)S(1)}, f32[2,64,128]{2,1,0:T(8,128)S(1)}, u32[]{:S(2)}, u32[]{:S(2)}) collective-permute-start(f32[2,64,128]{2,1,0:T(8,128)S(1)} %get-tuple-element.130), channel_id=1, source_target_pairs={{0,3},{1,0},{2,1},{3,2},{4,7},{5,4},{6,5},{7,6},{8,11},{9,8},{10,9... | collective-permute-start | bytes 196616 | tf_op jit(solution)/shard_map/ppermute | solution.py:575
  103.0 0.0 collective-permute-start.15
  103.0 1.6 %shard_map.96 = (s32[3,2048]{1,0:T(4,128)S(1)}, s32[8,4,2048]{2,1,0:T(4,128)S(1)}, f32[128,128]{1,0:T(8,128)}) custom-call(f32[3,8,128]{2,1,0:T(8,128)S(1)} %get-tuple-element.122.after_ref.keep_ref.refs_8_, s32[3,2048]{1,0:T(4,128)} %get-tuple-element.85.table_any.own_ref, s32[8,4,2048]{2,1,0:T(4,128)} %get-tuple-element.106.ghost_any, f32[128,128]{1,0:T(8,128)} %bitcast.21), custom_call_target="tpu_custom_call" | custom-call | tf_op jit(solution)/shard_map/pallas_call | solution.py:563
  104.6 1.6 %collective-permute-done.14.refs_6_ = f32[2,64,128]{2,1,0:T(8,128)S(1)} collective-permute-done((f32[2,64,128]{2,1,0:T(8,128)S(1)}, f32[2,64,128]{2,1,0:T(8,128)S(1)}, u32[]{:S(2)}, u32[]{:S(2)}) %collective-permute-start.14) | collective-permute-done | bytes 65568 | tf_op jit(solution)/shard_map/ppermute | solution.py:575
  106.2 2.2 %collective-permute-done.15.refs_7_ = f32[2,64,128]{2,1,0:T(8,128)S(1)} collective-permute-done((f32[2,64,128]{2,1,0:T(8,128)S(1)}, f32[2,64,128]{2,1,0:T(8,128)S(1)}, u32[]{:S(2)}, u32[]{:S(2)}) %collective-permute-start.15) | collective-permute-done | bytes 65568 | tf_op jit(solution)/shard_map/ppermute | solution.py:575
  108.4 3.2 %all-to-all-done.3.refs_0_ = f32[128,4,128]{2,1,0:T(4,128)S(1)} async-done(((f32[128,4,128]{2,1,0:T(4,128)}), f32[128,4,128]{2,1,0:T(4,128)S(1)}, u32[]{:S(2)}, u32[]{:S(2)}) %all-to-all-start.3) | async-done | bytes 262176 | tf_op jit(solution)/shard_map/all_to_all | solution.py:588
  111.6 4.2 %shard_map.98 = f32[2,512,128]{2,1,0:T(8,128)} custom-call(f32[128,4,128]{2,1,0:T(4,128)S(1)} %all-to-all-done.3.refs_0_, s32[3,2048]{1,0:T(4,128)S(1)} %get-tuple-element.123.refs_1_, s32[8,4,2048]{2,1,0:T(4,128)S(1)} %get-tuple-element.124.refs_2_, f32[2,512,128]{2,1,0:T(8,128)S(1)} %get-tuple-element.125.refs_3_, ...), custom_call_target="tpu_custom_call" | custom-call | tf_op jit(solution)/shard_map/pallas_call | solution.py:563
  (4 shorter events, 0.1 us)
Async XLA Ops:
  2.5 20.5 %all-to-all-start = ((f32[128,1,128]{2,1,0:T(1,128)}), f32[128,1,128]{2,1,0:T(1,128)S(1)}, u32[]{:S(2)}, u32[]{:S(2)}) async-start(f32[128,1,128]{2,1,0:T(1,128)} %bitcast.4), calls=%async_computation | async-start | bytes 131072 | tf_op jit(solution)/shard_map/all_to_all | solution.py:588
  16.8 8.3 %copy-start.3 = (s32[3,2048]{1,0:T(4,128)S(1)}, s32[3,2048]{1,0:T(4,128)}, u32[]{:S(2)}) copy-start(s32[3,2048]{1,0:T(4,128)} %get-tuple-element.81) | copy-start | bytes 73732
  16.8 10.6 %copy-start.2 = (s32[3,2048]{1,0:T(4,128)S(1)}, s32[3,2048]{1,0:T(4,128)}, u32[]{:S(2)}) copy-start(s32[3,2048]{1,0:T(4,128)} %get-tuple-element.82) | copy-start | bytes 73732
  16.8 23.5 %copy-start.1 = (s32[3,2048]{1,0:T(4,128)S(1)}, s32[3,2048]{1,0:T(4,128)}, u32[]{:S(2)}) copy-start(s32[3,2048]{1,0:T(4,128)} %get-tuple-element.85.table_any.own_ref) | copy-start | bytes 73732
  23.0 23.6 %copy-start = (f32[128,1,128]{2,1,0:T(1,128)}, f32[128,1,128]{2,1,0:T(1,128)S(1)}, u32[]{:S(2)}) copy-start(f32[128,1,128]{2,1,0:T(1,128)S(1)} %all-to-all-done) | copy-start | bytes 196612
  23.0 9.5 %collective-permute-start = (f32[2,64,128]{2,1,0:T(8,128)S(1)}, f32[2,64,128]{2,1,0:T(8,128)S(1)}, u32[]{:S(2)}, u32[]{:S(2)}) collective-permute-start(f32[2,64,128]{2,1,0:T(8,128)S(1)} %get-tuple-element.79), channel_id=1, source_target_pairs={{0,3},{1,0},{2,1},{3,2},{4,7},{5,4},{6,5},{7,6},{8,11},{9,8},{10,9... | collective-permute-start | bytes 196616 | tf_op jit(solution)/shard_map/ppermute | solution.py:575
  24.1 8.4 %collective-permute-start.1 = (f32[2,64,128]{2,1,0:T(8,128)S(1)}, f32[2,64,128]{2,1,0:T(8,128)S(1)}, u32[]{:S(2)}, u32[]{:S(2)}) collective-permute-start(f32[2,64,128]{2,1,0:T(8,128)S(1)} %get-tuple-element.80), channel_id=1, source_target_pairs={{0,1},{1,2},{2,3},{3,0},{4,5},{5,6},{6,7},{7,4},{8,9},{9,10},{10,1... | collective-permute-start | bytes 196616 | tf_op jit(solution)/shard_map/ppermute | solution.py:575
  25.0 7.0 %collective-permute-start.2 = (s32[3,2048]{1,0:T(4,128)S(1)}, s32[3,2048]{1,0:T(4,128)S(1)}, u32[]{:S(2)}, u32[]{:S(2)}) collective-permute-start(s32[3,2048]{1,0:T(4,128)S(1)} %copy-done.3), channel_id=1, source_target_pairs={{0,3},{1,0},{2,1},{3,2},{4,7},{5,4},{6,5},{7,6},{8,11},{9,8},{10,9... | collective-permute-start | bytes 73736 | tf_op jit(solution)/shard_map/ppermute | solution.py:575
  27.4 5.1 %collective-permute-start.3 = (s32[3,2048]{1,0:T(4,128)S(1)}, s32[3,2048]{1,0:T(4,128)S(1)}, u32[]{:S(2)}, u32[]{:S(2)}) collective-permute-start(s32[3,2048]{1,0:T(4,128)S(1)} %copy-done.2), channel_id=1, source_target_pairs={{0,1},{1,2},{2,3},{3,0},{4,5},{5,6},{6,7},{7,4},{8,9},{9,10},{10,1... | collective-permute-start | bytes 73736 | tf_op jit(solution)/shard_map/ppermute | solution.py:575
  32.5 20.9 %all-to-all-start.1 = ((f32[128,4,128]{2,1,0:T(4,128)}), f32[128,4,128]{2,1,0:T(4,128)S(1)}, u32[]{:S(2)}, u32[]{:S(2)}) async-start(f32[128,4,128]{2,1,0:T(4,128)} %shard_map.85), calls=%async_computation.1 | async-start | bytes 524288 | tf_op jit(solution)/shard_map/all_to_all | solution.py:588
  40.8 9.7 %collective-permute-start.4 = (s32[9,2048]{1,0:T(8,128)S(1)}, s32[9,2048]{1,0:T(8,128)S(1)}, u32[]{:S(2)}, u32[]{:S(2)}) collective-permute-start(s32[9,2048]{1,0:T(8,128)S(1)} %get-tuple-element.88), channel_id=1, source_target_pairs={{0,4},{4,8},{8,12},{12,16},{16,20},{20,24},{24,28},{28,32},{32,36}... | collective-permute-start | bytes 221192 | tf_op jit(solution)/shard_map/ppermute | solution.py:575
  40.9 9.6 %collective-permute-start.5 = (s32[9,2048]{1,0:T(8,128)S(1)}, s32[9,2048]{1,0:T(8,128)S(1)}, u32[]{:S(2)}, u32[]{:S(2)}) collective-permute-start(s32[9,2048]{1,0:T(8,128)S(1)} %get-tuple-element.89), channel_id=1, source_target_pairs={{0,124},{4,0},{8,4},{12,8},{16,12},{20,16},{24,20},{28,24},{32,28}... | collective-permute-start | bytes 221192 | tf_op jit(solution)/shard_map/ppermute | solution.py:575
  46.0 5.3 %collective-permute-start.6 = (f32[2,64,128]{2,1,0:T(8,128)S(1)}, f32[2,64,128]{2,1,0:T(8,128)S(1)}, u32[]{:S(2)}, u32[]{:S(2)}) collective-permute-start(f32[2,64,128]{2,1,0:T(8,128)S(1)} %get-tuple-element.97), channel_id=1, source_target_pairs={{0,124},{4,0},{8,4},{12,8},{16,12},{20,16},{24,20},{28,24},{32,28}... | collective-permute-start | bytes 196616 | tf_op jit(solution)/shard_map/ppermute | solution.py:575
  46.4 7.0 %collective-permute-start.7 = (f32[2,64,128]{2,1,0:T(8,128)S(1)}, f32[2,64,128]{2,1,0:T(8,128)S(1)}, u32[]{:S(2)}, u32[]{:S(2)}) collective-permute-start(f32[2,64,128]{2,1,0:T(8,128)S(1)} %get-tuple-element.98), channel_id=1, source_target_pairs={{0,4},{4,8},{8,12},{12,16},{16,20},{20,24},{24,28},{28,32},{32,36}... | collective-permute-start | bytes 196616 | tf_op jit(solution)/shard_map/ppermute | solution.py:575
  58.4 4.3 %collective-permute-start.8 = (f32[2,64,128]{2,1,0:T(8,128)S(1)}, f32[2,64,128]{2,1,0:T(8,128)S(1)}, u32[]{:S(2)}, u32[]{:S(2)}) collective-permute-start(f32[2,64,128]{2,1,0:T(8,128)S(1)} %get-tuple-element.102), channel_id=1, source_target_pairs={{0,4},{4,0},{8,12},{12,8},{16,20},{20,16},{24,28},{28,24},{32,36},... | collective-permute-start | bytes 196616 | tf_op jit(solution)/shard_map/ppermute | solution.py:582
  58.5 4.2 %collective-permute-start.9 = (f32[2,64,128]{2,1,0:T(8,128)S(1)}, f32[2,64,128]{2,1,0:T(8,128)S(1)}, u32[]{:S(2)}, u32[]{:S(2)}) collective-permute-start(f32[2,64,128]{2,1,0:T(8,128)S(1)} %get-tuple-element.103), channel_id=1, source_target_pairs={{0,0},{4,8},{8,4},{12,16},{16,12},{20,24},{24,20},{28,32},{32,28},... | collective-permute-start | bytes 196616 | tf_op jit(solution)/shard_map/ppermute | solution.py:583
  62.7 20.1 %all-to-all-start.2 = ((f32[128,4,128]{2,1,0:T(4,128)}), f32[128,4,128]{2,1,0:T(4,128)S(1)}, u32[]{:S(2)}, u32[]{:S(2)}) async-start(f32[128,4,128]{2,1,0:T(4,128)} %shard_map.91), calls=%async_computation.2 | async-start | bytes 524288 | tf_op jit(solution)/shard_map/all_to_all | solution.py:588
  71.9 5.5 %collective-permute-start.10 = (f32[2,64,128]{2,1,0:T(8,128)S(1)}, f32[2,64,128]{2,1,0:T(8,128)S(1)}, u32[]{:S(2)}, u32[]{:S(2)}) collective-permute-start(f32[2,64,128]{2,1,0:T(8,128)S(1)} %get-tuple-element.114), channel_id=1, source_target_pairs={{0,3},{1,0},{2,1},{3,2},{4,7},{5,4},{6,5},{7,6},{8,11},{9,8},{10,9... | collective-permute-start | bytes 196616 | tf_op jit(solution)/shard_map/ppermute | solution.py:575
  74.2 5.5 %collective-permute-start.11 = (f32[2,64,128]{2,1,0:T(8,128)S(1)}, f32[2,64,128]{2,1,0:T(8,128)S(1)}, u32[]{:S(2)}, u32[]{:S(2)}) collective-permute-start(f32[2,64,128]{2,1,0:T(8,128)S(1)} %get-tuple-element.115), channel_id=1, source_target_pairs={{0,1},{1,2},{2,3},{3,0},{4,5},{5,6},{6,7},{7,4},{8,9},{9,10},{10,1... | collective-permute-start | bytes 196616 | tf_op jit(solution)/shard_map/ppermute | solution.py:575
  87.9 4.6 %collective-permute-start.12 = (f32[2,64,128]{2,1,0:T(8,128)S(1)}, f32[2,64,128]{2,1,0:T(8,128)S(1)}, u32[]{:S(2)}, u32[]{:S(2)}) collective-permute-start(f32[2,64,128]{2,1,0:T(8,128)S(1)} %get-tuple-element.119), channel_id=1, source_target_pairs={{0,4},{4,0},{8,12},{12,8},{16,20},{20,16},{24,28},{28,24},{32,36},... | collective-permute-start | bytes 196616 | tf_op jit(solution)/shard_map/ppermute | solution.py:582
  88.1 4.4 %collective-permute-start.13 = (f32[2,64,128]{2,1,0:T(8,128)S(1)}, f32[2,64,128]{2,1,0:T(8,128)S(1)}, u32[]{:S(2)}, u32[]{:S(2)}) collective-permute-start(f32[2,64,128]{2,1,0:T(8,128)S(1)} %get-tuple-element.120), channel_id=1, source_target_pairs={{0,0},{4,8},{8,4},{12,16},{16,12},{20,24},{24,20},{28,32},{32,28},... | collective-permute-start | bytes 196616 | tf_op jit(solution)/shard_map/ppermute | solution.py:583
  92.5 19.1 %all-to-all-start.3 = ((f32[128,4,128]{2,1,0:T(4,128)}), f32[128,4,128]{2,1,0:T(4,128)S(1)}, u32[]{:S(2)}, u32[]{:S(2)}) async-start(f32[128,4,128]{2,1,0:T(4,128)} %shard_map.95), calls=%async_computation.3 | async-start | bytes 524288 | tf_op jit(solution)/shard_map/all_to_all | solution.py:588
  100.7 5.5 %collective-permute-start.14 = (f32[2,64,128]{2,1,0:T(8,128)S(1)}, f32[2,64,128]{2,1,0:T(8,128)S(1)}, u32[]{:S(2)}, u32[]{:S(2)}) collective-permute-start(f32[2,64,128]{2,1,0:T(8,128)S(1)} %get-tuple-element.130), channel_id=1, source_target_pairs={{0,3},{1,0},{2,1},{3,2},{4,7},{5,4},{6,5},{7,6},{8,11},{9,8},{10,9... | collective-permute-start | bytes 196616 | tf_op jit(solution)/shard_map/ppermute | solution.py:575
  103.0 5.5 %collective-permute-start.15 = (f32[2,64,128]{2,1,0:T(8,128)S(1)}, f32[2,64,128]{2,1,0:T(8,128)S(1)}, u32[]{:S(2)}, u32[]{:S(2)}) collective-permute-start(f32[2,64,128]{2,1,0:T(8,128)S(1)} %get-tuple-element.131), channel_id=1, source_target_pairs={{0,1},{1,2},{2,3},{3,0},{4,5},{5,6},{6,7},{7,4},{8,9},{9,10},{10,1... | collective-permute-start | bytes 196616 | tf_op jit(solution)/shard_map/ppermute | solution.py:575

commit v5 on v4

--- a/solution.py
+++ b/solution.py
@@ -346,9 +346,7 @@
     send_first_faces(loc_ref, mask_ref, xl_ref, xr_ref, yl_ref, yr_ref, keep_ref)
 
 
-def interpolate(u, received_ref, ans_ref, wx_ref, wy_ref, wz_ref):
-    parts = [split_two(v) for v in u]
-    cat = jnp.concatenate([parts[0][0], parts[1][0], parts[0][1], parts[1][1]], axis=1)
+def interpolate(u_ref, received_ref, ans_ref, wx_ref, wy_ref, wz_ref, copies):
     turned = received_ref[...].T
     for v, ref in enumerate((wx_ref, wy_ref, wz_ref)):
         x = turned[v * 32 : v * 32 + 32, :]
@@ -371,6 +369,10 @@
             else:
                 ref[j] = w
     ids = turned[96:128, :].astype(i32)
+    for copy in copies:
+        copy.wait()
+    parts = [split_two(u_ref[m]) for m in range(2)]
+    cat = jnp.concatenate([parts[0][0], parts[1][0], parts[0][1], parts[1][1]], axis=1)
     rows = []
     for g in range(16):
         hot = [one_hot_rows(ids[s : s + 1, :], 256) for s in (2 * g, 2 * g + 1)]
@@ -400,13 +402,12 @@
 
 
 def answer_kernel(u_ref, received_ref, ans_ref, wx_ref, wy_ref, wz_ref):
-    interpolate([u_ref[0], u_ref[1]], received_ref, ans_ref, wx_ref, wy_ref, wz_ref)
+    interpolate(u_ref, received_ref, ans_ref, wx_ref, wy_ref, wz_ref, [])
 
 
 def first_kernel(u_any, received_ref, ans_ref, u_ref, wx_ref, wy_ref, wz_ref, sems):
     copies = start_copies([(u_any, u_ref)], sems)
-    copies[0].wait()
-    interpolate([u_ref[0], u_ref[1]], received_ref, ans_ref, wx_ref, wy_ref, wz_ref)
+    interpolate(u_ref, received_ref, ans_ref, wx_ref, wy_ref, wz_ref, copies)
 
 
 def edge_kernel(yl_ref, yr_ref, pair_ref, cross_ref, keep_ref, yl_out, yr_out):
@@ -513,9 +514,9 @@
             work_ref[m, rows, :] = with_faces(parts, m, ij) + (c * wk) * g
 
 
-def advance(blend, start_ref, u_ref, inv_ref, work_ref, new_ref):
+def advance(blend, start_ref, u_ref, inv_ref, work_ref, new_ref, meshes=(0, 1)):
     lane = lax.broadcasted_iota(i32, (64, 128), 1)
-    for m in range(2):
+    for m in meshes:
         left = work_ref[m, pl.ds(0, 64, stride=8), :]
         right = work_ref[m, pl.ds(7, 64, stride=8), :]
         work_ref[m, pl.ds(0, 64, stride=8), :] = left + jnp.where(lane > 0, pltpu.roll(right, 1, 1), 0.0)
@@ -546,13 +547,19 @@
     out.wait()
 
 
-def last_kernel(blend, replies_ref, table_ref, ghost_ref, old_ref, xn_ref, xp_ref, yn_ref, yp_ref, kept_ref, start_any, u_any, inv_any, new_ref,
-                work_ref, start_ref, u_ref, inv_ref, sems):
+def last_kernel(blend, replies_ref, table_ref, ghost_ref, old_ref, xn_ref, xp_ref, yn_ref, yp_ref, kept_ref, start_any, u_any, inv_any, new_any,
+                work_ref, start_ref, u_ref, inv_ref, new_ref, sems):
     copies = start_copies([(u_any, u_ref), (inv_any, inv_ref), (start_any, start_ref)], sems)
     add_replies(replies_ref, table_ref, ghost_ref, (old_ref, xn_ref, xp_ref, yn_ref, yp_ref, kept_ref, blend is None), work_ref)
     for copy in copies:
         copy.wait()
-    advance(blend, start_ref, u_ref, inv_ref, work_ref, new_ref)
+    outs = []
+    for m in range(2):
+        advance(blend, start_ref, u_ref, inv_ref, work_ref, new_ref, (m,))
+        outs.append(pltpu.make_async_copy(new_ref.at[m], new_any.at[m], sems.at[3 + m]))
+        outs[m].start()
+    for out in outs:
+        out.wait()
 
 
 PINNED = "ap"
@@ -723,9 +730,9 @@
         lambda *refs: last_kernel((1.0 / 3.0, 2.0 / 3.0), *refs),
         [(field, f32)],
         (replies, own, near, loc, xn, xp, yn, yp, keep, start, u, inv),
-        [vmem(field)] * 3 + [vmem((512, 128)), dma(3)],
+        [vmem(field)] * 3 + [vmem((512, 128)), vmem(field), dma(5)],
         "vvvvvvvvvaaa",
-        "v",
+        "a",
     )[0]
     return third.reshape(scalar.shape)
 

time: 118 us -> 117 us (level)
  no operation moved by 1% of the time
where the time goes in v5:
time: 117 us; the launch traced here: 116 us
  starting transfers between devices  52.5 us (45%)
  Pallas kernels  38.7 us (33%)
  waiting for transfers between devices  23.9 us (20%)
    pallas_call x17, Pallas kernels, call(): pl.pallas_call(kernel, out_shape=[SPACES[c](s, d) if c in PINNED else jax...  38.7 us
    all_to_all x4, starting transfers between devices, exchange(): lax.all_to_all(x, ('gx', 'gy'), split_axis=0, concat_axis=0, tiled=True)  36.1 us
    ppermute x12, starting transfers between devices, passed_around(): lax.ppermute(value, axis, [(n, (n + steps) % count) for n in range(count)])  14.6 us
    ppermute x12, waiting for transfers between devices, passed_around(): lax.ppermute(value, axis, [(n, (n + steps) % count) for n in range(count)])  14.2 us
    all_to_all x4, waiting for transfers between devices, exchange(): lax.all_to_all(x, ('gx', 'gy'), split_axis=0, concat_axis=0, tiled=True)  9.74 us
  transfers between devices with their start and end apart: 20, of which 10 were waited for; matrix products, arithmetic and copies ran while one was open for 0% of the time, Pallas kernels for 19%

profile of v5, /device:TPU:0, one launch (start us, length us, event | category | flops | bytes accessed | tf_op | source)
XLA Modules:
  0.0 115.7 jit_solution(4386312363000900639)
XLA Ops:
  0.0 2.5 %shard_map.82 = (f32[128,128]{1,0:T(8,128)}, s32[1,2048]{1,0:T(1,128)}) custom-call(s32[1,2048]{1,0:T(1,128)} %bitcast.31, s32[1,2048]{1,0:T(1,128)} %bitcast.37, f32[3,2048]{1,0:T(4,128)} %coords_any.1), custom_call_target="tpu_custom_call" | custom-call | tf_op jit(solution)/shard_map/pallas_call | solution.py:570
  2.5 11.1 %all-to-all-start = ((f32[128,1,128]{2,1,0:T(1,128)}), f32[128,1,128]{2,1,0:T(1,128)S(1)}, u32[]{:S(2)}, u32[]{:S(2)}) async-start(f32[128,1,128]{2,1,0:T(1,128)} %bitcast.4), calls=%async_computation | async-start | bytes 131072 | tf_op jit(solution)/shard_map/all_to_all | solution.py:595
  13.7 0.1 stack.23
  13.8 2.9 %shard_map.83 = (f32[2,512,128]{2,1,0:T(8,128)}, f32[512,128]{1,0:T(8,128)}, s32[3,2048]{1,0:T(4,128)}, f32[5,8,128]{2,1,0:T(8,128)}, s32[3,2048]{1,0:T(4,128)}, /*index=5*/s32[3,2048]{1,0:T(4,128)}) custom-call(s32[5]{0:T(128)S(1)} %convert_element_type.3.flags_ref, s32[1,2048]{1,0:T(1,128)} %bitcast.32, s32[1,2048]{1,0:T(1,128)} %get-tuple-element.70.rank_any, ...), custom_call_target="tpu_custom_call" | custom-call | tf_op jit(solution)/shard_map/pallas_call | solution.py:570
  16.8 0.0 copy-start.3
  16.8 0.0 copy-start.2
  16.8 0.0 copy-start.1
  16.8 2.8 %shard_map.84 = (f32[2,512,128]{2,1,0:T(8,128)S(1)}, f32[2,64,128]{2,1,0:T(8,128)S(1)}, f32[2,64,128]{2,1,0:T(8,128)S(1)}, f32[2,64,128]{2,1,0:T(8,128)S(1)}, f3...) custom-call(f32[2,512,128]{2,1,0:T(8,128)} %bitcast.22, f32[3,2,512,128]{3,2,1,0:T(8,128)} %bitcast.28, ...), custom_call_target="tpu_custom_call" | custom-call | tf_op jit(solution)/shard_map/pallas_call | solution.py:570
  19.5 3.4 %all-to-all-done = f32[128,1,128]{2,1,0:T(1,128)S(1)} async-done(((f32[128,1,128]{2,1,0:T(1,128)}), f32[128,1,128]{2,1,0:T(1,128)S(1)}, u32[]{:S(2)}, u32[]{:S(2)}) %all-to-all-start) | async-done | bytes 65568 | tf_op jit(solution)/shard_map/all_to_all | solution.py:595
  23.0 0.0 copy-start
  23.0 1.2 %collective-permute-start = (f32[2,64,128]{2,1,0:T(8,128)S(1)}, f32[2,64,128]{2,1,0:T(8,128)S(1)}, u32[]{:S(2)}, u32[]{:S(2)}) collective-permute-start(f32[2,64,128]{2,1,0:T(8,128)S(1)} %get-tuple-element.79), channel_id=1, source_target_pairs={{0,3},{1,0},{2,1},{3,2},{4,7},{5,4},{6,5},{7,6},{8,11},{9,8},{10,9... | collective-permute-start | bytes 196616 | tf_op jit(solution)/shard_map/ppermute | solution.py:582
  24.1 0.9 collective-permute-start.1
  25.0 0.0 copy-done.3
  25.0 2.4 %collective-permute-start.2 = (s32[3,2048]{1,0:T(4,128)S(1)}, s32[3,2048]{1,0:T(4,128)S(1)}, u32[]{:S(2)}, u32[]{:S(2)}) collective-permute-start(s32[3,2048]{1,0:T(4,128)S(1)} %copy-done.3), channel_id=1, source_target_pairs={{0,3},{1,0},{2,1},{3,2},{4,7},{5,4},{6,5},{7,6},{8,11},{9,8},{10,9... | collective-permute-start | bytes 73736 | tf_op jit(solution)/shard_map/ppermute | solution.py:582
  27.4 0.0 copy-done.2
  27.4 0.0 collective-permute-start.3
  27.4 4.4 %shard_map.85 = f32[128,4,128]{2,1,0:T(4,128)} custom-call(f32[2,512,128]{2,1,0:T(8,128)} %bitcast.23, f32[128,128]{1,0:T(8,128)S(1)} %bitcast.18), custom_call_target="tpu_custom_call" | custom-call | tf_op jit(solution)/shard_map/pallas_call | solution.py:570
  31.8 0.0 collective-permute-done.2.after_ref.above_ref.yn_ref
  31.8 0.7 collective-permute-done.3.below_ref.yp_ref
  32.5 0.0 collective-permute-done.yn_ref.refs_6_
  32.5 0.0 collective-permute-done.1.yp_ref.refs_7_
  32.5 7.5 %all-to-all-start.1 = ((f32[128,4,128]{2,1,0:T(4,128)}), f32[128,4,128]{2,1,0:T(4,128)S(1)}, u32[]{:S(2)}, u32[]{:S(2)}) async-start(f32[128,4,128]{2,1,0:T(4,128)} %shard_map.85), calls=%async_computation.1 | async-start | bytes 524288 | tf_op jit(solution)/shard_map/all_to_all | solution.py:595
  40.1 0.0 copy-done.1
  40.1 0.6 shard_map.87
  40.6 0.1 collective-permute-start.4
  40.7 5.1 %collective-permute-start.5 = (s32[9,2048]{1,0:T(8,128)S(1)}, s32[9,2048]{1,0:T(8,128)S(1)}, u32[]{:S(2)}, u32[]{:S(2)}) collective-permute-start(s32[9,2048]{1,0:T(8,128)S(1)} %get-tuple-element.89), channel_id=1, source_target_pairs={{0,124},{4,0},{8,4},{12,8},{16,12},{20,16},{24,20},{28,24},{32,28}... | collective-permute-start | bytes 221192 | tf_op jit(solution)/shard_map/ppermute | solution.py:582
  45.8 0.4 collective-permute-start.6
  46.2 0.2 collective-permute-start.7
  46.4 0.0 copy-done
  46.4 0.9 shard_map.86
  47.3 3.1 %collective-permute-done.4.xp_ref = s32[9,2048]{1,0:T(8,128)S(1)} collective-permute-done((s32[9,2048]{1,0:T(8,128)S(1)}, s32[9,2048]{1,0:T(8,128)S(1)}, u32[]{:S(2)}, u32[]{:S(2)}) %collective-permute-start.4) | collective-permute-done | bytes 73760 | tf_op jit(solution)/shard_map/ppermute | solution.py:582
  50.3 0.0 collective-permute-done.5.xn_ref
  50.3 0.8 shard_map.88
  51.1 0.0 collective-permute-done.6.refs_4_
  51.1 2.1 %collective-permute-done.7.refs_5_ = f32[2,64,128]{2,1,0:T(8,128)S(1)} collective-permute-done((f32[2,64,128]{2,1,0:T(8,128)S(1)}, f32[2,64,128]{2,1,0:T(8,128)S(1)}, u32[]{:S(2)}, u32[]{:S(2)}) %collective-permute-start.7) | collective-permute-done | bytes 65568 | tf_op jit(solution)/shard_map/ppermute | solution.py:582
  53.2 0.0 all-to-all-done.1.refs_0_
  53.2 4.9 %shard_map.90 = (f32[2,512,128]{2,1,0:T(8,128)}, f32[2,512,128]{2,1,0:T(8,128)S(1)}, f32[2,512,128]{2,1,0:T(8,128)S(1)}, f32[2,64,128]{2,1,0:T(8,128)S(1)}, f32[...) custom-call(f32[128,4,128]{2,1,0:T(4,128)S(1)} %all-to-all-done.1.refs_, ...), custom_call_target="tpu_custom_call" | custom-call | tf_op jit(solution)/shard_map/pallas_call | solution.py:570
  58.2 0.1 collective-permute-start.8
  58.3 0.7 collective-permute-start.9
  58.9 3.5 %shard_map.91 = f32[128,4,128]{2,1,0:T(4,128)} custom-call(f32[2,512,128]{2,1,0:T(8,128)S(1)} %get-tuple-element.100.u_ref, f32[128,128]{1,0:T(8,128)S(1)} %get-tuple-element.101.received_ref), custom_call_target="tpu_custom_call" | custom-call | tf_op jit(solution)/shard_map/pallas_call | solution.py:570
  62.5 0.0 collective-permute-done.8.pair_ref.refs_4_
  62.5 0.0 collective-permute-done.9.cross_ref.refs_5_
  62.5 9.2 %all-to-all-start.2 = ((f32[128,4,128]{2,1,0:T(4,128)}), f32[128,4,128]{2,1,0:T(4,128)S(1)}, u32[]{:S(2)}, u32[]{:S(2)}) async-start(f32[128,4,128]{2,1,0:T(4,128)} %shard_map.91), calls=%async_computation.2 | async-start | bytes 524288 | tf_op jit(solution)/shard_map/all_to_all | solution.py:595
  71.7 2.2 %collective-permute-start.10 = (f32[2,64,128]{2,1,0:T(8,128)S(1)}, f32[2,64,128]{2,1,0:T(8,128)S(1)}, u32[]{:S(2)}, u32[]{:S(2)}) collective-permute-start(f32[2,64,128]{2,1,0:T(8,128)S(1)} %get-tuple-element.114), channel_id=1, source_target_pairs={{0,3},{1,0},{2,1},{3,2},{4,7},{5,4},{6,5},{7,6},{8,11},{9,8},{10,9... | collective-permute-start | bytes 196616 | tf_op jit(solution)/shard_map/ppermute | solution.py:582
  74.0 0.0 collective-permute-start.11
  74.0 1.0 shard_map.92
  75.0 2.2 %collective-permute-done.10.refs_6_ = f32[2,64,128]{2,1,0:T(8,128)S(1)} collective-permute-done((f32[2,64,128]{2,1,0:T(8,128)S(1)}, f32[2,64,128]{2,1,0:T(8,128)S(1)}, u32[]{:S(2)}, u32[]{:S(2)}) %collective-permute-start.10) | collective-permute-done | bytes 65568 | tf_op jit(solution)/shard_map/ppermute | solution.py:582
  77.2 2.2 %collective-permute-done.11.refs_7_ = f32[2,64,128]{2,1,0:T(8,128)S(1)} collective-permute-done((f32[2,64,128]{2,1,0:T(8,128)S(1)}, f32[2,64,128]{2,1,0:T(8,128)S(1)}, u32[]{:S(2)}, u32[]{:S(2)}) %collective-permute-start.11) | collective-permute-done | bytes 65568 | tf_op jit(solution)/shard_map/ppermute | solution.py:582
  79.5 3.2 %all-to-all-done.2.refs_0_ = f32[128,4,128]{2,1,0:T(4,128)S(1)} async-done(((f32[128,4,128]{2,1,0:T(4,128)}), f32[128,4,128]{2,1,0:T(4,128)S(1)}, u32[]{:S(2)}, u32[]{:S(2)}) %all-to-all-start.2) | async-done | bytes 262176 | tf_op jit(solution)/shard_map/all_to_all | solution.py:595
  82.6 5.1 %shard_map.94 = (f32[2,512,128]{2,1,0:T(8,128)}, f32[2,512,128]{2,1,0:T(8,128)S(1)}, f32[2,512,128]{2,1,0:T(8,128)S(1)}, f32[2,64,128]{2,1,0:T(8,128)S(1)}, f32[...) custom-call(f32[128,4,128]{2,1,0:T(4,128)S(1)} %all-to-all-done.2.refs_, ...), custom_call_target="tpu_custom_call" | custom-call | tf_op jit(solution)/shard_map/pallas_call | solution.py:570
  87.7 0.2 collective-permute-start.12
  87.9 0.9 collective-permute-start.13
  88.8 3.5 %shard_map.95 = f32[128,4,128]{2,1,0:T(4,128)} custom-call(f32[2,512,128]{2,1,0:T(8,128)S(1)} %get-tuple-element.117.u_ref, f32[128,128]{1,0:T(8,128)S(1)} %get-tuple-element.118.received_ref), custom_call_target="tpu_custom_call" | custom-call | tf_op jit(solution)/shard_map/pallas_call | solution.py:570
  92.3 0.0 collective-permute-done.12.pair_ref.refs_4_
  92.3 0.0 collective-permute-done.13.cross_ref.refs_5_
  92.4 8.2 %all-to-all-start.3 = ((f32[128,4,128]{2,1,0:T(4,128)}), f32[128,4,128]{2,1,0:T(4,128)S(1)}, u32[]{:S(2)}, u32[]{:S(2)}) async-start(f32[128,4,128]{2,1,0:T(4,128)} %shard_map.95), calls=%async_computation.3 | async-start | bytes 524288 | tf_op jit(solution)/shard_map/all_to_all | solution.py:595
  100.5 2.2 %collective-permute-start.14 = (f32[2,64,128]{2,1,0:T(8,128)S(1)}, f32[2,64,128]{2,1,0:T(8,128)S(1)}, u32[]{:S(2)}, u32[]{:S(2)}) collective-permute-start(f32[2,64,128]{2,1,0:T(8,128)S(1)} %get-tuple-element.130), channel_id=1, source_target_pairs={{0,3},{1,0},{2,1},{3,2},{4,7},{5,4},{6,5},{7,6},{8,11},{9,8},{10,9... | collective-permute-start | bytes 196616 | tf_op jit(solution)/shard_map/ppermute | solution.py:582
  102.8 0.0 collective-permute-start.15
  102.8 1.6 %shard_map.96 = (s32[3,2048]{1,0:T(4,128)S(1)}, s32[8,4,2048]{2,1,0:T(4,128)S(1)}, f32[128,128]{1,0:T(8,128)}) custom-call(f32[3,8,128]{2,1,0:T(8,128)S(1)} %get-tuple-element.122.after_ref.keep_ref.refs_8_, s32[3,2048]{1,0:T(4,128)} %get-tuple-element.85.table_any.own_ref, s32[8,4,2048]{2,1,0:T(4,128)} %get-tuple-element.106.ghost_any, f32[128,128]{1,0:T(8,128)} %bitcast.21), custom_call_target="tpu_custom_call" | custom-call | tf_op jit(solution)/shard_map/pallas_call | solution.py:570
  104.4 1.6 %collective-permute-done.14.refs_6_ = f32[2,64,128]{2,1,0:T(8,128)S(1)} collective-permute-done((f32[2,64,128]{2,1,0:T(8,128)S(1)}, f32[2,64,128]{2,1,0:T(8,128)S(1)}, u32[]{:S(2)}, u32[]{:S(2)}) %collective-permute-start.14) | collective-permute-done | bytes 65568 | tf_op jit(solution)/shard_map/ppermute | solution.py:582
  106.0 2.2 %collective-permute-done.15.refs_7_ = f32[2,64,128]{2,1,0:T(8,128)S(1)} collective-permute-done((f32[2,64,128]{2,1,0:T(8,128)S(1)}, f32[2,64,128]{2,1,0:T(8,128)S(1)}, u32[]{:S(2)}, u32[]{:S(2)}) %collective-permute-start.15) | collective-permute-done | bytes 65568 | tf_op jit(solution)/shard_map/ppermute | solution.py:582
  108.3 3.2 %all-to-all-done.3.refs_0_ = f32[128,4,128]{2,1,0:T(4,128)S(1)} async-done(((f32[128,4,128]{2,1,0:T(4,128)}), f32[128,4,128]{2,1,0:T(4,128)S(1)}, u32[]{:S(2)}, u32[]{:S(2)}) %all-to-all-start.3) | async-done | bytes 262176 | tf_op jit(solution)/shard_map/all_to_all | solution.py:595
  111.4 4.1 %shard_map.98 = f32[2,512,128]{2,1,0:T(8,128)} custom-call(f32[128,4,128]{2,1,0:T(4,128)S(1)} %all-to-all-done.3.refs_0_, s32[3,2048]{1,0:T(4,128)S(1)} %get-tuple-element.123.refs_1_, s32[8,4,2048]{2,1,0:T(4,128)S(1)} %get-tuple-element.124.refs_2_, f32[2,512,128]{2,1,0:T(8,128)S(1)} %get-tuple-element.125.refs_3_, ...), custom_call_target="tpu_custom_call" | custom-call | tf_op jit(solution)/shard_map/pallas_call | solution.py:570
  (4 shorter events, 0.1 us)
Async XLA Ops:
  2.5 20.5 %all-to-all-start = ((f32[128,1,128]{2,1,0:T(1,128)}), f32[128,1,128]{2,1,0:T(1,128)S(1)}, u32[]{:S(2)}, u32[]{:S(2)}) async-start(f32[128,1,128]{2,1,0:T(1,128)} %bitcast.4), calls=%async_computation | async-start | bytes 131072 | tf_op jit(solution)/shard_map/all_to_all | solution.py:595
  16.8 8.3 %copy-start.3 = (s32[3,2048]{1,0:T(4,128)S(1)}, s32[3,2048]{1,0:T(4,128)}, u32[]{:S(2)}) copy-start(s32[3,2048]{1,0:T(4,128)} %get-tuple-element.81) | copy-start | bytes 73732
  16.8 10.6 %copy-start.2 = (s32[3,2048]{1,0:T(4,128)S(1)}, s32[3,2048]{1,0:T(4,128)}, u32[]{:S(2)}) copy-start(s32[3,2048]{1,0:T(4,128)} %get-tuple-element.82) | copy-start | bytes 73732
  16.8 23.3 %copy-start.1 = (s32[3,2048]{1,0:T(4,128)S(1)}, s32[3,2048]{1,0:T(4,128)}, u32[]{:S(2)}) copy-start(s32[3,2048]{1,0:T(4,128)} %get-tuple-element.85.table_any.own_ref) | copy-start | bytes 73732
  23.0 23.4 %copy-start = (f32[128,1,128]{2,1,0:T(1,128)}, f32[128,1,128]{2,1,0:T(1,128)S(1)}, u32[]{:S(2)}) copy-start(f32[128,1,128]{2,1,0:T(1,128)S(1)} %all-to-all-done) | copy-start | bytes 196612
  23.0 9.5 %collective-permute-start = (f32[2,64,128]{2,1,0:T(8,128)S(1)}, f32[2,64,128]{2,1,0:T(8,128)S(1)}, u32[]{:S(2)}, u32[]{:S(2)}) collective-permute-start(f32[2,64,128]{2,1,0:T(8,128)S(1)} %get-tuple-element.79), channel_id=1, source_target_pairs={{0,3},{1,0},{2,1},{3,2},{4,7},{5,4},{6,5},{7,6},{8,11},{9,8},{10,9... | collective-permute-start | bytes 196616 | tf_op jit(solution)/shard_map/ppermute | solution.py:582
  24.1 8.4 %collective-permute-start.1 = (f32[2,64,128]{2,1,0:T(8,128)S(1)}, f32[2,64,128]{2,1,0:T(8,128)S(1)}, u32[]{:S(2)}, u32[]{:S(2)}) collective-permute-start(f32[2,64,128]{2,1,0:T(8,128)S(1)} %get-tuple-element.80), channel_id=1, source_target_pairs={{0,1},{1,2},{2,3},{3,0},{4,5},{5,6},{6,7},{7,4},{8,9},{9,10},{10,1... | collective-permute-start | bytes 196616 | tf_op jit(solution)/shard_map/ppermute | solution.py:582
  25.0 6.8 %collective-permute-start.2 = (s32[3,2048]{1,0:T(4,128)S(1)}, s32[3,2048]{1,0:T(4,128)S(1)}, u32[]{:S(2)}, u32[]{:S(2)}) collective-permute-start(s32[3,2048]{1,0:T(4,128)S(1)} %copy-done.3), channel_id=1, source_target_pairs={{0,3},{1,0},{2,1},{3,2},{4,7},{5,4},{6,5},{7,6},{8,11},{9,8},{10,9... | collective-permute-start | bytes 73736 | tf_op jit(solution)/shard_map/ppermute | solution.py:582
  27.4 5.1 %collective-permute-start.3 = (s32[3,2048]{1,0:T(4,128)S(1)}, s32[3,2048]{1,0:T(4,128)S(1)}, u32[]{:S(2)}, u32[]{:S(2)}) collective-permute-start(s32[3,2048]{1,0:T(4,128)S(1)} %copy-done.2), channel_id=1, source_target_pairs={{0,1},{1,2},{2,3},{3,0},{4,5},{5,6},{6,7},{7,4},{8,9},{9,10},{10,1... | collective-permute-start | bytes 73736 | tf_op jit(solution)/shard_map/ppermute | solution.py:582
  32.5 20.7 %all-to-all-start.1 = ((f32[128,4,128]{2,1,0:T(4,128)}), f32[128,4,128]{2,1,0:T(4,128)S(1)}, u32[]{:S(2)}, u32[]{:S(2)}) async-start(f32[128,4,128]{2,1,0:T(4,128)} %shard_map.85), calls=%async_computation.1 | async-start | bytes 524288 | tf_op jit(solution)/shard_map/all_to_all | solution.py:595
  40.6 9.7 %collective-permute-start.4 = (s32[9,2048]{1,0:T(8,128)S(1)}, s32[9,2048]{1,0:T(8,128)S(1)}, u32[]{:S(2)}, u32[]{:S(2)}) collective-permute-start(s32[9,2048]{1,0:T(8,128)S(1)} %get-tuple-element.88), channel_id=1, source_target_pairs={{0,4},{4,8},{8,12},{12,16},{16,20},{20,24},{24,28},{28,32},{32,36}... | collective-permute-start | bytes 221192 | tf_op jit(solution)/shard_map/ppermute | solution.py:582
  40.7 9.6 %collective-permute-start.5 = (s32[9,2048]{1,0:T(8,128)S(1)}, s32[9,2048]{1,0:T(8,128)S(1)}, u32[]{:S(2)}, u32[]{:S(2)}) collective-permute-start(s32[9,2048]{1,0:T(8,128)S(1)} %get-tuple-element.89), channel_id=1, source_target_pairs={{0,124},{4,0},{8,4},{12,8},{16,12},{20,16},{24,20},{28,24},{32,28}... | collective-permute-start | bytes 221192 | tf_op jit(solution)/shard_map/ppermute | solution.py:582
  45.8 5.3 %collective-permute-start.6 = (f32[2,64,128]{2,1,0:T(8,128)S(1)}, f32[2,64,128]{2,1,0:T(8,128)S(1)}, u32[]{:S(2)}, u32[]{:S(2)}) collective-permute-start(f32[2,64,128]{2,1,0:T(8,128)S(1)} %get-tuple-element.97), channel_id=1, source_target_pairs={{0,124},{4,0},{8,4},{12,8},{16,12},{20,16},{24,20},{28,24},{32,28}... | collective-permute-start | bytes 196616 | tf_op jit(solution)/shard_map/ppermute | solution.py:582
  46.2 7.0 %collective-permute-start.7 = (f32[2,64,128]{2,1,0:T(8,128)S(1)}, f32[2,64,128]{2,1,0:T(8,128)S(1)}, u32[]{:S(2)}, u32[]{:S(2)}) collective-permute-start(f32[2,64,128]{2,1,0:T(8,128)S(1)} %get-tuple-element.98), channel_id=1, source_target_pairs={{0,4},{4,8},{8,12},{12,16},{16,20},{20,24},{24,28},{28,32},{32,36}... | collective-permute-start | bytes 196616 | tf_op jit(solution)/shard_map/ppermute | solution.py:582
  58.2 4.3 %collective-permute-start.8 = (f32[2,64,128]{2,1,0:T(8,128)S(1)}, f32[2,64,128]{2,1,0:T(8,128)S(1)}, u32[]{:S(2)}, u32[]{:S(2)}) collective-permute-start(f32[2,64,128]{2,1,0:T(8,128)S(1)} %get-tuple-element.102), channel_id=1, source_target_pairs={{0,4},{4,0},{8,12},{12,8},{16,20},{20,16},{24,28},{28,24},{32,36},... | collective-permute-start | bytes 196616 | tf_op jit(solution)/shard_map/ppermute | solution.py:589
  58.3 4.2 %collective-permute-start.9 = (f32[2,64,128]{2,1,0:T(8,128)S(1)}, f32[2,64,128]{2,1,0:T(8,128)S(1)}, u32[]{:S(2)}, u32[]{:S(2)}) collective-permute-start(f32[2,64,128]{2,1,0:T(8,128)S(1)} %get-tuple-element.103), channel_id=1, source_target_pairs={{0,0},{4,8},{8,4},{12,16},{16,12},{20,24},{24,20},{28,32},{32,28},... | collective-permute-start | bytes 196616 | tf_op jit(solution)/shard_map/ppermute | solution.py:590
  62.5 20.1 %all-to-all-start.2 = ((f32[128,4,128]{2,1,0:T(4,128)}), f32[128,4,128]{2,1,0:T(4,128)S(1)}, u32[]{:S(2)}, u32[]{:S(2)}) async-start(f32[128,4,128]{2,1,0:T(4,128)} %shard_map.91), calls=%async_computation.2 | async-start | bytes 524288 | tf_op jit(solution)/shard_map/all_to_all | solution.py:595
  71.7 5.5 %collective-permute-start.10 = (f32[2,64,128]{2,1,0:T(8,128)S(1)}, f32[2,64,128]{2,1,0:T(8,128)S(1)}, u32[]{:S(2)}, u32[]{:S(2)}) collective-permute-start(f32[2,64,128]{2,1,0:T(8,128)S(1)} %get-tuple-element.114), channel_id=1, source_target_pairs={{0,3},{1,0},{2,1},{3,2},{4,7},{5,4},{6,5},{7,6},{8,11},{9,8},{10,9... | collective-permute-start | bytes 196616 | tf_op jit(solution)/shard_map/ppermute | solution.py:582
  74.0 5.5 %collective-permute-start.11 = (f32[2,64,128]{2,1,0:T(8,128)S(1)}, f32[2,64,128]{2,1,0:T(8,128)S(1)}, u32[]{:S(2)}, u32[]{:S(2)}) collective-permute-start(f32[2,64,128]{2,1,0:T(8,128)S(1)} %get-tuple-element.115), channel_id=1, source_target_pairs={{0,1},{1,2},{2,3},{3,0},{4,5},{5,6},{6,7},{7,4},{8,9},{9,10},{10,1... | collective-permute-start | bytes 196616 | tf_op jit(solution)/shard_map/ppermute | solution.py:582
  87.7 4.6 %collective-permute-start.12 = (f32[2,64,128]{2,1,0:T(8,128)S(1)}, f32[2,64,128]{2,1,0:T(8,128)S(1)}, u32[]{:S(2)}, u32[]{:S(2)}) collective-permute-start(f32[2,64,128]{2,1,0:T(8,128)S(1)} %get-tuple-element.119), channel_id=1, source_target_pairs={{0,4},{4,0},{8,12},{12,8},{16,20},{20,16},{24,28},{28,24},{32,36},... | collective-permute-start | bytes 196616 | tf_op jit(solution)/shard_map/ppermute | solution.py:589
  87.9 4.4 %collective-permute-start.13 = (f32[2,64,128]{2,1,0:T(8,128)S(1)}, f32[2,64,128]{2,1,0:T(8,128)S(1)}, u32[]{:S(2)}, u32[]{:S(2)}) collective-permute-start(f32[2,64,128]{2,1,0:T(8,128)S(1)} %get-tuple-element.120), channel_id=1, source_target_pairs={{0,0},{4,8},{8,4},{12,16},{16,12},{20,24},{24,20},{28,32},{32,28},... | collective-permute-start | bytes 196616 | tf_op jit(solution)/shard_map/ppermute | solution.py:590
  92.4 19.1 %all-to-all-start.3 = ((f32[128,4,128]{2,1,0:T(4,128)}), f32[128,4,128]{2,1,0:T(4,128)S(1)}, u32[]{:S(2)}, u32[]{:S(2)}) async-start(f32[128,4,128]{2,1,0:T(4,128)} %shard_map.95), calls=%async_computation.3 | async-start | bytes 524288 | tf_op jit(solution)/shard_map/all_to_all | solution.py:595
  100.5 5.5 %collective-permute-start.14 = (f32[2,64,128]{2,1,0:T(8,128)S(1)}, f32[2,64,128]{2,1,0:T(8,128)S(1)}, u32[]{:S(2)}, u32[]{:S(2)}) collective-permute-start(f32[2,64,128]{2,1,0:T(8,128)S(1)} %get-tuple-element.130), channel_id=1, source_target_pairs={{0,3},{1,0},{2,1},{3,2},{4,7},{5,4},{6,5},{7,6},{8,11},{9,8},{10,9... | collective-permute-start | bytes 196616 | tf_op jit(solution)/shard_map/ppermute | solution.py:582
  102.8 5.5 %collective-permute-start.15 = (f32[2,64,128]{2,1,0:T(8,128)S(1)}, f32[2,64,128]{2,1,0:T(8,128)S(1)}, u32[]{:S(2)}, u32[]{:S(2)}) collective-permute-start(f32[2,64,128]{2,1,0:T(8,128)S(1)} %get-tuple-element.131), channel_id=1, source_target_pairs={{0,1},{1,2},{2,3},{3,0},{4,5},{5,6},{6,7},{7,4},{8,9},{9,10},{10,1... | collective-permute-start | bytes 196616 | tf_op jit(solution)/shard_map/ppermute | solution.py:582
